TPU v7x, 128 devices: a whole 4x4x4 slice. The times are simulated.
128 devices in a mesh: rows: 8 (over x, core), cols: 16 (over z, y).
Axes of the slice: x: 4, y: 4, z: 4, core: 2. Of those that a mesh axis runs over, the one named last changes fastest.
Arguments:
- low_feats: bfloat16 [128, 512, 256], P('rows', 'cols'), may hold values from -6 to 6
- skip_feats: bfloat16 [256, 1024, 256], P('rows', 'cols'), may hold values from -6 to 6
- tissue_mask: int32 [64, 256], P('rows', 'cols'), may hold values 0 or 1
- owner_slot: int32 [64, 256], P('rows', 'cols'), may hold values from 0 to 16383, as said below
- filter_one: bfloat16 [32, 3, 3, 256], replicated, may hold values from -0.125 to 0.125
- filter_two: bfloat16 [32, 3, 3, 256], replicated, may hold values from -0.125 to 0.125
- out_grad: bfloat16 [256, 1024, 256], P('rows', 'cols'), may hold values from -6 to 6
Outputs:
- output: bfloat16 [256, 1024, 256], P('rows', 'cols')
- skip_grad: bfloat16 [16384, 4, 4, 256], P(('rows', 'cols'))
- low_grad: bfloat16 [128, 512, 256], P('rows', 'cols')
- filter_grad_one: float32 [32, 3, 3, 256], replicated
- filter_grad_two: float32 [32, 3, 3, 256], replicated
Inputs may be any that keep to these rules, and one draw needn't show every extreme that they name: `owner_slot`: all values are distinct, so every encoder slot receives exactly one tile: each owner gets exactly 128 tiles. At most 2 tiles of one device go to one owner, and every device sends exactly 2 tiles to some owner.
All inputs are finite; a program needn't handle non-finite values. No bound on the sum of `tissue_mask` on one device may be relied on, other than what follows from the above.
Results may differ from a plain program's by a relative error of at most 0.006.
Values may be sent and summed in bfloat16 or wider, within the bound.
No kernel may reach another device: no remote copies, remote signals or barrier semaphores. Data moves between devices by JAX's collectives and lax.ppermute only.
A program may use at most 128 MiB of HBM per device.

v0:
```python
import math

import jax
import jax.numpy as jnp
import numpy as np
from jax import lax
from jax.sharding import PartitionSpec as P

G = 8


def padded_2(cells, sides, width):
    for axis, dim in sides:
        count = lax.axis_size(axis)
        ends = count - 1
        head = lax.slice_in_dim(cells, 0, width, axis=dim)
        tail = lax.slice_in_dim(cells, cells.shape[dim] - width, cells.shape[dim], axis=dim)
        cells = jnp.concatenate(
            [
                lax.ppermute(tail, axis, [(i, (i + 1) % count) for i in range(ends)]),
                cells,
                lax.ppermute(head, axis, [((i + 1) % count, i) for i in range(ends)]),
            ],
            axis=dim,
        )
    return cells


def element_inverse(element):
    mirror = element // 4
    turns = element % 4
    return np.where(mirror == 0, (4 - turns) % 4, element)


def element_product(first, second):
    mirror = (first // 4 + second // 4) % 2
    turns = (first % 4 + (1 - 2 * (first // 4)) * (second % 4)) % 4
    return mirror * 4 + turns


def element_act(element, row_off, col_off):
    mirror = element // 4
    turns = element % 4
    col_now = np.where(mirror == 1, -col_off, col_off)
    row_now = row_off
    for step in range(3):
        rotated_row = -col_now
        rotated_col = row_now
        row_now = np.where(turns > step, rotated_row, row_now)
        col_now = np.where(turns > step, rotated_col, col_now)
    return (row_now, col_now)


def cell_source(inverse, row_in, col_in):
    moved_row, moved_col = element_act(
        np.array(inverse), np.array(row_in - 1), np.array(col_in - 1)
    )
    return (int(moved_row) + 1, int(moved_col) + 1)


def expand(base):
    channels = base.shape[0]
    features = base.shape[3]
    split = base.reshape(channels, 3, 3, features // G, G)
    per_elem = []
    for out_elem in range(G):
        inverse = int(element_inverse(np.array(out_elem)))
        permuted = jnp.stack(
            [
                split[..., int(element_product(np.array(inverse), np.array(h_elem)))]
                for h_elem in range(G)
            ],
            axis=-1,
        ).reshape(channels, 3, 3, features)
        cell_rows = []
        for row_in in range(3):
            cell_line = []
            for col_in in range(3):
                src_row, src_col = cell_source(inverse, row_in, col_in)
                cell_line.append(permuted[:, src_row, src_col, :])
            cell_rows.append(jnp.stack(cell_line))
        per_elem.append(jnp.stack(cell_rows).transpose(0, 1, 3, 2))
    return jnp.stack(per_elem, axis=-1).reshape(3, 3, features, channels * G)


def fold_filter(grad_full, channels):
    features = channels * G
    shaped = grad_full.reshape(3, 3, features, channels, G)
    total = jnp.zeros((channels, 3, 3, features), jnp.float32)
    for out_elem in range(G):
        inverse = int(element_inverse(np.array(out_elem)))
        piece = shaped[..., out_elem].transpose(3, 0, 1, 2)
        placed = {}
        for row_in in range(3):
            for col_in in range(3):
                placed[cell_source(inverse, row_in, col_in)] = piece[:, row_in, col_in, :]
        moved = jnp.stack(
            [
                jnp.stack([placed[row_to, col_to] for col_to in range(3)], axis=1)
                for row_to in range(3)
            ],
            axis=1,
        )
        moved = moved.reshape(channels, 3, 3, features // G, G)
        source_of = {}
        for h_elem in range(G):
            source_of[int(element_product(np.array(inverse), np.array(h_elem)))] = h_elem
        back = jnp.stack([moved[..., source_of[m_elem]] for m_elem in range(G)], axis=-1).reshape(
            channels, 3, 3, features
        )
        total = total + back
    return total


def extend(field):
    return padded_2(field, (("rows", 0), ("cols", 1)), 1)


def conv_valid(padded, kernel):
    result = lax.conv_general_dilated(
        padded[None],
        kernel,
        (1, 1),
        "VALID",
        dimension_numbers=("NHWC", "HWIO", "NHWC"),
        preferred_element_type=jnp.float32,
    )
    return result[0]


def flipped(kernel):
    return jnp.flip(kernel, (0, 1)).transpose(0, 1, 3, 2)


def filter_terms(padded, grad_out):
    height = grad_out.shape[0]
    breadth = grad_out.shape[1]
    flat_grad = grad_out.reshape(-1, grad_out.shape[2])
    stacked = []
    for row_off in range(3):
        for col_off in range(3):
            window = padded[row_off : row_off + height, col_off : col_off + breadth].reshape(
                -1, padded.shape[2]
            )
            stacked.append(
                lax.dot_general(
                    window, flat_grad, (((0,), (0,)), ((), ())), preferred_element_type=jnp.float32
                )
            )
    return jnp.stack(stacked).reshape(3, 3, padded.shape[2], grad_out.shape[2])


def silu_slope(value):
    sigma = jax.nn.sigmoid(value)
    return sigma * (1.0 + value * (1.0 - sigma))


def return_tiles(tiles, slot_list):
    row_devices = lax.axis_size("rows")
    col_devices = lax.axis_size("cols")
    owners_all = row_devices * col_devices
    tile_count = tiles.shape[0]
    per_owner = 2 * tile_count // owners_all
    owner = slot_list // tile_count
    local_slot = slot_list % tile_count
    same_owner = owner[:, None] == owner[None, :]
    earlier = local_slot[None, :] < local_slot[:, None]
    within = jnp.sum((same_owner & earlier).astype(jnp.int32), axis=1)
    place = owner * per_owner + within
    positions = jnp.arange(owners_all * per_owner, dtype=jnp.int32)
    picked = place[None, :] == positions[:, None]
    send_tiles = jnp.dot(
        picked.astype(jnp.bfloat16), tiles, preferred_element_type=jnp.float32
    ).astype(jnp.bfloat16)
    send_slots = (
        jnp.sum(jnp.where(picked, local_slot[None, :] + 1, 0), axis=1).astype(jnp.int32) - 1
    )
    got_tiles, got_slots = (
        lax.all_to_all(send_tiles, ("rows", "cols"), split_axis=0, concat_axis=0, tiled=True),
        lax.all_to_all(send_slots, ("rows", "cols"), split_axis=0, concat_axis=0, tiled=True),
    )
    targets = jnp.arange(tile_count, dtype=jnp.int32)
    placed = (got_slots[None, :] == targets[:, None]).astype(jnp.bfloat16)
    return jnp.dot(placed, got_tiles, preferred_element_type=jnp.float32).astype(jnp.bfloat16)


def on_device(low_feats, skip_feats, tissue_mask, owner_slot, filter_one, filter_two, out_grad):
    tile_rows, tile_cols = tissue_mask.shape
    height, breadth, features = skip_feats.shape
    side = height // tile_rows
    channels = filter_one.shape[0]
    pixel_mask = jnp.broadcast_to(
        tissue_mask.astype(jnp.float32)[:, None, :, None], (tile_rows, side, tile_cols, side)
    ).reshape(height, breadth, 1)
    upsampled = jnp.broadcast_to(
        low_feats[:, None, :, None, :], (height // 2, 2, breadth // 2, 2, features)
    ).reshape(height, breadth, features)
    merged = ((upsampled.astype(jnp.float32) + skip_feats.astype(jnp.float32)) * pixel_mask).astype(
        jnp.bfloat16
    )
    kernel_one = expand(filter_one)
    kernel_two = expand(filter_two)
    grad_two = (out_grad.astype(jnp.float32) * pixel_mask).astype(jnp.bfloat16)
    padded_merged = extend(merged)
    pre_one = conv_valid(padded_merged, kernel_one)
    hidden = (jax.nn.silu(pre_one) * pixel_mask).astype(jnp.bfloat16)
    padded_hidden = extend(hidden)
    output = (conv_valid(padded_hidden, kernel_two) * pixel_mask).astype(jnp.bfloat16)
    grad_hidden = conv_valid(extend(grad_two), flipped(kernel_two))
    grad_pre = (grad_hidden * silu_slope(pre_one) * pixel_mask).astype(jnp.bfloat16)
    grad_merged = conv_valid(extend(grad_pre), flipped(kernel_one)) * pixel_mask
    tiles = (
        grad_merged.astype(jnp.bfloat16)
        .reshape(tile_rows, side, tile_cols, side, features)
        .transpose(0, 2, 1, 3, 4)
        .reshape(tile_rows * tile_cols, side * side * features)
    )
    skip_grad = return_tiles(tiles, owner_slot.reshape(-1)).reshape(
        tile_rows * tile_cols, side, side, features
    )
    low_grad = (
        grad_merged.reshape(height // 2, 2, breadth // 2, 2, features)
        .sum(axis=(1, 3))
        .astype(jnp.bfloat16)
    )
    local_one = fold_filter(filter_terms(padded_merged, grad_pre), channels)
    local_two = fold_filter(filter_terms(padded_hidden, grad_two), channels)
    total_one, total_two = lax.psum((local_one, local_two), ("rows", "cols"))
    device_count = lax.axis_size("rows") * lax.axis_size("cols")
    scale = 1.0 / math.sqrt(height * breadth * device_count)
    return (output, skip_grad, low_grad, total_one * scale, total_two * scale)


def solution(mesh):
    placed = (
        P("rows", "cols", None),
        P("rows", "cols", None),
        P("rows", "cols"),
        P("rows", "cols"),
        P(),
        P(),
        P("rows", "cols", None),
    )
    return jax.shard_map(
        on_device,
        mesh=mesh,
        in_specs=placed,
        out_specs=(
            P("rows", "cols", None),
            P(("rows", "cols"), None, None, None),
            P("rows", "cols", None),
            P(),
            P(),
        ),
        check_vma=False,
    )
```

profile of v0, /device:TPU:1, one launch (start us, length us, event | category | flops | bytes accessed | tf_op | source)
XLA Modules:
  0.0 696.6 jit_solution(8971407958032506310)
XLA Ops:
  8.7 1.9 broadcast_in_dim.28
  10.6 2.5 convert_element_type.50
  13.0 2.7 multiply_convert_fusion
  16.4 3.3 collective-permute-start.9
  19.8 3.1 collective-permute-start.8
  23.5 1.9 collective-permute-start.1
  25.4 3.6 collective-permute-start
  30.2 10.9 %all-to-all-start = ((s32[128,2,1]{1,2,0:T(1,128)}), s32[128,2,1]{1,2,0:T(1,128)}, u32[]{:S(2)}, u32[]{:S(2)}) async-start(s32[128,2,1]{1,2,0:T(1,128)} %bitcast.252), calls=%async_computation | async-start | bytes 131072 | tf_op jit(solution)/shard_map/all_to_all | solution.py:180
  43.7 2.0 fusion.217
  47.1 4.4 stack.1189
  51.5 3.4 stack.1198
  54.9 3.4 stack.1207
  58.3 3.3 stack.1216
  65.1 2.1 fusion.220
  68.6 4.4 stack.1117
  73.0 3.4 stack.1126
  76.4 3.4 stack.1135
  79.8 4.7 stack.1144
  84.5 3.7 maximum_bitcast_fusion.7
  180.7 2.9 maximum_bitcast_fusion.4
  283.4 6.8 stack.1225
  290.2 7.1 %stack.1153 = bf16[3,3,256,32,8]{2,4,3,1,0:T(8,128)(2,1)} concatenate(bf16[3,3,256,32,1]{2,4,3,1,0:T(2,128)(2,1)} %copy.327, bf16[3,3,256,32,1]{2,4,3,1,0:T(2,128)(2,1)} %copy.328, bf16[3,3,256,32,1]{2,4,3,1,0:T(2,128)(2,1)} %copy.329, bf16[3,3,256,32,1]{2,4,3,1,0:T(2,128)(2,1)} %copy.330, bf16[3,3,256,32,1]{2,4,3,1,0:T(2,128)(2,1)} %copy.331, ...), dimensions={4} | concatenate | bytes 2359296 | tf_op jit(solution)/shard_map/stack | solution.py:83
  302.3 4.0 collective-permute-start.10
  307.6 4.0 collective-permute-start.2
  314.8 3.2 convolution_select_fusion.1
  321.4 3.2 convolution_select_fusion.3
  325.6 2.9 fusion.6
  329.2 4.0 collective-permute-start.5
  333.2 2.6 collective-permute-start.4
  336.4 2.3 collective-permute-start.13
  338.7 3.2 collective-permute-start.12
  348.1 3.4 fusion.198
  353.0 1.9 fusion.212
  355.8 2.1 fusion.211
  358.8 1.9 fusion.210
  361.6 2.0 fusion.209
  375.5 3.8 stack.1346
  379.3 4.6 stack.1332
  383.9 4.6 stack.1318
  388.4 4.6 stack.1304
  393.0 6.5 fusion.48
  401.7 4.4 collective-permute-start.14
  408.1 4.8 collective-permute-start.6
  416.1 3.2 convolution_select_fusion
  422.0 2.2 squeeze.66
  427.3 3.2 convolution_select_fusion.2
  436.7 1.9 convolution_convert_fusion
  438.6 2.6 all_to_all.13
  441.3 16.7 %all-to-all-start.1 = ((bf16[128,2,4096]{2,1,0:T(2,128)(2,1)}), bf16[128,2,4096]{2,1,0:T(2,128)(2,1)S(1)}, u32[]{:S(2)}, u32[]{:S(2)}) async-start(bf16[128,2,4096]{2,1,0:T(2,128)(2,1)} %all_to_all.13), calls=%async_computation.1 | async-start | bytes 4194304 | tf_op jit(solution)/shard_map/all_to_all | solution.py:179
  458.0 3.2 multiply_reduce_fusion
  469.7 3.4 fusion.197
  474.8 1.9 fusion.205
  478.3 2.1 fusion.204
  482.0 1.9 fusion.203
  485.7 2.1 fusion.202
  501.7 3.8 stack.1467
  505.5 4.6 stack.1453
  510.1 4.6 stack.1439
  514.7 4.6 stack.1425
  519.2 6.6 fusion.94
  525.9 3.8 fusion.8
  529.7 149.2 %all-reduce.3.cloned.1.call-done = (f32[32,3,3,256]{0,3,2,1:T(8,128)}, f32[32,3,3,256]{0,3,2,1:T(8,128)}) async-done(((f32[32,3,3,256]{0,3,2,1:T(8,128)}, f32[32,3,3,256]{0,3,2,1:T(8,128)}), (f32[32,3,3,256]{0,3,2,1:T(8,128)}, f32[32,3,3,256]{0,3,2,1:T(8,128)})) %all-reduce.3.cloned.1.call-update) | async-done | bytes 589840 | tf_op jit(solution)/shard_map/psum | solution.py:228
  683.7 2.2 all_to_all.15
  685.9 2.0 convolution_convert_fusion.1
  (769 shorter events, 293.6 us)
Async XLA Ops:
  13.0 16.0 %copy-start.192 = (s32[8,16]{1,0:T(8,128)S(1)}, s32[8,16]{1,0:T(8,128)}, u32[]{:S(2)}) copy-start(s32[8,16]{1,0:T(8,128)} %param.10) | copy-start | bytes 1540
  13.0 28.1 %copy-start.66 = (bf16[32,3,3,256]{3,0,2,1:T(8,128)(2,1)S(1)}, bf16[32,3,3,256]{3,0,2,1:T(8,128)(2,1)}, u32[]{:S(2)}) copy-start(bf16[32,3,3,256]{3,0,2,1:T(8,128)(2,1)} %param.12) | copy-start | bytes 442372
  15.7 295.9 %copy-start = (bf16[32,64,256]{2,1,0:T(8,128)(2,1)}, bf16[32,64,256]{2,1,0:T(8,128)(2,1)S(1)}, u32[]{:S(2)}) copy-start(bf16[32,64,256]{2,1,0:T(8,128)(2,1)S(1)} %get-tuple-element.462) | copy-start | bytes 3145732
  16.4 283.8 %collective-permute-start.9 = (bf16[1,64,256]{2,1,0:T(8,128)(2,1)}, bf16[1,64,256]{2,1,0:T(8,128)(2,1)}, u32[]{:S(2)}, u32[]{:S(2)}) collective-permute-start(bf16[1,64,256]{2,1,0:T(8,128)(2,1)} %get-tuple-element.281), channel_id=1, source_target_pairs={{16,0},{32,16},{48,32},{64,48},{80,64},{96,80},{112,96},{17,1},{33... | collective-permute-start | bytes 98312 | tf_op jit(solution)/shard_map/ppermute | solution.py:22
  19.8 280.5 %collective-permute-start.8 = (bf16[1,64,256]{2,1,0:T(8,128)(2,1)}, bf16[1,64,256]{2,1,0:T(8,128)(2,1)}, u32[]{:S(2)}, u32[]{:S(2)}) collective-permute-start(bf16[1,64,256]{2,1,0:T(8,128)(2,1)} %get-tuple-element.280), channel_id=1, source_target_pairs={{0,16},{16,32},{32,48},{48,64},{64,80},{80,96},{96,112},{1,17},{17... | collective-permute-start | bytes 98312 | tf_op jit(solution)/shard_map/ppermute | solution.py:20
  23.5 282.8 %collective-permute-start.1 = (bf16[1,64,256]{2,1,0:T(8,128)(2,1)}, bf16[1,64,256]{2,1,0:T(8,128)(2,1)S(1)}, u32[]{:S(2)}, u32[]{:S(2)}) collective-permute-start(bf16[1,64,256]{2,1,0:T(8,128)(2,1)} %get-tuple-element.285), channel_id=1, source_target_pairs={{16,0},{32,16},{48,32},{64,48},{80,64},{96,80},{112,96},{17,1},{33... | collective-permute-start | bytes 98312 | tf_op jit(solution)/shard_map/ppermute | solution.py:22
  25.4 280.9 %collective-permute-start = (bf16[1,64,256]{2,1,0:T(8,128)(2,1)}, bf16[1,64,256]{2,1,0:T(8,128)(2,1)S(1)}, u32[]{:S(2)}, u32[]{:S(2)}) collective-permute-start(bf16[1,64,256]{2,1,0:T(8,128)(2,1)} %get-tuple-element.284), channel_id=1, source_target_pairs={{0,16},{16,32},{32,48},{48,64},{64,80},{80,96},{96,112},{1,17},{17... | collective-permute-start | bytes 98312 | tf_op jit(solution)/shard_map/ppermute | solution.py:20
  29.3 14.3 %copy-start.193 = (s32[128]{0:T(128)}, s32[128]{0:T(128)S(1)}, u32[]{:S(2)}) copy-start(s32[128]{0:T(128)S(1)} %multiply_add_fusion) | copy-start | bytes 1540
  30.2 267.1 %all-to-all-start = ((s32[128,2,1]{1,2,0:T(1,128)}), s32[128,2,1]{1,2,0:T(1,128)}, u32[]{:S(2)}, u32[]{:S(2)}) async-start(s32[128,2,1]{1,2,0:T(1,128)} %bitcast.252), calls=%async_computation | async-start | bytes 131072 | tf_op jit(solution)/shard_map/all_to_all | solution.py:180
  45.7 12.6 %copy-start.5 = (bf16[32,3,3,32,1]{0,4,3,2,1:T(2,128)(2,1)}, bf16[32,3,3,32,1]{0,4,3,2,1:T(2,128)(2,1)S(1)}, u32[]{:S(2)}) copy-start(bf16[32,3,3,32,1]{0,4,3,2,1:T(2,128)(2,1)S(1)} %get-tuple-element.327) | copy-start | bytes 55300
  45.7 12.6 %copy-start.7 = (bf16[32,3,3,32,1]{0,4,3,2,1:T(2,128)(2,1)}, bf16[32,3,3,32,1]{0,4,3,2,1:T(2,128)(2,1)S(1)}, u32[]{:S(2)}) copy-start(bf16[32,3,3,32,1]{0,4,3,2,1:T(2,128)(2,1)S(1)} %get-tuple-element.328) | copy-start | bytes 55300
  45.7 12.6 %copy-start.9 = (bf16[32,3,3,32,1]{0,4,3,2,1:T(2,128)(2,1)}, bf16[32,3,3,32,1]{0,4,3,2,1:T(2,128)(2,1)S(1)}, u32[]{:S(2)}) copy-start(bf16[32,3,3,32,1]{0,4,3,2,1:T(2,128)(2,1)S(1)} %get-tuple-element.329) | copy-start | bytes 55300
  79.8 4.7 copy-start.6
  79.8 4.7 copy-start.8
  79.8 4.7 copy-start.10
  88.2 12.8 %copy-start.62 = (bf16[32,3,3,32,2]{0,4,3,2,1:T(2,128)(2,1)S(1)}, bf16[32,3,3,32,2]{0,4,3,2,1:T(2,128)(2,1)}, u32[]{:S(2)}) copy-start(bf16[32,3,3,32,2]{0,4,3,2,1:T(2,128)(2,1)} %get-tuple-element.352) | copy-start | bytes 110596
  88.2 12.8 %copy-start.63 = (bf16[32,3,3,32,2]{0,4,3,2,1:T(2,128)(2,1)S(1)}, bf16[32,3,3,32,2]{0,4,3,2,1:T(2,128)(2,1)}, u32[]{:S(2)}) copy-start(bf16[32,3,3,32,2]{0,4,3,2,1:T(2,128)(2,1)} %get-tuple-element.353) | copy-start | bytes 110596
  88.2 12.8 %copy-start.64 = (bf16[32,3,3,32,2]{0,4,3,2,1:T(2,128)(2,1)S(1)}, bf16[32,3,3,32,2]{0,4,3,2,1:T(2,128)(2,1)}, u32[]{:S(2)}) copy-start(bf16[32,3,3,32,2]{0,4,3,2,1:T(2,128)(2,1)} %get-tuple-element.354) | copy-start | bytes 110596
  88.2 12.8 %copy-start.65 = (bf16[32,3,3,32,2]{0,4,3,2,1:T(2,128)(2,1)S(1)}, bf16[32,3,3,32,2]{0,4,3,2,1:T(2,128)(2,1)}, u32[]{:S(2)}) copy-start(bf16[32,3,3,32,2]{0,4,3,2,1:T(2,128)(2,1)} %get-tuple-element.355) | copy-start | bytes 110596
  101.8 12.8 %copy-start.24 = (bf16[32,3,3,256]{0,3,2,1:T(8,128)(2,1)S(1)}, bf16[32,3,3,256]{0,3,2,1:T(8,128)(2,1)}, u32[]{:S(2)}) copy-start(bf16[32,3,3,256]{0,3,2,1:T(8,128)(2,1)} %get-tuple-element.468) | copy-start | bytes 442372
  121.4 19.8 %copy-start.23 = (bf16[32,3,3,32,8]{0,4,3,2,1:T(8,128)(2,1)S(1)}, bf16[32,3,3,32,8]{0,4,3,2,1:T(8,128)(2,1)}, u32[]{:S(2)}) copy-start(bf16[32,3,3,32,8]{0,4,3,2,1:T(8,128)(2,1)} %stack.1198) | copy-start | bytes 442372
  148.1 19.8 %copy-start.22 = (bf16[32,3,3,32,8]{0,4,3,2,1:T(8,128)(2,1)S(1)}, bf16[32,3,3,32,8]{0,4,3,2,1:T(8,128)(2,1)}, u32[]{:S(2)}) copy-start(bf16[32,3,3,32,8]{0,4,3,2,1:T(8,128)(2,1)} %stack.1216) | copy-start | bytes 442372
  183.6 12.8 %copy-start.58 = (bf16[32,3,3,32,2]{0,4,3,2,1:T(2,128)(2,1)S(1)}, bf16[32,3,3,32,2]{0,4,3,2,1:T(2,128)(2,1)}, u32[]{:S(2)}) copy-start(bf16[32,3,3,32,2]{0,4,3,2,1:T(2,128)(2,1)} %get-tuple-element.431) | copy-start | bytes 110596
  183.6 12.8 %copy-start.59 = (bf16[32,3,3,32,2]{0,4,3,2,1:T(2,128)(2,1)S(1)}, bf16[32,3,3,32,2]{0,4,3,2,1:T(2,128)(2,1)}, u32[]{:S(2)}) copy-start(bf16[32,3,3,32,2]{0,4,3,2,1:T(2,128)(2,1)} %get-tuple-element.432) | copy-start | bytes 110596
  183.6 12.8 %copy-start.60 = (bf16[32,3,3,32,2]{0,4,3,2,1:T(2,128)(2,1)S(1)}, bf16[32,3,3,32,2]{0,4,3,2,1:T(2,128)(2,1)}, u32[]{:S(2)}) copy-start(bf16[32,3,3,32,2]{0,4,3,2,1:T(2,128)(2,1)} %get-tuple-element.433) | copy-start | bytes 110596
  183.6 12.8 %copy-start.61 = (bf16[32,3,3,32,2]{0,4,3,2,1:T(2,128)(2,1)S(1)}, bf16[32,3,3,32,2]{0,4,3,2,1:T(2,128)(2,1)}, u32[]{:S(2)}) copy-start(bf16[32,3,3,32,2]{0,4,3,2,1:T(2,128)(2,1)} %get-tuple-element.434) | copy-start | bytes 110596
  200.7 18.8 %copy-start.21 = (bf16[32,3,3,32,8]{0,4,3,2,1:T(8,128)(2,1)S(1)}, bf16[32,3,3,32,8]{0,4,3,2,1:T(8,128)(2,1)}, u32[]{:S(2)}) copy-start(bf16[32,3,3,32,8]{0,4,3,2,1:T(8,128)(2,1)} %stack.1117) | copy-start | bytes 442372
  213.5 18.8 %copy-start.20 = (bf16[32,3,3,32,8]{0,4,3,2,1:T(8,128)(2,1)S(1)}, bf16[32,3,3,32,8]{0,4,3,2,1:T(8,128)(2,1)}, u32[]{:S(2)}) copy-start(bf16[32,3,3,32,8]{0,4,3,2,1:T(8,128)(2,1)} %stack.1126) | copy-start | bytes 442372
  226.3 18.8 %copy-start.19 = (bf16[32,3,3,32,8]{0,4,3,2,1:T(8,128)(2,1)S(1)}, bf16[32,3,3,32,8]{0,4,3,2,1:T(8,128)(2,1)}, u32[]{:S(2)}) copy-start(bf16[32,3,3,32,8]{0,4,3,2,1:T(8,128)(2,1)} %stack.1135) | copy-start | bytes 442372
  239.1 18.8 %copy-start.18 = (bf16[32,3,3,32,8]{0,4,3,2,1:T(8,128)(2,1)S(1)}, bf16[32,3,3,32,8]{0,4,3,2,1:T(8,128)(2,1)}, u32[]{:S(2)}) copy-start(bf16[32,3,3,32,8]{0,4,3,2,1:T(8,128)(2,1)} %stack.1144) | copy-start | bytes 442372
  253.4 8.0 %copy-start.80 = (bf16[1,32,256]{2,1,0:T(8,128)(2,1)S(1)}, bf16[1,32,256]{2,1,0:T(8,128)(2,1)}, u32[]{:S(2)}) copy-start(bf16[1,32,256]{2,1,0:T(8,128)(2,1)} %get-tuple-element.444) | copy-start | bytes 49156
  257.9 4.6 copy-start.144
  258.0 4.6 copy-start.147
  258.0 4.6 copy-start.148
  258.0 4.6 copy-start.149
  258.0 4.6 copy-start.81
  258.0 4.6 copy-start.82
  258.0 4.6 copy-start.83
  258.0 4.6 copy-start.84
  258.0 4.6 copy-start.85
  258.1 4.6 copy-start.86
  277.6 4.9 copy-start.71
  301.0 10.7 %collective-permute-start.11 = (bf16[34,1,256]{2,1,0:T(2,128)(2,1)S(1)}, bf16[34,1,256]{2,1,0:T(2,128)(2,1)S(1)}, u32[]{:S(2)}, u32[]{:S(2)}) collective-permute-start(bf16[34,1,256]{2,1,0:T(2,128)(2,1)S(1)} %get-tuple-element.273), channel_id=1, source_target_pairs={{1,0},{2,1},{3,2},{4,3},{5,4},{6,5},{7,6},{8,7},{9,8},{10,9},{11,1... | collective-permute-start | bytes 52232 | tf_op jit(solution)/shard_map/ppermute | solution.py:22
  302.3 9.4 %collective-permute-start.10 = (bf16[34,1,256]{2,1,0:T(2,128)(2,1)S(1)}, bf16[34,1,256]{2,1,0:T(2,128)(2,1)S(1)}, u32[]{:S(2)}, u32[]{:S(2)}) collective-permute-start(bf16[34,1,256]{2,1,0:T(2,128)(2,1)S(1)} %get-tuple-element.272), channel_id=1, source_target_pairs={{0,1},{1,2},{2,3},{3,4},{4,5},{5,6},{6,7},{7,8},{8,9},{9,10},{10,1... | collective-permute-start | bytes 52232 | tf_op jit(solution)/shard_map/ppermute | solution.py:20
  306.3 12.6 %collective-permute-start.3 = (bf16[34,1,256]{2,1,0:T(2,128)(2,1)S(1)}, bf16[34,1,256]{2,1,0:T(2,128)(2,1)S(1)}, u32[]{:S(2)}, u32[]{:S(2)}) collective-permute-start(bf16[34,1,256]{2,1,0:T(2,128)(2,1)S(1)} %get-tuple-element.277), channel_id=1, source_target_pairs={{1,0},{2,1},{3,2},{4,3},{5,4},{6,5},{7,6},{8,7},{9,8},{10,9},{11,1... | collective-permute-start | bytes 52232 | tf_op jit(solution)/shard_map/ppermute | solution.py:22
  307.6 11.3 %collective-permute-start.2 = (bf16[34,1,256]{2,1,0:T(2,128)(2,1)S(1)}, bf16[34,1,256]{2,1,0:T(2,128)(2,1)S(1)}, u32[]{:S(2)}, u32[]{:S(2)}) collective-permute-start(bf16[34,1,256]{2,1,0:T(2,128)(2,1)S(1)} %get-tuple-element.276), channel_id=1, source_target_pairs={{0,1},{1,2},{2,3},{3,4},{4,5},{5,6},{6,7},{7,8},{8,9},{9,10},{10,1... | collective-permute-start | bytes 52232 | tf_op jit(solution)/shard_map/ppermute | solution.py:20
  328.5 18.9 %copy-start.2 = (bf16[32,64,256]{2,1,0:T(8,128)(2,1)}, bf16[32,64,256]{2,1,0:T(8,128)(2,1)S(1)}, u32[]{:S(2)}) copy-start(bf16[32,64,256]{2,1,0:T(8,128)(2,1)S(1)} %get-tuple-element.40) | copy-start | bytes 3145732
  329.2 76.9 %collective-permute-start.5 = (bf16[1,64,256]{2,1,0:T(8,128)(2,1)}, bf16[1,64,256]{2,1,0:T(8,128)(2,1)S(1)}, u32[]{:S(2)}, u32[]{:S(2)}) collective-permute-start(bf16[1,64,256]{2,1,0:T(8,128)(2,1)} %get-tuple-element.283), channel_id=1, source_target_pairs={{16,0},{32,16},{48,32},{64,48},{80,64},{96,80},{112,96},{17,1},{33... | collective-permute-start | bytes 98312 | tf_op jit(solution)/shard_map/ppermute | solution.py:22
  333.2 72.9 %collective-permute-start.4 = (bf16[1,64,256]{2,1,0:T(8,128)(2,1)}, bf16[1,64,256]{2,1,0:T(8,128)(2,1)}, u32[]{:S(2)}, u32[]{:S(2)}) collective-permute-start(bf16[1,64,256]{2,1,0:T(8,128)(2,1)} %get-tuple-element.282), channel_id=1, source_target_pairs={{0,16},{16,32},{32,48},{48,64},{64,80},{80,96},{96,112},{1,17},{17... | collective-permute-start | bytes 98312 | tf_op jit(solution)/shard_map/ppermute | solution.py:20
  336.4 63.2 %collective-permute-start.13 = (bf16[1,64,256]{2,1,0:T(8,128)(2,1)}, bf16[1,64,256]{2,1,0:T(8,128)(2,1)}, u32[]{:S(2)}, u32[]{:S(2)}) collective-permute-start(bf16[1,64,256]{2,1,0:T(8,128)(2,1)} %get-tuple-element.279), channel_id=1, source_target_pairs={{16,0},{32,16},{48,32},{64,48},{80,64},{96,80},{112,96},{17,1},{33... | collective-permute-start | bytes 98312 | tf_op jit(solution)/shard_map/ppermute | solution.py:22
  338.7 60.9 %collective-permute-start.12 = (bf16[1,64,256]{2,1,0:T(8,128)(2,1)}, bf16[1,64,256]{2,1,0:T(8,128)(2,1)}, u32[]{:S(2)}, u32[]{:S(2)}) collective-permute-start(bf16[1,64,256]{2,1,0:T(8,128)(2,1)} %get-tuple-element.278), channel_id=1, source_target_pairs={{0,16},{16,32},{32,48},{48,64},{64,80},{80,96},{96,112},{1,17},{17... | collective-permute-start | bytes 98312 | tf_op jit(solution)/shard_map/ppermute | solution.py:20
  364.5 5.1 copy-start.25
  364.5 5.1 copy-start.26
  364.5 5.1 copy-start.27
  364.5 5.1 copy-start.28
  393.0 6.6 copy-start.3
  400.4 12.6 %collective-permute-start.15 = (bf16[34,1,256]{2,1,0:T(2,128)(2,1)S(1)}, bf16[34,1,256]{2,1,0:T(2,128)(2,1)S(1)}, u32[]{:S(2)}, u32[]{:S(2)}) collective-permute-start(bf16[34,1,256]{2,1,0:T(2,128)(2,1)S(1)} %get-tuple-element.271), channel_id=1, source_target_pairs={{1,0},{2,1},{3,2},{4,3},{5,4},{6,5},{7,6},{8,7},{9,8},{10,9},{11,1... | collective-permute-start | bytes 52232 | tf_op jit(solution)/shard_map/ppermute | solution.py:22
  401.7 11.3 %collective-permute-start.14 = (bf16[34,1,256]{2,1,0:T(2,128)(2,1)S(1)}, bf16[34,1,256]{2,1,0:T(2,128)(2,1)S(1)}, u32[]{:S(2)}, u32[]{:S(2)}) collective-permute-start(bf16[34,1,256]{2,1,0:T(2,128)(2,1)S(1)} %get-tuple-element.270), channel_id=1, source_target_pairs={{0,1},{1,2},{2,3},{3,4},{4,5},{5,6},{6,7},{7,8},{8,9},{9,10},{10,1... | collective-permute-start | bytes 52232 | tf_op jit(solution)/shard_map/ppermute | solution.py:20
  406.1 8.4 %copy-start.68 = (bf16[1,64,256]{2,1,0:T(8,128)(2,1)}, bf16[1,64,256]{2,1,0:T(8,128)(2,1)S(1)}, u32[]{:S(2)}) copy-start(bf16[1,64,256]{2,1,0:T(8,128)(2,1)S(1)} %collective-permute-done.5) | copy-start | bytes 98308
  406.8 17.4 %collective-permute-start.7 = (bf16[34,1,256]{2,1,0:T(2,128)(2,1)S(1)}, bf16[34,1,256]{2,1,0:T(2,128)(2,1)S(1)}, u32[]{:S(2)}, u32[]{:S(2)}) collective-permute-start(bf16[34,1,256]{2,1,0:T(2,128)(2,1)S(1)} %get-tuple-element.275), channel_id=1, source_target_pairs={{1,0},{2,1},{3,2},{4,3},{5,4},{6,5},{7,6},{8,7},{9,8},{10,9},{11,1... | collective-permute-start | bytes 52232 | tf_op jit(solution)/shard_map/ppermute | solution.py:22
  408.1 16.1 %collective-permute-start.6 = (bf16[34,1,256]{2,1,0:T(2,128)(2,1)S(1)}, bf16[34,1,256]{2,1,0:T(2,128)(2,1)S(1)}, u32[]{:S(2)}, u32[]{:S(2)}) collective-permute-start(bf16[34,1,256]{2,1,0:T(2,128)(2,1)S(1)} %get-tuple-element.274), channel_id=1, source_target_pairs={{0,1},{1,2},{2,3},{3,4},{4,5},{5,6},{6,7},{7,8},{8,9},{9,10},{10,1... | collective-permute-start | bytes 52232 | tf_op jit(solution)/shard_map/ppermute | solution.py:20
  441.3 16.7 %copy-start.73 = (f32[16,32]{0,1:T(8,128)S(1)}, f32[16,32]{0,1:T(8,128)}, u32[]{:S(2)}) copy-start(f32[16,32]{0,1:T(8,128)} %copy.425) | copy-start | bytes 6148
  441.3 242.4 %all-to-all-start.1 = ((bf16[128,2,4096]{2,1,0:T(2,128)(2,1)}), bf16[128,2,4096]{2,1,0:T(2,128)(2,1)S(1)}, u32[]{:S(2)}, u32[]{:S(2)}) async-start(bf16[128,2,4096]{2,1,0:T(2,128)(2,1)} %all_to_all.13), calls=%async_computation.1 | async-start | bytes 4194304 | tf_op jit(solution)/shard_map/all_to_all | solution.py:179
  458.0 220.9 %all-reduce.3.cloned.1.call-start = ((), (), s32[]{:S(2)}) async-start(), calls=%async_computation.2 | async-start | bytes 4718592 | tf_op jit(solution)/shard_map/psum | solution.py:228
  (152 other events, 341.7 us)
Sparse Core Ops, SparseCore 0:
  526.0 152.7 all-reduce.2
where the time goes:
time: 711 us; the launch traced here: 697 us
  local copies, waits for them, and re-layouts  369 us (52%)
  waiting for transfers between devices  149 us (21%)
  starting transfers between devices  74 us (10%)
  other arithmetic  58.4 us (8%)
  matrix products  28 us (4%)
  between operations  18.2 us (3%)
    another operation x142, local copies, waits for them, and re-layouts, expand(): cell_rows.append(jnp.stack(cell_line))  169 us
    psum x1, waiting for transfers between devices, on_device(): total_one, total_two = lax.psum((local_one, local_two), ('rows', 'cols'))  149 us
    another operation x8, local copies, waits for them, and re-layouts, fold_filter(): jnp.stack([moved[..., source_of[m_elem]] for m_elem in range(G)], axis=-1)  35.1 us
    unnamed x419, local copies, waits for them, and re-layouts  33 us
    another operation x8, local copies, waits for them, and re-layouts, expand(): jnp.stack([split[..., int(element_product(np.array(inverse), np.array(h_e...  30.4 us
    ppermute x8, starting transfers between devices, padded_2(): lax.ppermute(tail, axis, [(i, (i + 1) % count) for i in range(ends)])  29.7 us
    another operation x18, local copies, waits for them, and re-layouts, expand(): return jnp.stack(per_elem, axis=-1).reshape(3, 3, features, channels * G)  26.5 us
    slice x14, local copies, waits for them, and re-layouts, fold_filter(): moved[..., source_of[m_elem]]  23.5 us
  transfers between devices with their start and end apart: 19, of which 1 were waited for; matrix products, arithmetic and copies ran while one was open for 59% of the time, Pallas kernels for 0%

commit v1 on v0

v1 whole, which is shorter than its diff:
```python
import functools
import math

import jax
import jax.numpy as jnp
import numpy as np
from jax import lax
from jax.experimental import pallas as pl
from jax.experimental.pallas import tpu as pltpu
from jax.sharding import PartitionSpec as P

G = 8
F = 256
ROWS = 32
WIDE = 64
STRIP = 48
MASK_ROWS = 16
BF = jnp.bfloat16
F32 = jnp.float32
VMEM = pl.BlockSpec(memory_space=pltpu.VMEM)
SMEM = pl.BlockSpec(memory_space=pltpu.SMEM)


def inverse_of(element):
    return (4 - element % 4) % 4 if element < 4 else element


def product(first, second):
    mirror = (first // 4 + second // 4) % 2
    turns = (first % 4 + (1 - 2 * (first // 4)) * (second % 4)) % 4
    return mirror * 4 + turns


def act(element, row, col):
    if element // 4:
        col = -col
    for _ in range(element % 4):
        row, col = -col, row
    return row, col


def source_cell(elem, pos):
    row, col = act(inverse_of(elem), pos // 3 - 1, pos % 3 - 1)
    return (row + 1) * 3 + col + 1


def iota(shape, dim):
    return lax.broadcasted_iota(jnp.int32, shape, dim)


def one_hot(cond):
    return jnp.where(cond, 1.0, 0.0).astype(BF)


def permuted_index(index, elem):
    inverse = inverse_of(elem)
    mirror, turns = inverse // 4, inverse % 4
    second = index & 7
    new_mirror = (second >> 2) ^ mirror
    spin = second & 3
    new_turns = (turns + (-spin if mirror else spin)) & 3
    return (index & ~7) | (new_mirror << 2) | new_turns


def dot(lhs, rhs):
    return jnp.dot(lhs, rhs, preferred_element_type=F32)


def dot_nt(lhs, rhs):
    return lax.dot_general(lhs, rhs, (((1,), (1,)), ((), ())), preferred_element_type=F32)


def call(kernel, out_shape, n_in, scratch=(), specs=None, flops=1 << 30, limit=40 << 20, name=None):
    return pl.pallas_call(
        kernel,
        out_shape=out_shape,
        in_specs=specs or [VMEM] * n_in,
        out_specs=jax.tree.map(lambda _: VMEM, out_shape),
        scratch_shapes=list(scratch),
        compiler_params=pltpu.CompilerParams(vmem_limit_bytes=limit),
        cost_estimate=pl.CostEstimate(flops=flops, bytes_accessed=4 << 20, transcendentals=0),
        name=name,
    )


def shape(dims, dtype=BF):
    return jax.ShapeDtypeStruct(dims, dtype)


def prep_kernel(low, skip, grad, mask_rows, merged, grad_two, up, down):
    spread = one_hot((iota((WIDE, 16), 0) >> 2) == iota((WIDE, 16), 1))
    twice = one_hot((iota((WIDE, 32), 0) >> 1) == iota((WIDE, 32), 1))
    for tile_row in range(8):
        mask = dot(spread, mask_rows[tile_row * 16 : tile_row * 16 + 16, :].astype(BF))
        for half in range(2):
            low_row = tile_row * 2 + half
            coarse = dot(twice, low[low_row * 32 : low_row * 32 + 32, :])
            for sub in range(2):
                here = pl.ds((low_row * 2 + sub) * WIDE, WIDE)
                merged[here, :] = ((coarse + skip[here, :].astype(F32)) * mask).astype(BF)
                grad_two[here, :] = (grad[here, :].astype(F32) * mask).astype(BF)
    two = 2 * WIDE
    up[0:two, :] = merged[0:two, :]
    up[two : 2 * two, :] = grad_two[0:two, :]
    up[2 * two : 2 * two + 16, :] = mask_rows[0:16, :].astype(BF)
    last = ROWS * WIDE - two
    down[0:two, :] = merged[last : last + two, :]
    down[two : 2 * two, :] = grad_two[last : last + two, :]
    down[2 * two : 2 * two + 16, :] = mask_rows[112:128, :].astype(BF)


def expand_kernel(filter_one, filter_two, fwd_one, fwd_two, bwd_one, bwd_two):
    across = iota((F, F), 0)
    along = iota((F, F), 1)
    weave = one_hot(((across & 7) * 32 + (across >> 3)) == along)
    perms = [one_hot(across == permuted_index(along, elem)) for elem in range(G)]
    for base, fwd, bwd in ((filter_one, fwd_one, bwd_one), (filter_two, fwd_two, bwd_two)):
        turned = [dot(base[...], perms[elem]).astype(BF) for elem in range(G)]
        for pos in range(9):
            rows = []
            for elem in range(G):
                cell = source_cell(elem, pos)
                rows.append(turned[elem][cell * 32 : cell * 32 + 32, :])
            gathered = jnp.concatenate(rows, axis=0)
            woven = dot(weave, gathered)
            bwd[(8 - pos) * F : (9 - pos) * F, :] = woven.astype(BF)
            fwd[pos * F : (pos + 1) * F, :] = woven.T.astype(BF)


def edge_kernel(merged, grad_two, top, bottom, mask_rows, left, right, tall, masks):
    two = 2 * WIDE
    tall[:, 36 * 16 : 48 * 16, :] = jnp.zeros((2, 12 * 16, 128), F32)

    def keep(row, values):
        for half in range(2):
            tall[half, row * 16 : row * 16 + 16, :] = values[:, half * 128 : half * 128 + 128].astype(F32)

    for side, (target, offset, picks, tile_col) in enumerate(
        ((left, 0, (0, 1), 0), (right, 48, (14, 15), 15))
    ):
        for image, source in enumerate((merged, grad_two)):
            for row in range(2):
                place = image * two + row * WIDE + offset
                keep(row, top[place : place + 16, :])
                keep(34 + row, bottom[place : place + 16, :])
            for row in range(ROWS):
                place = row * WIDE + offset
                keep(row + 2, source[place : place + 16, :])
            for col in range(2):
                strip = (image * 2 + col) * STRIP
                for half in range(2):
                    target[strip : strip + STRIP, half * 128 : half * 128 + 128] = tall[
                        half, pl.ds(picks[col], STRIP, stride=16), :
                    ].astype(BF)
        masks[...] = jnp.zeros((STRIP, F), F32)
        above = top[2 * two : 2 * two + 16, :].astype(F32)
        below = bottom[2 * two : 2 * two + 16, :].astype(F32)
        masks[0:2, :] = jnp.broadcast_to(above[tile_col : tile_col + 1, :], (2, F))
        masks[34:36, :] = jnp.broadcast_to(below[tile_col : tile_col + 1, :], (2, F))
        for tile_row in range(8):
            at = tile_row * 16 + tile_col
            masks[2 + 4 * tile_row : 6 + 4 * tile_row, :] = jnp.broadcast_to(mask_rows[at : at + 1, :], (4, F))
        target[4 * STRIP : 5 * STRIP, :] = masks[...].astype(BF)


def shifted_store(target, at, value, plain, before, after):
    row = iota((WIDE, F), 0)
    target[pl.ds(at, WIDE), 0:F] = jnp.where(row == 0, before, pltpu.roll(value, 1, 0)).astype(BF)
    target[pl.ds(at, WIDE), F : 2 * F] = plain
    target[pl.ds(at, WIDE), 2 * F : 3 * F] = jnp.where(
        row == WIDE - 1, after, pltpu.roll(value, WIDE - 1, 0)
    ).astype(BF)


def conv(shifted, start, count, weight):
    lhs = jnp.concatenate([shifted[pl.ds(start + ky * WIDE, count), :] for ky in range(3)], axis=1)
    return dot(lhs, weight[...])


def main_kernel(
    slots, merged, grad_two, top, bottom, left, right, from_left, from_right, mask_rows,
    fwd_one, fwd_two, bwd_one, bwd_two,
    output, low_grad, send, slot_rows, merged_shift, hidden_shift, grad_pre,
    grad_shift, pre_shift, strips, edge, mask_wide, pre, grad_hidden, pair, tiles, count,
):
    two = 2 * WIDE
    spread = one_hot((iota((WIDE, 16), 0) >> 2) == iota((WIDE, 16), 1))
    mask_wide[0:WIDE, :] = dot(spread, top[2 * two : 2 * two + 16, :])
    mask_wide[9 * WIDE : 10 * WIDE, :] = dot(spread, bottom[2 * two : 2 * two + 16, :])
    for tile_row in range(8):
        mask_wide[(tile_row + 1) * WIDE : (tile_row + 2) * WIDE, :] = dot(
            spread, mask_rows[tile_row * 16 : tile_row * 16 + 16, :].astype(BF)
        )
    strip_pre = []
    for image, (source, target, weight) in enumerate(
        ((merged, merged_shift, fwd_one), (grad_two, grad_shift, bwd_two))
    ):
        first = image * 2 * STRIP
        columns = (
            from_left[first : first + STRIP, :],
            from_left[first + STRIP : first + 2 * STRIP, :],
            left[first : first + STRIP, :],
            right[first + STRIP : first + 2 * STRIP, :],
            from_right[first : first + STRIP, :],
            from_right[first + STRIP : first + 2 * STRIP, :],
        )
        for index, column in enumerate(columns):
            strips[index * STRIP : (index + 1) * STRIP, :] = column.astype(F32)
        for row in range(2):
            at = image * two + row * WIDE
            for halo, place in ((top, row), (bottom, 34 + row)):
                plain = halo[at : at + WIDE, :]
                shifted_store(
                    target, place * WIDE, plain.astype(F32), plain,
                    strips[STRIP + place : STRIP + place + 1, :],
                    strips[4 * STRIP + place : 4 * STRIP + place + 1, :],
                )

        def shift_row(row, _, source=source, target=target):
            plain = source[pl.ds(pl.multiple_of(row * WIDE, WIDE), WIDE), :]
            shifted_store(
                target, pl.multiple_of((row + 2) * WIDE, WIDE), plain.astype(F32), plain,
                strips[pl.ds(STRIP + 2 + row, 1), :],
                strips[pl.ds(4 * STRIP + 2 + row, 1), :],
            )
            return 0

        lax.fori_loop(0, ROWS, shift_row, 0)
        parts = []
        for ky in range(3):
            for kx in range(3):
                parts.append(
                    jnp.concatenate(
                        [
                            strips[kx * STRIP + ky : kx * STRIP + ky + 40, :],
                            strips[(kx + 3) * STRIP + ky : (kx + 3) * STRIP + ky + 40, :],
                        ],
                        axis=0,
                    ).astype(BF)
                )
        strip_pre.append(dot(jnp.concatenate(parts, axis=1), weight[...]))
    strips[0:STRIP, :] = from_left[4 * STRIP : 5 * STRIP, :].astype(F32)
    strips[STRIP : 2 * STRIP, :] = from_right[4 * STRIP : 5 * STRIP, :].astype(F32)
    strip_mask = jnp.concatenate([strips[1:41, :], strips[STRIP + 1 : STRIP + 41, :]], axis=0)
    sigma = jax.nn.sigmoid(strip_pre[0])
    edge[0:80, :] = (strip_pre[0] * sigma * strip_mask).astype(BF).astype(F32)
    edge[80:160, :] = (
        (strip_pre[1] * (sigma * (1.0 + strip_pre[0] * (1.0 - sigma))) * strip_mask).astype(BF).astype(F32)
    )

    def first_convs(step, _):
        at = pl.multiple_of(step * 544, 16)
        pre[pl.ds(at, 544), :] = conv(merged_shift, at, 544, fwd_one)
        grad_hidden[pl.ds(at, 544), :] = conv(grad_shift, at, 544, bwd_two)
        return 0

    lax.fori_loop(0, 4, first_convs, 0)

    def activate(row, _):
        at = pl.multiple_of(row * WIDE, WIDE)
        mask = mask_wide[pl.ds(pl.multiple_of(((row + 3) >> 2) * WIDE, WIDE), WIDE), :]
        value = pre[pl.ds(at, WIDE), :]
        sigma = jax.nn.sigmoid(value)
        hidden = value * sigma * mask
        slope = sigma * (1.0 + value * (1.0 - sigma))
        grad_value = grad_hidden[pl.ds(at, WIDE), :] * slope * mask
        shifted_store(
            hidden_shift, at, hidden, hidden.astype(BF), edge[pl.ds(row, 1), :], edge[pl.ds(40 + row, 1), :]
        )
        shifted_store(
            pre_shift, at, grad_value, grad_value.astype(BF),
            edge[pl.ds(80 + row, 1), :], edge[pl.ds(120 + row, 1), :],
        )
        return 0

    lax.fori_loop(0, ROWS + 2, activate, 0)
    grad_pre[...] = pre_shift[WIDE : 33 * WIDE, F : 2 * F]

    order = iota((F, F), 0)
    tile_order = one_hot(
        iota((F, F), 1) == (((order >> 2) & 3) * WIDE + (order >> 4) * 4 + (order & 3))
    )

    def second_convs(step, _):
        at = pl.multiple_of(step * 512, 512)
        masks = []
        for tile_row in range(2):
            mask = mask_wide[pl.ds(pl.multiple_of((step * 2 + tile_row + 1) * WIDE, WIDE), WIDE), :]
            masks.append(jnp.concatenate([mask] * 4, axis=0))
        mask = jnp.concatenate(masks, axis=0)
        output[pl.ds(at, 512), :] = (conv(hidden_shift, at, 512, fwd_two) * mask).astype(BF)
        grad_merged = conv(pre_shift, at, 512, bwd_one) * mask
        rounded = grad_merged.astype(BF)
        for tile_row in range(2):
            tiles[pl.ds(at + tile_row * F, F), :] = dot(
                tile_order, rounded[tile_row * F : (tile_row + 1) * F, :]
            ).astype(BF)
        for row in range(4):
            both = grad_merged[row * two : row * two + WIDE, :] + grad_merged[row * two + WIDE : row * two + two, :]
            for half in range(2):
                pair[half, row * WIDE : (row + 1) * WIDE, :] = both[:, half * 128 : half * 128 + 128]
        for half in range(2):
            low_grad[pl.ds(pl.multiple_of(step * 128, 128), 128), half * 128 : half * 128 + 128] = (
                pair[half, pl.ds(0, 128, stride=2), :] + pair[half, pl.ds(1, 128, stride=2), :]
            ).astype(BF)
        return 0

    lax.fori_loop(0, 4, second_convs, 0)

    def clear(index, _):
        count[index] = 0
        return 0

    lax.fori_loop(0, 128, clear, 0)
    slot_rows[...] = jnp.full((128, 128), -1.0, F32)
    lane = iota((1, 128), 1)

    def pack(tile, _):
        flat = slots[tile >> 4, tile & 15]
        owner = flat >> 7
        used = count[owner]
        count[owner] = used + 1
        send[pl.ds(pl.multiple_of((owner * 2 + used) * 16, 16), 16), :] = tiles[
            pl.ds(pl.multiple_of(tile * 16, 16), 16), :
        ]
        local = (flat & 127).astype(F32)
        slot_rows[pl.ds(owner, 1), :] = jnp.where(lane == used, local, slot_rows[pl.ds(owner, 1), :])
        return 0

    lax.fori_loop(0, 128, pack, 0)


def filter_kernel(merged_shift, hidden_shift, grad_pre, grad_two, slot_rows, message, folded):
    across = iota((F, F), 0)
    along = iota((F, F), 1)
    unweave = one_hot(((along & 7) * 32 + (along >> 3)) == across)
    perms = [one_hot(along == permuted_index(across, elem)) for elem in range(G)]
    back = jnp.concatenate(perms, axis=0)
    for index, (values, grads, skip) in enumerate(
        ((merged_shift, grad_pre, WIDE), (hidden_shift, grad_two, 0))
    ):
        turned = dot_nt(unweave, grads[...]).astype(BF)
        full = []
        for ky in range(3):
            start = skip + ky * WIDE
            full.append(dot(turned, values[start : start + ROWS * WIDE, :]).astype(BF))
        pieces = []
        for elem in range(G):
            of_cell = {source_cell(elem, pos): pos for pos in range(9)}
            rows = []
            for cell in range(9):
                pos = of_cell[cell]
                kx = pos % 3
                rows.append(full[pos // 3][elem * 32 : elem * 32 + 32, kx * F : (kx + 1) * F])
            pieces.append(jnp.concatenate(rows, axis=0))
        folded[index * 288 : (index + 1) * 288, :] = dot(jnp.concatenate(pieces, axis=1), back)
    folded[576:592, :] = jnp.zeros((16, F), F32)
    row = iota((16, 128), 0)
    for part in range(128):
        start, lanes = 9 * (part % 64), (part // 64) * 128
        data = folded[start : start + 16, lanes : lanes + 128]
        message[part, :, :] = jnp.where(row == 9, slot_rows[part : part + 1, :], data).astype(BF)


def sum_kernel(got, message, slots):
    total = jnp.zeros((16, 128), F32)
    for part in range(128):
        total = total + got[part, :, :].astype(F32)
    rounded = total.astype(BF)
    for part in range(128):
        message[part, :, :] = rounded
    slots[...] = got[:, 9, :].astype(F32).astype(jnp.int32)


def place_kernel(scale, slots, got, sums, skip_grad, one, two, folded):
    def put(index, _):
        for which in range(2):
            slot = slots[index, which]

            @pl.when(slot >= 0)
            def _():
                skip_grad[pl.ds(pl.multiple_of(slot * 16, 16), 16), :] = got[
                    pl.ds(pl.multiple_of((index * 2 + which) * 16, 16), 16), :
                ]

        return 0

    lax.fori_loop(0, 128, put, 0)
    for part in range(128):
        start, lanes = 9 * (part % 64), (part // 64) * 128
        folded[start : start + 16, lanes : lanes + 128] = sums[part, :, :].astype(F32) * scale
    one[...] = folded[0:288, :]
    two[...] = folded[288:576, :]


def shift(values, axis, step):
    size = lax.axis_size(axis)
    if step > 0:
        pairs = [(i, i + 1) for i in range(size - 1)]
    else:
        pairs = [(i + 1, i) for i in range(size - 1)]
    return lax.ppermute(values, axis, pairs)


def on_device(low_feats, skip_feats, tissue_mask, owner_slot, filter_one, filter_two, out_grad):
    everyone = ("rows", "cols")
    height, breadth, features = skip_feats.shape
    pixels = height * breadth
    mask_rows = jnp.broadcast_to(tissue_mask.astype(F32).reshape(128, 1), (128, F))
    merged, grad_two, up, down = call(
        prep_kernel,
        [shape((pixels, F)), shape((pixels, F)), shape((272, F)), shape((272, F))],
        4, name="prep",
    )(
        low_feats.reshape(-1, F), skip_feats.reshape(pixels, F), out_grad.reshape(pixels, F), mask_rows
    )
    bottom = shift(up, "rows", -1)
    top = shift(down, "rows", 1)
    bases = [f.transpose(1, 2, 0, 3).reshape(288, F) for f in (filter_one, filter_two)]
    fwd_one, fwd_two, bwd_one, bwd_two = call(
        expand_kernel, [shape((9 * F, F))] * 4, 2, name="expand"
    )(*bases)
    left, right = call(
        edge_kernel,
        [shape((5 * STRIP, F))] * 2,
        5, [pltpu.VMEM((2, 48 * 16, 128), F32), pltpu.VMEM((STRIP, F), F32)], name="edge",
    )(merged, grad_two, top, bottom, mask_rows)
    from_right = shift(left, "cols", -1)
    from_left = shift(right, "cols", 1)
    output, low_grad, send, slot_rows, merged_shift, hidden_shift, grad_pre = call(
        main_kernel,
        [
            shape((pixels, F)), shape((pixels // 4, F)), shape((4096, F)), shape((128, 128), F32),
            shape((36 * WIDE, 3 * F)), shape((34 * WIDE, 3 * F)), shape((pixels, F)),
        ],
        14,
        [
            pltpu.VMEM((36 * WIDE, 3 * F), BF), pltpu.VMEM((34 * WIDE, 3 * F), BF),
            pltpu.VMEM((6 * STRIP, F), F32), pltpu.VMEM((160, F), F32), pltpu.VMEM((10 * WIDE, F), F32),
            pltpu.VMEM((34 * WIDE, F), F32), pltpu.VMEM((34 * WIDE, F), F32),
            pltpu.VMEM((2, 4 * WIDE, 128), F32), pltpu.VMEM((pixels, F), BF), pltpu.SMEM((128,), jnp.int32),
        ],
        specs=[SMEM] + [VMEM] * 13, flops=10 << 30, name="convs",
    )(
        owner_slot, merged, grad_two, top, bottom, left, right, from_left, from_right, mask_rows,
        fwd_one, fwd_two, bwd_one, bwd_two,
    )
    got_tiles = lax.all_to_all(send.reshape(128, 32, F), everyone, 0, 0, tiled=True)
    message = call(
        filter_kernel, shape((128, 16, 128)), 5, [pltpu.VMEM((592, F), F32)], flops=6 << 30, name="filters"
    )(merged_shift, hidden_shift, grad_pre, grad_two, slot_rows)
    got_terms = lax.all_to_all(message, everyone, 0, 0, tiled=True)
    sums, slots = call(
        sum_kernel, [shape((128, 16, 128)), shape((128, 128), jnp.int32)], 1, name="sums"
    )(got_terms)
    got_sums = lax.all_to_all(sums, everyone, 0, 0, tiled=True)
    scale = 1.0 / math.sqrt(pixels * lax.axis_size("rows") * lax.axis_size("cols"))
    skip_grad, one, two = call(
        functools.partial(place_kernel, scale),
        [shape((2048, F)), shape((288, F), F32), shape((288, F), F32)],
        3, [pltpu.VMEM((592, F), F32)], specs=[SMEM, VMEM, VMEM], name="place",
    )(slots, got_tiles.reshape(4096, F), got_sums)
    return (
        output.reshape(height, breadth, F),
        skip_grad.reshape(128, 4, 4, F),
        low_grad.reshape(height // 2, breadth // 2, F),
        one.reshape(3, 3, 32, F).transpose(2, 0, 1, 3),
        two.reshape(3, 3, 32, F).transpose(2, 0, 1, 3),
    )


def solution(mesh):
    placed = (
        P("rows", "cols", None),
        P("rows", "cols", None),
        P("rows", "cols"),
        P("rows", "cols"),
        P(),
        P(),
        P("rows", "cols", None),
    )
    return jax.shard_map(
        on_device,
        mesh=mesh,
        in_specs=placed,
        out_specs=(
            P("rows", "cols", None),
            P(("rows", "cols"), None, None, None),
            P("rows", "cols", None),
            P(),
            P(),
        ),
        check_vma=False,
    )
```

time: 711 us -> 141 us (0.20); the launches traced: 697 us -> 141 us
  local copies, waits for them, and re-layouts: 369 us -> 6.67 us
  waiting for transfers between devices: 149 us -> 4.45 us
  blocking collectives: 0 us -> 78.4 us
  starting transfers between devices: 74 us -> 11.8 us
  other arithmetic: 58.4 us -> 0.69 us
  Pallas kernels: 0 us -> 37.7 us
  matrix products: 28 us -> 0 us
  between operations: 18.2 us -> 0.78 us
    another operation x192 -> x0, local copies, waits for them, and re-layouts: 267 us -> none  [the longest x142 169 us: expand(): cell_rows.append(jnp.stack(cell_line))]
    psum x1 -> x0, waiting for transfers between devices: 149 us -> none  [on_device(): total_one, total_two = lax.psum((local_one, local_two), ('rows', 'cols'))]
    all_to_all x0 -> x3, blocking collectives: none -> 78.4 us  [the longest x1 33 us: on_device(): lax.all_to_all(send.reshape(128, 32, F), everyone, 0, 0, tiled=True)]
    slice x26 -> x0, local copies, waits for them, and re-layouts: 42.8 us -> none  [the longest x14 23.5 us: fold_filter(): moved[..., source_of[m_elem]]]
    pallas_call x0 -> x7, Pallas kernels: none -> 37.7 us  [the longest x1 22.1 us: on_device(): call(main_kernel, [shape((pixels, F)), shape((pixels // 4, F)), shape((40...]
    ppermute x16 -> x4, starting transfers between devices: 46.4 us -> 11.8 us  [shift(): return lax.ppermute(values, axis, pairs)]
    unnamed x419 -> x14, local copies, waits for them, and re-layouts: 33 us -> 5.41 us
    all_to_all x2 -> x0, starting transfers between devices: 27.6 us -> none  [the longest x1 16.7 us: return_tiles(): lax.all_to_all(send_tiles, ('rows', 'cols'), split_axis=0, concat_axis=0,...]
  transfers between devices with their start and end apart: 19 -> 4, of which waited for: 1 -> 2; matrix products, arithmetic and copies ran while one was open for 59% -> 0% of each run, Pallas kernels for 0% -> 1%
where the time goes in v1:
time: 141 us
  blocking collectives  78.4 us (56%)
  Pallas kernels  37.7 us (27%)
  starting transfers between devices  11.8 us (8%)
  local copies, waits for them, and re-layouts  6.67 us (5%)
  waiting for transfers between devices  4.45 us (3%)
    all_to_all x1, blocking collectives, on_device(): lax.all_to_all(send.reshape(128, 32, F), everyone, 0, 0, tiled=True)  33 us
    all_to_all x1, blocking collectives, on_device(): got_terms = lax.all_to_all(message, everyone, 0, 0, tiled=True)  27.5 us
    pallas_call x1, Pallas kernels, on_device(): call(main_kernel, [shape((pixels, F)), shape((pixels // 4, F)), shape((40...  22.1 us
    all_to_all x1, blocking collectives, on_device(): got_sums = lax.all_to_all(sums, everyone, 0, 0, tiled=True)  17.9 us
    ppermute x4, starting transfers between devices, shift(): return lax.ppermute(values, axis, pairs)  11.8 us
    pallas_call x1, Pallas kernels, on_device(): call(filter_kernel, shape((128, 16, 128)), 5, [pltpu.VMEM((592, F), F32)]...  7.38 us
    unnamed x14, local copies, waits for them, and re-layouts  5.41 us
    pallas_call x1, Pallas kernels, on_device(): call(functools.partial(place_kernel, scale), [shape((2048, F)), shape((28...  5.33 us
  transfers between devices with their start and end apart: 4, of which 2 were waited for; matrix products, arithmetic and copies ran while one was open for 0% of the time, Pallas kernels for 1%

profile of v1, /device:TPU:1, one launch (start us, length us, event | category | flops | bytes accessed | tf_op | source)
XLA Modules:
  0.0 140.6 jit_solution(17759720657772167172)
XLA Ops:
  0.6 0.7 convert_element_type.3
  1.3 0.1 broadcast_in_dim.7
  1.4 0.1 broadcast_in_dim.8.mask_rows
  1.5 0.0 copy-start
  1.5 1.2 copy-done
  2.7 0.0 copy-start.1
  2.7 1.2 copy-done.1
  3.9 0.0 copy-start.2
  3.9 0.9 copy-done.2
  4.9 0.6 prep.1
  5.5 0.0 copy-start.3
  5.5 0.0 copy-start.4
  5.5 4.6 %collective-permute-start = (bf16[272,256]{1,0:T(8,128)(2,1)S(1)}, bf16[272,256]{1,0:T(8,128)(2,1)S(1)}, u32[]{:S(2)}, u32[]{:S(2)}) collective-permute-start(bf16[272,256]{1,0:T(8,128)(2,1)S(1)} %get-tuple-element.29), channel_id=1, source_target_pairs={{0,16},{16,32},{32,48},{48,64},{64,80},{80,96},{96,112},{1,17},{17... | collective-permute-start | bytes 417800 | tf_op jit(solution)/shard_map/ppermute | solution.py:402
  10.1 1.9 %collective-permute-start.1 = (bf16[272,256]{1,0:T(8,128)(2,1)S(1)}, bf16[272,256]{1,0:T(8,128)(2,1)S(1)}, u32[]{:S(2)}, u32[]{:S(2)}) collective-permute-start(bf16[272,256]{1,0:T(8,128)(2,1)S(1)} %get-tuple-element.30), channel_id=1, source_target_pairs={{16,0},{32,16},{48,32},{64,48},{80,64},{96,80},{112,96},{17,1},{33... | collective-permute-start | bytes 417800 | tf_op jit(solution)/shard_map/ppermute | solution.py:402
  12.1 0.1 collective-permute-done.top
  12.1 4.4 %collective-permute-done.1.bottom = bf16[272,256]{1,0:T(8,128)(2,1)S(1)} collective-permute-done((bf16[272,256]{1,0:T(8,128)(2,1)S(1)}, bf16[272,256]{1,0:T(8,128)(2,1)S(1)}, u32[]{:S(2)}, u32[]{:S(2)}) %collective-permute-start.1) | collective-permute-done | bytes 139296 | tf_op jit(solution)/shard_map/ppermute | solution.py:402
  16.5 0.3 edge.1
  16.8 0.0 copy-start.5
  16.8 1.3 collective-permute-start.3
  18.1 4.0 %collective-permute-start.2 = (bf16[240,256]{1,0:T(8,128)(2,1)S(1)}, bf16[240,256]{1,0:T(8,128)(2,1)S(1)}, u32[]{:S(2)}, u32[]{:S(2)}) collective-permute-start(bf16[240,256]{1,0:T(8,128)(2,1)S(1)} %get-tuple-element.32.right), channel_id=1, source_target_pairs={{0,1},{1,2},{2,3},{3,4},{4,5},{5,6},{6,7},{7,8},{8,9},{9,10},{10,1... | collective-permute-start | bytes 368648 | tf_op jit(solution)/shard_map/ppermute | solution.py:402
  22.1 0.0 copy-done.3
  22.1 0.0 copy-done.4
  22.1 1.9 %expand.1 = (bf16[2304,256]{1,0:T(8,128)(2,1)S(1)}, bf16[2304,256]{1,0:T(8,128)(2,1)S(1)}, bf16[2304,256]{1,0:T(8,128)(2,1)S(1)}, bf16[2304,256]{1,0:T(8,128)(2,1)S(1)}) custom-call(bf16[288,256]{1,0:T(8,128)(2,1)S(1)} %bitcast.24, bf16[288,256]{1,0:T(8,128)(2,1)S(1)} %bitcast.25), custom_call_target="tpu_custom_call" | custom-call | flops 1073741824 | bytes 4194304 | tf_op jit(solution)/shard_map/expand/pallas_call | solution.py:420
  24.1 0.0 collective-permute-done.3.from_right
  24.1 0.0 collective-permute-done.2.from_left
  24.1 0.0 copy-done.5
  24.1 22.1 %convs.1 = (bf16[2048,256]{1,0:T(8,128)(2,1)}, bf16[512,256]{1,0:T(8,128)(2,1)}, bf16[4096,256]{1,0:T(8,128)(2,1)S(1)}, f32[128,128]{1,0:T(8,128)S(1)}, bf16[230...) custom-call(s32[8,16]{1,0:T(8,128)S(1)} %copy-done.5, ...), custom_call_target="tpu_custom_call" | custom-call | flops 10737418240 | bytes 4194304 | tf_op jit(solution)/shard_map/convs/pallas_call | solution.py:430
  46.2 0.0 copy-start.6
  46.2 2.0 %copy-done.6 = bf16[2304,768]{1,0:T(8,128)(2,1)S(1)} copy-done((bf16[2304,768]{1,0:T(8,128)(2,1)S(1)}, bf16[2304,768]{1,0:T(8,128)(2,1)}, u32[]{:S(2)}) %copy-start.6) | copy-done | bytes 3538968
  48.2 7.4 %filters.1 = bf16[128,16,128]{2,1,0:T(8,128)(2,1)S(1)} custom-call(bf16[2304,768]{1,0:T(8,128)(2,1)S(1)} %copy-done.6, bf16[2176,768]{1,0:T(8,128)(2,1)S(1)} %get-tuple-element.39.hidden_shift, bf16[2048,256]{1,0:T(8,128)(2,1)S(1)} %get-tuple-element.40.grad_pre, bf16[2048,256]{1,0:T(8,128)(2,1)S(1)} %get-tuple-element.28.grad_two, ...), custom_call_target="tpu_custom_call" | custom-call | flops 6442450944 | bytes 4194304 | tf_op jit(solution)/shard_map/filters/pallas_call | solution.py:449
  55.6 27.5 %all_to_all.15.got = bf16[128,16,128]{2,1,0:T(8,128)(2,1)S(1)} all-to-all(bf16[128,16,128]{2,1,0:T(8,128)(2,1)S(1)} %filters.1), channel_id=1, replica_groups=mesh['rows'=8,'cols'=16] {'rows','cols'}, dimensions={0} | all-to-all | bytes 1048576 | tf_op jit(solution)/shard_map/all_to_all | solution.py:452
  83.1 0.2 sums.1
  83.3 17.9 %all_to_all.16.sums = bf16[128,16,128]{2,1,0:T(8,128)(2,1)S(1)} all-to-all(bf16[128,16,128]{2,1,0:T(8,128)(2,1)S(1)} %get-tuple-element.44), channel_id=1, replica_groups=mesh['rows'=8,'cols'=16] {'rows','cols'}, dimensions={0} | all-to-all | bytes 1048576 | tf_op jit(solution)/shard_map/all_to_all | solution.py:456
  101.1 33.0 %all_to_all.17 = bf16[128,32,256]{2,1,0:T(8,128)(2,1)S(1)} all-to-all(bf16[128,32,256]{2,1,0:T(8,128)(2,1)S(1)} %bitcast.19), channel_id=1, replica_groups=mesh['rows'=8,'cols'=16] {'rows','cols'}, dimensions={0} | all-to-all | bytes 4194304 | tf_op jit(solution)/shard_map/all_to_all | solution.py:448
  134.1 5.3 %place.1 = (bf16[2048,256]{1,0:T(8,128)(2,1)S(1)}, f32[288,256]{1,0:T(8,128)}, f32[288,256]{1,0:T(8,128)}) custom-call(s32[128,128]{1,0:T(8,128)S(1)} %get-tuple-element.42.slots, bf16[4096,256]{1,0:T(8,128)(2,1)S(1)} %bitcast.20, bf16[128,16,128]{2,1,0:T(8,128)(2,1)S(1)} %all_to_all.16.sums), custom_call_target="tpu_custom_call" | custom-call | flops 1073741824 | bytes 4194304 | tf_op jit(solution)/shard_map/place/pallas_call | solution.py:458
  139.5 1.1 reshape.56
Async XLA Ops:
  1.5 1.2 copy-start
  2.7 1.2 copy-start.1
  3.9 0.9 copy-start.2
  5.5 16.7 %copy-start.3 = (bf16[32,3,3,256]{3,0,2,1:T(8,128)(2,1)S(1)}, bf16[32,3,3,256]{3,0,2,1:T(8,128)(2,1)}, u32[]{:S(2)}) copy-start(bf16[32,3,3,256]{3,0,2,1:T(8,128)(2,1)} %param.11) | copy-start | bytes 442372
  5.5 16.7 %copy-start.4 = (bf16[32,3,3,256]{3,0,2,1:T(8,128)(2,1)S(1)}, bf16[32,3,3,256]{3,0,2,1:T(8,128)(2,1)}, u32[]{:S(2)}) copy-start(bf16[32,3,3,256]{3,0,2,1:T(8,128)(2,1)} %param.12) | copy-start | bytes 442372
  5.5 6.7 %collective-permute-start = (bf16[272,256]{1,0:T(8,128)(2,1)S(1)}, bf16[272,256]{1,0:T(8,128)(2,1)S(1)}, u32[]{:S(2)}, u32[]{:S(2)}) collective-permute-start(bf16[272,256]{1,0:T(8,128)(2,1)S(1)} %get-tuple-element.29), channel_id=1, source_target_pairs={{0,16},{16,32},{32,48},{48,64},{64,80},{80,96},{96,112},{1,17},{17... | collective-permute-start | bytes 417800 | tf_op jit(solution)/shard_map/ppermute | solution.py:402
  10.1 6.4 %collective-permute-start.1 = (bf16[272,256]{1,0:T(8,128)(2,1)S(1)}, bf16[272,256]{1,0:T(8,128)(2,1)S(1)}, u32[]{:S(2)}, u32[]{:S(2)}) collective-permute-start(bf16[272,256]{1,0:T(8,128)(2,1)S(1)} %get-tuple-element.30), channel_id=1, source_target_pairs={{16,0},{32,16},{48,32},{64,48},{80,64},{96,80},{112,96},{17,1},{33... | collective-permute-start | bytes 417800 | tf_op jit(solution)/shard_map/ppermute | solution.py:402
  16.8 7.3 %copy-start.5 = (s32[8,16]{1,0:T(8,128)S(1)}, s32[8,16]{1,0:T(8,128)}, u32[]{:S(2)}) copy-start(s32[8,16]{1,0:T(8,128)} %slots.1) | copy-start | bytes 1540
  16.8 7.3 %collective-permute-start.3 = (bf16[240,256]{1,0:T(8,128)(2,1)S(1)}, bf16[240,256]{1,0:T(8,128)(2,1)S(1)}, u32[]{:S(2)}, u32[]{:S(2)}) collective-permute-start(bf16[240,256]{1,0:T(8,128)(2,1)S(1)} %get-tuple-element.31.left), channel_id=1, source_target_pairs={{1,0},{2,1},{3,2},{4,3},{5,4},{6,5},{7,6},{8,7},{9,8},{10,9},{11,1... | collective-permute-start | bytes 368648 | tf_op jit(solution)/shard_map/ppermute | solution.py:402
  18.1 6.0 %collective-permute-start.2 = (bf16[240,256]{1,0:T(8,128)(2,1)S(1)}, bf16[240,256]{1,0:T(8,128)(2,1)S(1)}, u32[]{:S(2)}, u32[]{:S(2)}) collective-permute-start(bf16[240,256]{1,0:T(8,128)(2,1)S(1)} %get-tuple-element.32.right), channel_id=1, source_target_pairs={{0,1},{1,2},{2,3},{3,4},{4,5},{5,6},{6,7},{7,8},{8,9},{9,10},{10,1... | collective-permute-start | bytes 368648 | tf_op jit(solution)/shard_map/ppermute | solution.py:402
  46.2 2.0 %copy-start.6 = (bf16[2304,768]{1,0:T(8,128)(2,1)S(1)}, bf16[2304,768]{1,0:T(8,128)(2,1)}, u32[]{:S(2)}) copy-start(bf16[2304,768]{1,0:T(8,128)(2,1)} %get-tuple-element.38.merged_shift) | copy-start | bytes 10616836

commit v2 on v1

--- a/solution.py
+++ b/solution.py
@@ -180,8 +180,9 @@
 def main_kernel(
     slots, merged, grad_two, top, bottom, left, right, from_left, from_right, mask_rows,
     fwd_one, fwd_two, bwd_one, bwd_two,
-    output, low_grad, send, slot_rows, merged_shift, hidden_shift, grad_pre,
-    grad_shift, pre_shift, strips, edge, mask_wide, pre, grad_hidden, pair, tiles, count,
+    output, low_grad, send,
+    merged_shift, hidden_shift, grad_shift, pre_shift, strips, edge, mask_wide, pre, grad_hidden,
+    pair, tiles, slot_rows, folded, count,
 ):
     two = 2 * WIDE
     spread = one_hot((iota((WIDE, 16), 0) >> 2) == iota((WIDE, 16), 1))
@@ -274,8 +275,6 @@
         return 0
 
     lax.fori_loop(0, ROWS + 2, activate, 0)
-    grad_pre[...] = pre_shift[WIDE : 33 * WIDE, F : 2 * F]
-
     order = iota((F, F), 0)
     tile_order = one_hot(
         iota((F, F), 1) == (((order >> 2) & 3) * WIDE + (order >> 4) * 4 + (order & 3))
@@ -320,7 +319,7 @@
         owner = flat >> 7
         used = count[owner]
         count[owner] = used + 1
-        send[pl.ds(pl.multiple_of((owner * 2 + used) * 16, 16), 16), :] = tiles[
+        send[owner, pl.ds(pl.multiple_of(used * 16, 16), 16), :] = tiles[
             pl.ds(pl.multiple_of(tile * 16, 16), 16), :
         ]
         local = (flat & 127).astype(F32)
@@ -329,17 +328,18 @@
 
     lax.fori_loop(0, 128, pack, 0)
 
-
-def filter_kernel(merged_shift, hidden_shift, grad_pre, grad_two, slot_rows, message, folded):
     across = iota((F, F), 0)
     along = iota((F, F), 1)
     unweave = one_hot(((along & 7) * 32 + (along >> 3)) == across)
     perms = [one_hot(along == permuted_index(across, elem)) for elem in range(G)]
     back = jnp.concatenate(perms, axis=0)
     for index, (values, grads, skip) in enumerate(
-        ((merged_shift, grad_pre, WIDE), (hidden_shift, grad_two, 0))
+        (
+            (merged_shift, pre_shift[WIDE : 33 * WIDE, F : 2 * F], WIDE),
+            (hidden_shift, grad_two[...], 0),
+        )
     ):
-        turned = dot_nt(unweave, grads[...]).astype(BF)
+        turned = dot_nt(unweave, grads).astype(BF)
         full = []
         for ky in range(3):
             start = skip + ky * WIDE
@@ -355,37 +355,49 @@
             pieces.append(jnp.concatenate(rows, axis=0))
         folded[index * 288 : (index + 1) * 288, :] = dot(jnp.concatenate(pieces, axis=1), back)
     folded[576:592, :] = jnp.zeros((16, F), F32)
-    row = iota((16, 128), 0)
     for part in range(128):
         start, lanes = 9 * (part % 64), (part // 64) * 128
-        data = folded[start : start + 16, lanes : lanes + 128]
-        message[part, :, :] = jnp.where(row == 9, slot_rows[part : part + 1, :], data).astype(BF)
-
-
-def sum_kernel(got, message, slots):
-    total = jnp.zeros((16, 128), F32)
+        send[part, 32:40, 0:128] = folded[start : start + 8, lanes : lanes + 128].astype(BF)
+        tail = jnp.concatenate(
+            [
+                folded[start + 8 : start + 9, lanes : lanes + 128],
+                slot_rows[part : part + 1, :],
+                jnp.zeros((6, 128), F32),
+            ],
+            axis=0,
+        )
+        send[part, 32:40, 128:256] = tail.astype(BF)
+
+
+def sum_kernel(got, message, slots, gathered):
+    total = jnp.zeros((8, F), F32)
     for part in range(128):
-        total = total + got[part, :, :].astype(F32)
-    rounded = total.astype(BF)
+        terms = got[part, 32:40, :].astype(F32)
+        total = total + terms
+        gathered[part : part + 1, :] = terms[1:2, 128:256]
+    rounded = jnp.concatenate([total[:, 0:128], total[:, 128:256]], axis=0).astype(BF)
     for part in range(128):
         message[part, :, :] = rounded
-    slots[...] = got[:, 9, :].astype(F32).astype(jnp.int32)
-
-
-def place_kernel(scale, slots, got, sums, skip_grad, one, two, folded):
+    slots[...] = gathered[...].T[0:8, :].astype(jnp.int32)
+
+
+def place_kernel(slots, got, skip_grad):
     def put(index, _):
         for which in range(2):
-            slot = slots[index, which]
+            slot = slots[which, index]
 
             @pl.when(slot >= 0)
             def _():
                 skip_grad[pl.ds(pl.multiple_of(slot * 16, 16), 16), :] = got[
-                    pl.ds(pl.multiple_of((index * 2 + which) * 16, 16), 16), :
+                    index, which * 16 : which * 16 + 16, :
                 ]
 
         return 0
 
     lax.fori_loop(0, 128, put, 0)
+
+
+def finish_kernel(scale, sums, one, two, folded):
     for part in range(128):
         start, lanes = 9 * (part % 64), (part // 64) * 128
         folded[start : start + 16, lanes : lanes + 128] = sums[part, :, :].astype(F32) * scale
@@ -427,39 +439,35 @@
     )(merged, grad_two, top, bottom, mask_rows)
     from_right = shift(left, "cols", -1)
     from_left = shift(right, "cols", 1)
-    output, low_grad, send, slot_rows, merged_shift, hidden_shift, grad_pre = call(
+    output, low_grad, send = call(
         main_kernel,
-        [
-            shape((pixels, F)), shape((pixels // 4, F)), shape((4096, F)), shape((128, 128), F32),
-            shape((36 * WIDE, 3 * F)), shape((34 * WIDE, 3 * F)), shape((pixels, F)),
-        ],
+        [shape((pixels, F)), shape((pixels // 4, F)), shape((128, 40, F))],
         14,
         [
             pltpu.VMEM((36 * WIDE, 3 * F), BF), pltpu.VMEM((34 * WIDE, 3 * F), BF),
+            pltpu.VMEM((36 * WIDE, 3 * F), BF), pltpu.VMEM((34 * WIDE, 3 * F), BF),
             pltpu.VMEM((6 * STRIP, F), F32), pltpu.VMEM((160, F), F32), pltpu.VMEM((10 * WIDE, F), F32),
             pltpu.VMEM((34 * WIDE, F), F32), pltpu.VMEM((34 * WIDE, F), F32),
-            pltpu.VMEM((2, 4 * WIDE, 128), F32), pltpu.VMEM((pixels, F), BF), pltpu.SMEM((128,), jnp.int32),
+            pltpu.VMEM((2, 4 * WIDE, 128), F32), pltpu.VMEM((pixels, F), BF),
+            pltpu.VMEM((128, 128), F32), pltpu.VMEM((592, F), F32), pltpu.SMEM((128,), jnp.int32),
         ],
-        specs=[SMEM] + [VMEM] * 13, flops=10 << 30, name="convs",
+        specs=[SMEM] + [VMEM] * 13, flops=16 << 30, name="convs",
     )(
         owner_slot, merged, grad_two, top, bottom, left, right, from_left, from_right, mask_rows,
         fwd_one, fwd_two, bwd_one, bwd_two,
     )
-    got_tiles = lax.all_to_all(send.reshape(128, 32, F), everyone, 0, 0, tiled=True)
-    message = call(
-        filter_kernel, shape((128, 16, 128)), 5, [pltpu.VMEM((592, F), F32)], flops=6 << 30, name="filters"
-    )(merged_shift, hidden_shift, grad_pre, grad_two, slot_rows)
-    got_terms = lax.all_to_all(message, everyone, 0, 0, tiled=True)
+    got = lax.all_to_all(send, everyone, 0, 0, tiled=True)
     sums, slots = call(
-        sum_kernel, [shape((128, 16, 128)), shape((128, 128), jnp.int32)], 1, name="sums"
-    )(got_terms)
+        sum_kernel, [shape((128, 16, 128)), shape((8, 128), jnp.int32)], 1,
+        [pltpu.VMEM((128, 128), F32)], name="sums",
+    )(got)
     got_sums = lax.all_to_all(sums, everyone, 0, 0, tiled=True)
+    skip_grad = call(place_kernel, shape((2048, F)), 2, specs=[SMEM, VMEM], name="place")(slots, got)
     scale = 1.0 / math.sqrt(pixels * lax.axis_size("rows") * lax.axis_size("cols"))
-    skip_grad, one, two = call(
-        functools.partial(place_kernel, scale),
-        [shape((2048, F)), shape((288, F), F32), shape((288, F), F32)],
-        3, [pltpu.VMEM((592, F), F32)], specs=[SMEM, VMEM, VMEM], name="place",
-    )(slots, got_tiles.reshape(4096, F), got_sums)
+    one, two = call(
+        functools.partial(finish_kernel, scale),
+        [shape((288, F), F32), shape((288, F), F32)], 1, [pltpu.VMEM((592, F), F32)], name="finish",
+    )(got_sums)
     return (
         output.reshape(height, breadth, F),
         skip_grad.reshape(128, 4, 4, F),

time: 141 us -> 121 us (0.86)
  blocking collectives: 78.4 us -> 48 us
  waiting for transfers between devices: 4.45 us -> 11.8 us
  starting transfers between devices: 11.8 us -> 17 us
  Pallas kernels: 37.7 us -> 34.7 us
    all_to_all x3 -> x1, blocking collectives: 78.4 us -> 48 us  [on_device(): got = lax.all_to_all(send, everyone, 0, 0, tiled=True)]
    all_to_all x0 -> x1, waiting for transfers between devices: none -> 7.39 us  [on_device(): got_sums = lax.all_to_all(sums, everyone, 0, 0, tiled=True)]
    all_to_all x0 -> x1, starting transfers between devices: none -> 5.33 us  [on_device(): got_sums = lax.all_to_all(sums, everyone, 0, 0, tiled=True)]
    pallas_call x4, Pallas kernels: 35 us -> 31.9 us  [the longest x1 27.2 us: on_device(): call(main_kernel, [shape((pixels, F)), shape((pixels // 4, F)), shape((12...]
    unnamed x14 -> x16, local copies, waits for them, and re-layouts: 5.41 us -> 5.19 us
  transfers between devices with their start and end apart: 4 -> 5, of which waited for: 2 -> 3; matrix products, arithmetic and copies ran while one was open for 0% -> 2% of each run, Pallas kernels for 1% -> 5%
where the time goes in v2:
time: 121 us
  blocking collectives  48 us (40%)
  Pallas kernels  34.7 us (29%)
  starting transfers between devices  17 us (14%)
  waiting for transfers between devices  11.8 us (10%)
  local copies, waits for them, and re-layouts  7.48 us (6%)
    all_to_all x1, blocking collectives, on_device(): got = lax.all_to_all(send, everyone, 0, 0, tiled=True)  48 us
    pallas_call x1, Pallas kernels, on_device(): call(main_kernel, [shape((pixels, F)), shape((pixels // 4, F)), shape((12...  27.2 us
    ppermute x4, starting transfers between devices, shift(): return lax.ppermute(values, axis, pairs)  11.7 us
    all_to_all x1, waiting for transfers between devices, on_device(): got_sums = lax.all_to_all(sums, everyone, 0, 0, tiled=True)  7.39 us
    all_to_all x1, starting transfers between devices, on_device(): got_sums = lax.all_to_all(sums, everyone, 0, 0, tiled=True)  5.33 us
    unnamed x16, local copies, waits for them, and re-layouts  5.19 us
    ppermute x4, waiting for transfers between devices, shift(): return lax.ppermute(values, axis, pairs)  4.45 us
    pallas_call x1, Pallas kernels, on_device(): call(place_kernel, shape((2048, F)), 2, specs=[SMEM, VMEM], name='place')  3.57 us
  transfers between devices with their start and end apart: 5, of which 3 were waited for; matrix products, arithmetic and copies ran while one was open for 2% of the time, Pallas kernels for 5%

profile of v2, /device:TPU:1, one launch (start us, length us, event | category | flops | bytes accessed | tf_op | source)
XLA Modules:
  0.0 120.6 jit_solution(10734395019995636434)
XLA Ops:
  0.6 0.7 convert_element_type.3
  1.3 0.1 broadcast_in_dim.7
  1.4 0.1 broadcast_in_dim.8.mask_rows
  1.5 0.0 copy-start.2
  1.5 1.2 %copy-done.2 = bf16[32,64,256]{2,1,0:T(8,128)(2,1)S(1)} copy-done((bf16[32,64,256]{2,1,0:T(8,128)(2,1)S(1)}, bf16[32,64,256]{2,1,0:T(8,128)(2,1)}, u32[]{:S(2)}) %copy-start.2) | copy-done | bytes 1048600
  2.7 0.0 copy-start.3
  2.7 1.2 %copy-done.3 = bf16[32,64,256]{2,1,0:T(8,128)(2,1)S(1)} copy-done((bf16[32,64,256]{2,1,0:T(8,128)(2,1)S(1)}, bf16[32,64,256]{2,1,0:T(8,128)(2,1)}, u32[]{:S(2)}) %copy-start.3) | copy-done | bytes 1048600
  3.9 0.0 copy-start.4
  3.9 0.9 copy-done.4
  4.9 0.6 prep.1
  5.5 4.5 %collective-permute-start = (bf16[272,256]{1,0:T(8,128)(2,1)S(1)}, bf16[272,256]{1,0:T(8,128)(2,1)S(1)}, u32[]{:S(2)}, u32[]{:S(2)}) collective-permute-start(bf16[272,256]{1,0:T(8,128)(2,1)S(1)} %get-tuple-element.24), channel_id=1, source_target_pairs={{0,16},{16,32},{32,48},{48,64},{64,80},{80,96},{96,112},{1,17},{17... | collective-permute-start | bytes 417800 | tf_op jit(solution)/shard_map/ppermute | solution.py:414
  10.0 1.9 %collective-permute-start.1 = (bf16[272,256]{1,0:T(8,128)(2,1)S(1)}, bf16[272,256]{1,0:T(8,128)(2,1)S(1)}, u32[]{:S(2)}, u32[]{:S(2)}) collective-permute-start(bf16[272,256]{1,0:T(8,128)(2,1)S(1)} %get-tuple-element.25), channel_id=1, source_target_pairs={{16,0},{32,16},{48,32},{64,48},{80,64},{96,80},{112,96},{17,1},{33... | collective-permute-start | bytes 417800 | tf_op jit(solution)/shard_map/ppermute | solution.py:414
  11.9 0.1 collective-permute-done.top
  12.0 4.4 %collective-permute-done.1.bottom = bf16[272,256]{1,0:T(8,128)(2,1)S(1)} collective-permute-done((bf16[272,256]{1,0:T(8,128)(2,1)S(1)}, bf16[272,256]{1,0:T(8,128)(2,1)S(1)}, u32[]{:S(2)}, u32[]{:S(2)}) %collective-permute-start.1) | collective-permute-done | bytes 139296 | tf_op jit(solution)/shard_map/ppermute | solution.py:414
  16.4 0.0 copy-start.5
  16.4 0.0 copy-start.6
  16.4 0.3 edge.1
  16.7 1.3 %collective-permute-start.3 = (bf16[240,256]{1,0:T(8,128)(2,1)S(1)}, bf16[240,256]{1,0:T(8,128)(2,1)S(1)}, u32[]{:S(2)}, u32[]{:S(2)}) collective-permute-start(bf16[240,256]{1,0:T(8,128)(2,1)S(1)} %get-tuple-element.26.left), channel_id=1, source_target_pairs={{1,0},{2,1},{3,2},{4,3},{5,4},{6,5},{7,6},{8,7},{9,8},{10,9},{11,1... | collective-permute-start | bytes 368648 | tf_op jit(solution)/shard_map/ppermute | solution.py:414
  18.0 4.0 %collective-permute-start.2 = (bf16[240,256]{1,0:T(8,128)(2,1)S(1)}, bf16[240,256]{1,0:T(8,128)(2,1)S(1)}, u32[]{:S(2)}, u32[]{:S(2)}) collective-permute-start(bf16[240,256]{1,0:T(8,128)(2,1)S(1)} %get-tuple-element.27.right), channel_id=1, source_target_pairs={{0,1},{1,2},{2,3},{3,4},{4,5},{5,6},{6,7},{7,8},{8,9},{9,10},{10,1... | collective-permute-start | bytes 368648 | tf_op jit(solution)/shard_map/ppermute | solution.py:414
  22.0 0.0 copy-done.5
  22.0 0.0 copy-done.6
  22.0 0.0 copy-start.7
  22.0 1.9 %expand.1 = (bf16[2304,256]{1,0:T(8,128)(2,1)S(1)}, bf16[2304,256]{1,0:T(8,128)(2,1)S(1)}, bf16[2304,256]{1,0:T(8,128)(2,1)S(1)}, bf16[2304,256]{1,0:T(8,128)(2,1)S(1)}) custom-call(bf16[288,256]{1,0:T(8,128)(2,1)S(1)} %bitcast.20, bf16[288,256]{1,0:T(8,128)(2,1)S(1)} %bitcast.21), custom_call_target="tpu_custom_call" | custom-call | flops 1073741824 | bytes 4194304 | tf_op jit(solution)/shard_map/expand/pallas_call | solution.py:432
  23.9 0.0 collective-permute-done.3.from_right
  23.9 0.0 collective-permute-done.2.from_left
  23.9 0.0 copy-done.7
  24.0 27.2 %convs.1 = (bf16[2048,256]{1,0:T(8,128)(2,1)}, bf16[512,256]{1,0:T(8,128)(2,1)}, bf16[128,40,256]{2,1,0:T(8,128)(2,1)S(1)}) custom-call(s32[8,16]{1,0:T(8,128)S(1)} %copy-done.7, bf16[2048,256]{1,0:T(8,128)(2,1)S(1)} %get-tuple-element.22.merged, bf16[2048,256]{1,0:T(8,128)(2,1)S(1)} %get-tuple-element.23.grad_two, ...), custom_call_target="tpu_custom_call" | custom-call | flops 17179869184 | bytes 4194304 | tf_op jit(solution)/shard_map/convs/pallas_call | solution.py:442
  51.2 48.0 %all_to_all.10.got = bf16[128,40,256]{2,1,0:T(8,128)(2,1)S(1)} all-to-all(bf16[128,40,256]{2,1,0:T(8,128)(2,1)S(1)} %get-tuple-element.33), channel_id=1, replica_groups=mesh['rows'=8,'cols'=16] {'rows','cols'}, dimensions={0} | all-to-all | bytes 5242880 | tf_op jit(solution)/shard_map/all_to_all | solution.py:459
  99.2 0.2 sums.1
  99.4 0.0 copy-start.1
  99.4 0.8 copy-done.1
  100.2 5.3 %all-to-all-start.1 = ((bf16[128,16,128]{2,1,0:T(8,128)(2,1)}), bf16[128,16,128]{2,1,0:T(8,128)(2,1)S(1)}, u32[]{:S(2)}, u32[]{:S(2)}) async-start(bf16[128,16,128]{2,1,0:T(8,128)(2,1)} %copy-done.1), calls=%async_computation.1 | async-start | bytes 1048576 | tf_op jit(solution)/shard_map/all_to_all | solution.py:464
  105.6 3.6 %place.1 = bf16[2048,256]{1,0:T(8,128)(2,1)S(1)} custom-call(s32[8,128]{1,0:T(8,128)S(1)} %get-tuple-element.34.slots, bf16[128,40,256]{2,1,0:T(8,128)(2,1)S(1)} %all_to_all.10.got), custom_call_target="tpu_custom_call" | custom-call | flops 1073741824 | bytes 4194304 | tf_op jit(solution)/shard_map/place/pallas_call | solution.py:465
  109.1 0.0 copy-start
  109.1 1.0 copy-done
  110.1 2.1 %reshape.48 = bf16[128,4,4,256]{3,2,1,0:T(4,128)(2,1)} reshape(bf16[2048,256]{1,0:T(8,128)(2,1)} %copy-done) | data formatting | bytes 2097152 | tf_op jit(solution)/shard_map/reshape | solution.py:473
  112.2 7.4 %all-to-all-done.1.sums = bf16[128,16,128]{2,1,0:T(8,128)(2,1)S(1)} async-done(((bf16[128,16,128]{2,1,0:T(8,128)(2,1)}), bf16[128,16,128]{2,1,0:T(8,128)(2,1)S(1)}, u32[]{:S(2)}, u32[]{:S(2)}) %all-to-all-start.1) | async-done | bytes 524320 | tf_op jit(solution)/shard_map/all_to_all | solution.py:464
  119.6 0.9 finish.1
Async XLA Ops:
  1.5 1.2 %copy-start.2 = (bf16[32,64,256]{2,1,0:T(8,128)(2,1)S(1)}, bf16[32,64,256]{2,1,0:T(8,128)(2,1)}, u32[]{:S(2)}) copy-start(bf16[32,64,256]{2,1,0:T(8,128)(2,1)} %param.8) | copy-start | bytes 3145732
  2.7 1.2 %copy-start.3 = (bf16[32,64,256]{2,1,0:T(8,128)(2,1)S(1)}, bf16[32,64,256]{2,1,0:T(8,128)(2,1)}, u32[]{:S(2)}) copy-start(bf16[32,64,256]{2,1,0:T(8,128)(2,1)} %param.13) | copy-start | bytes 3145732
  3.9 0.9 copy-start.4
  5.5 6.5 %collective-permute-start = (bf16[272,256]{1,0:T(8,128)(2,1)S(1)}, bf16[272,256]{1,0:T(8,128)(2,1)S(1)}, u32[]{:S(2)}, u32[]{:S(2)}) collective-permute-start(bf16[272,256]{1,0:T(8,128)(2,1)S(1)} %get-tuple-element.24), channel_id=1, source_target_pairs={{0,16},{16,32},{32,48},{48,64},{64,80},{80,96},{96,112},{1,17},{17... | collective-permute-start | bytes 417800 | tf_op jit(solution)/shard_map/ppermute | solution.py:414
  10.0 6.4 %collective-permute-start.1 = (bf16[272,256]{1,0:T(8,128)(2,1)S(1)}, bf16[272,256]{1,0:T(8,128)(2,1)S(1)}, u32[]{:S(2)}, u32[]{:S(2)}) collective-permute-start(bf16[272,256]{1,0:T(8,128)(2,1)S(1)} %get-tuple-element.25), channel_id=1, source_target_pairs={{16,0},{32,16},{48,32},{64,48},{80,64},{96,80},{112,96},{17,1},{33... | collective-permute-start | bytes 417800 | tf_op jit(solution)/shard_map/ppermute | solution.py:414
  16.4 5.6 %copy-start.5 = (bf16[32,3,3,256]{3,0,2,1:T(8,128)(2,1)S(1)}, bf16[32,3,3,256]{3,0,2,1:T(8,128)(2,1)}, u32[]{:S(2)}) copy-start(bf16[32,3,3,256]{3,0,2,1:T(8,128)(2,1)} %param.11) | copy-start | bytes 442372
  16.4 5.6 %copy-start.6 = (bf16[32,3,3,256]{3,0,2,1:T(8,128)(2,1)S(1)}, bf16[32,3,3,256]{3,0,2,1:T(8,128)(2,1)}, u32[]{:S(2)}) copy-start(bf16[32,3,3,256]{3,0,2,1:T(8,128)(2,1)} %param.12) | copy-start | bytes 442372
  16.7 7.3 %collective-permute-start.3 = (bf16[240,256]{1,0:T(8,128)(2,1)S(1)}, bf16[240,256]{1,0:T(8,128)(2,1)S(1)}, u32[]{:S(2)}, u32[]{:S(2)}) collective-permute-start(bf16[240,256]{1,0:T(8,128)(2,1)S(1)} %get-tuple-element.26.left), channel_id=1, source_target_pairs={{1,0},{2,1},{3,2},{4,3},{5,4},{6,5},{7,6},{8,7},{9,8},{10,9},{11,1... | collective-permute-start | bytes 368648 | tf_op jit(solution)/shard_map/ppermute | solution.py:414
  18.0 6.0 %collective-permute-start.2 = (bf16[240,256]{1,0:T(8,128)(2,1)S(1)}, bf16[240,256]{1,0:T(8,128)(2,1)S(1)}, u32[]{:S(2)}, u32[]{:S(2)}) collective-permute-start(bf16[240,256]{1,0:T(8,128)(2,1)S(1)} %get-tuple-element.27.right), channel_id=1, source_target_pairs={{0,1},{1,2},{2,3},{3,4},{4,5},{5,6},{6,7},{7,8},{8,9},{9,10},{10,1... | collective-permute-start | bytes 368648 | tf_op jit(solution)/shard_map/ppermute | solution.py:414
  22.0 2.0 %copy-start.7 = (s32[8,16]{1,0:T(8,128)S(1)}, s32[8,16]{1,0:T(8,128)}, u32[]{:S(2)}) copy-start(s32[8,16]{1,0:T(8,128)} %slots.1) | copy-start | bytes 1540
  99.4 0.8 copy-start.1
  100.2 19.4 %all-to-all-start.1 = ((bf16[128,16,128]{2,1,0:T(8,128)(2,1)}), bf16[128,16,128]{2,1,0:T(8,128)(2,1)S(1)}, u32[]{:S(2)}, u32[]{:S(2)}) async-start(bf16[128,16,128]{2,1,0:T(8,128)(2,1)} %copy-done.1), calls=%async_computation.1 | async-start | bytes 1048576 | tf_op jit(solution)/shard_map/all_to_all | solution.py:464
  109.1 1.0 copy-start

commit v3 on v2

--- a/solution.py
+++ b/solution.py
@@ -19,6 +19,7 @@
 F32 = jnp.float32
 VMEM = pl.BlockSpec(memory_space=pltpu.VMEM)
 SMEM = pl.BlockSpec(memory_space=pltpu.SMEM)
+HBM = pl.BlockSpec(memory_space=pltpu.HBM)
 
 
 def inverse_of(element):
@@ -70,12 +71,14 @@
     return lax.dot_general(lhs, rhs, (((1,), (1,)), ((), ())), preferred_element_type=F32)
 
 
-def call(kernel, out_shape, n_in, scratch=(), specs=None, flops=1 << 30, limit=40 << 20, name=None):
+def call(
+    kernel, out_shape, n_in, scratch=(), specs=None, outs=None, flops=1 << 30, limit=24 << 20, name=None
+):
     return pl.pallas_call(
         kernel,
         out_shape=out_shape,
         in_specs=specs or [VMEM] * n_in,
-        out_specs=jax.tree.map(lambda _: VMEM, out_shape),
+        out_specs=outs or jax.tree.map(lambda _: VMEM, out_shape),
         scratch_shapes=list(scratch),
         compiler_params=pltpu.CompilerParams(vmem_limit_bytes=limit),
         cost_estimate=pl.CostEstimate(flops=flops, bytes_accessed=4 << 20, transcendentals=0),
@@ -87,10 +90,42 @@
     return jax.ShapeDtypeStruct(dims, dtype)
 
 
-def prep_kernel(low, skip, grad, mask_rows, merged, grad_two, up, down):
+def far(dims):
+    return pltpu.HBM(dims, BF)
+
+
+def kept(values):
+    return pltpu.with_memory_space_constraint(values, pltpu.HBM)
+
+
+def start_copies(pairs, semaphores):
+    copies = [pltpu.make_async_copy(src, dst, semaphores.at[i]) for i, (src, dst) in enumerate(pairs)]
+    for copy in copies:
+        copy.start()
+    return copies
+
+
+def prep_kernel(
+    low_in, skip_in, grad_in, tissue, merged, grad_two, up, down, mask_rows, low, skip, grad, semaphores
+):
+    pairs = []
+    for part in range(4):
+        fine, coarse = pl.ds(part * 512, 512), pl.ds(part * 128, 128)
+        pairs.append((low_in.at[coarse], low.at[coarse]))
+        pairs.append((skip_in.at[fine], skip.at[fine]))
+        pairs.append((grad_in.at[fine], grad.at[fine]))
+    copies = start_copies(pairs, semaphores)
     spread = one_hot((iota((WIDE, 16), 0) >> 2) == iota((WIDE, 16), 1))
     twice = one_hot((iota((WIDE, 32), 0) >> 1) == iota((WIDE, 32), 1))
+    same = iota((16, 16), 0) == iota((16, 16), 1)
     for tile_row in range(8):
+        values = jnp.broadcast_to(tissue[tile_row : tile_row + 1, :].astype(F32), (16, 16))
+        column = jnp.sum(jnp.where(same, values, 0.0), axis=1, keepdims=True)
+        mask_rows[tile_row * 16 : tile_row * 16 + 16, :] = jnp.broadcast_to(column, (16, F))
+    for tile_row in range(8):
+        if tile_row % 2 == 0:
+            for copy in copies[tile_row // 2 * 3 : tile_row // 2 * 3 + 3]:
+                copy.wait()
         mask = dot(spread, mask_rows[tile_row * 16 : tile_row * 16 + 16, :].astype(BF))
         for half in range(2):
             low_row = tile_row * 2 + half
@@ -109,7 +144,22 @@
     down[2 * two : 2 * two + 16, :] = mask_rows[112:128, :].astype(BF)
 
 
-def expand_kernel(filter_one, filter_two, fwd_one, fwd_two, bwd_one, bwd_two):
+def expand_kernel(
+    slots, filter_one, filter_two, fwd_one, bwd_two, fwd_two_out, bwd_one_out, places, slot_rows,
+    fwd_two, bwd_one, semaphores,
+):
+    flat = jnp.concatenate([slots[row : row + 1, :] for row in range(8)], axis=1)
+    owner, local = flat >> 7, (flat & 127).astype(F32)
+    tile = iota((128, 128), 1)
+    match = owner == iota((128, 128), 0)
+    index = tile.astype(F32)
+    first = jnp.min(jnp.where(match, index, 1000.0), axis=1, keepdims=True)
+    second = match & (index > first)
+    used = jnp.sum(jnp.where(second, 1.0, 0.0), axis=0, keepdims=True)
+    places[...] = jnp.broadcast_to(owner * 2 + used.astype(jnp.int32), (8, 128))
+    slot_one = jnp.sum(jnp.where(match & (index == first), local + 1.0, 0.0), axis=1, keepdims=True)
+    slot_two = jnp.sum(jnp.where(second, local + 1.0, 0.0), axis=1, keepdims=True)
+    slot_rows[...] = jnp.where(tile == 0, slot_one, jnp.where(tile == 1, slot_two, 0.0)) - 1.0
     across = iota((F, F), 0)
     along = iota((F, F), 1)
     weave = one_hot(((across & 7) * 32 + (across >> 3)) == along)
@@ -125,10 +175,16 @@
             woven = dot(weave, gathered)
             bwd[(8 - pos) * F : (9 - pos) * F, :] = woven.astype(BF)
             fwd[pos * F : (pos + 1) * F, :] = woven.T.astype(BF)
-
-
-def edge_kernel(merged, grad_two, top, bottom, mask_rows, left, right, tall, masks):
+    for copy in start_copies([(fwd_two, fwd_two_out), (bwd_one, bwd_one_out)], semaphores):
+        copy.wait()
+
+
+def edge_kernel(merged, grad_two, above_in, below_in, mask_rows, left, right, top, bottom, tall, masks):
     two = 2 * WIDE
+    at_top = lax.axis_index("rows") == 0
+    at_bottom = lax.axis_index("rows") == lax.axis_size("rows") - 1
+    top[...] = jnp.where(at_top, jnp.zeros_like(above_in), above_in[...])
+    bottom[...] = jnp.where(at_bottom, jnp.zeros_like(below_in), below_in[...])
     tall[:, 36 * 16 : 48 * 16, :] = jnp.zeros((2, 12 * 16, 128), F32)
 
     def keep(row, values):
@@ -177,13 +233,21 @@
     return dot(lhs, weight[...])
 
 
-def main_kernel(
-    slots, merged, grad_two, top, bottom, left, right, from_left, from_right, mask_rows,
-    fwd_one, fwd_two, bwd_one, bwd_two,
-    output, low_grad, send,
-    merged_shift, hidden_shift, grad_shift, pre_shift, strips, edge, mask_wide, pre, grad_hidden,
-    pair, tiles, slot_rows, folded, count,
+def first_kernel(
+    merged, grad_two, top, bottom, left, right, from_left, from_right, mask_rows, fwd_one, bwd_two,
+    hidden_out, pre_out, edge, message,
+    hidden_shift, pre_shift, mask_wide, merged_shift, grad_shift, strips, pre, grad_hidden, folded, semaphores,
 ):
+    at_left = lax.axis_index("cols") == 0
+    at_right = lax.axis_index("cols") == lax.axis_size("cols") - 1
+    zero = jnp.zeros((STRIP, F), F32)
+
+    def left_strip(index):
+        return jnp.where(at_left, zero, from_left[index * STRIP : (index + 1) * STRIP, :].astype(F32))
+
+    def right_strip(index):
+        return jnp.where(at_right, zero, from_right[index * STRIP : (index + 1) * STRIP, :].astype(F32))
+
     two = 2 * WIDE
     spread = one_hot((iota((WIDE, 16), 0) >> 2) == iota((WIDE, 16), 1))
     mask_wide[0:WIDE, :] = dot(spread, top[2 * two : 2 * two + 16, :])
@@ -196,17 +260,17 @@
     for image, (source, target, weight) in enumerate(
         ((merged, merged_shift, fwd_one), (grad_two, grad_shift, bwd_two))
     ):
-        first = image * 2 * STRIP
+        first = image * 2
         columns = (
-            from_left[first : first + STRIP, :],
-            from_left[first + STRIP : first + 2 * STRIP, :],
-            left[first : first + STRIP, :],
-            right[first + STRIP : first + 2 * STRIP, :],
-            from_right[first : first + STRIP, :],
-            from_right[first + STRIP : first + 2 * STRIP, :],
+            left_strip(first),
+            left_strip(first + 1),
+            left[first * STRIP : (first + 1) * STRIP, :].astype(F32),
+            right[(first + 1) * STRIP : (first + 2) * STRIP, :].astype(F32),
+            right_strip(first),
+            right_strip(first + 1),
         )
         for index, column in enumerate(columns):
-            strips[index * STRIP : (index + 1) * STRIP, :] = column.astype(F32)
+            strips[index * STRIP : (index + 1) * STRIP, :] = column
         for row in range(2):
             at = image * two + row * WIDE
             for halo, place in ((top, row), (bottom, 34 + row)):
@@ -240,8 +304,8 @@
                     ).astype(BF)
                 )
         strip_pre.append(dot(jnp.concatenate(parts, axis=1), weight[...]))
-    strips[0:STRIP, :] = from_left[4 * STRIP : 5 * STRIP, :].astype(F32)
-    strips[STRIP : 2 * STRIP, :] = from_right[4 * STRIP : 5 * STRIP, :].astype(F32)
+    strips[0:STRIP, :] = left_strip(4)
+    strips[STRIP : 2 * STRIP, :] = right_strip(4)
     strip_mask = jnp.concatenate([strips[1:41, :], strips[STRIP + 1 : STRIP + 41, :]], axis=0)
     sigma = jax.nn.sigmoid(strip_pre[0])
     edge[0:80, :] = (strip_pre[0] * sigma * strip_mask).astype(BF).astype(F32)
@@ -275,59 +339,9 @@
         return 0
 
     lax.fori_loop(0, ROWS + 2, activate, 0)
-    order = iota((F, F), 0)
-    tile_order = one_hot(
-        iota((F, F), 1) == (((order >> 2) & 3) * WIDE + (order >> 4) * 4 + (order & 3))
-    )
-
-    def second_convs(step, _):
-        at = pl.multiple_of(step * 512, 512)
-        masks = []
-        for tile_row in range(2):
-            mask = mask_wide[pl.ds(pl.multiple_of((step * 2 + tile_row + 1) * WIDE, WIDE), WIDE), :]
-            masks.append(jnp.concatenate([mask] * 4, axis=0))
-        mask = jnp.concatenate(masks, axis=0)
-        output[pl.ds(at, 512), :] = (conv(hidden_shift, at, 512, fwd_two) * mask).astype(BF)
-        grad_merged = conv(pre_shift, at, 512, bwd_one) * mask
-        rounded = grad_merged.astype(BF)
-        for tile_row in range(2):
-            tiles[pl.ds(at + tile_row * F, F), :] = dot(
-                tile_order, rounded[tile_row * F : (tile_row + 1) * F, :]
-            ).astype(BF)
-        for row in range(4):
-            both = grad_merged[row * two : row * two + WIDE, :] + grad_merged[row * two + WIDE : row * two + two, :]
-            for half in range(2):
-                pair[half, row * WIDE : (row + 1) * WIDE, :] = both[:, half * 128 : half * 128 + 128]
-        for half in range(2):
-            low_grad[pl.ds(pl.multiple_of(step * 128, 128), 128), half * 128 : half * 128 + 128] = (
-                pair[half, pl.ds(0, 128, stride=2), :] + pair[half, pl.ds(1, 128, stride=2), :]
-            ).astype(BF)
-        return 0
-
-    lax.fori_loop(0, 4, second_convs, 0)
-
-    def clear(index, _):
-        count[index] = 0
-        return 0
-
-    lax.fori_loop(0, 128, clear, 0)
-    slot_rows[...] = jnp.full((128, 128), -1.0, F32)
-    lane = iota((1, 128), 1)
-
-    def pack(tile, _):
-        flat = slots[tile >> 4, tile & 15]
-        owner = flat >> 7
-        used = count[owner]
-        count[owner] = used + 1
-        send[owner, pl.ds(pl.multiple_of(used * 16, 16), 16), :] = tiles[
-            pl.ds(pl.multiple_of(tile * 16, 16), 16), :
-        ]
-        local = (flat & 127).astype(F32)
-        slot_rows[pl.ds(owner, 1), :] = jnp.where(lane == used, local, slot_rows[pl.ds(owner, 1), :])
-        return 0
-
-    lax.fori_loop(0, 128, pack, 0)
-
+    copies = start_copies(
+        [(hidden_shift.at[:, F : 2 * F], hidden_out), (pre_shift.at[:, F : 2 * F], pre_out)], semaphores
+    )
     across = iota((F, F), 0)
     along = iota((F, F), 1)
     unweave = one_hot(((along & 7) * 32 + (along >> 3)) == across)
@@ -357,60 +371,146 @@
     folded[576:592, :] = jnp.zeros((16, F), F32)
     for part in range(128):
         start, lanes = 9 * (part % 64), (part // 64) * 128
-        send[part, 32:40, 0:128] = folded[start : start + 8, lanes : lanes + 128].astype(BF)
-        tail = jnp.concatenate(
-            [
-                folded[start + 8 : start + 9, lanes : lanes + 128],
-                slot_rows[part : part + 1, :],
-                jnp.zeros((6, 128), F32),
-            ],
-            axis=0,
+        message[part, :, :] = folded[start : start + 16, lanes : lanes + 128].astype(BF)
+    for copy in copies:
+        copy.wait()
+
+
+def wide_mask(mask_rows, step):
+    spread = one_hot((iota((WIDE, 16), 0) >> 2) == iota((WIDE, 16), 1))
+    parts = []
+    for tile_row in range(2):
+        at = pl.multiple_of((step * 2 + tile_row) * 16, 16)
+        parts.extend([dot(spread, mask_rows[pl.ds(at, 16), :].astype(BF))] * 4)
+    return jnp.concatenate(parts, axis=0)
+
+
+def load_shifted(values, weight, edges, base, plain, held, shifted, semaphores):
+    cuts = (0, 640, 1152, 1664, 2176)
+    pairs = [(weight.at[pl.ds(part * 768, 768)], held.at[pl.ds(part * 768, 768)]) for part in range(3)]
+    for first, last in zip(cuts[:-1], cuts[1:]):
+        pairs.append((values.at[pl.ds(first, last - first)], plain.at[pl.ds(first, last - first)]))
+    copies = start_copies(pairs, semaphores)
+
+    def row_of(row, _):
+        at = pl.multiple_of(row * WIDE, WIDE)
+        value = plain[pl.ds(at, WIDE), :]
+        shifted_store(
+            shifted, at, value.astype(F32), value,
+            edges[pl.ds(base + row, 1), :], edges[pl.ds(base + 40 + row, 1), :],
         )
-        send[part, 32:40, 128:256] = tail.astype(BF)
-
-
-def sum_kernel(got, message, slots, gathered):
-    total = jnp.zeros((8, F), F32)
+        return 0
+
+    for part in range(4):
+        copies[3 + part].wait()
+        lax.fori_loop(cuts[part] // WIDE, cuts[part + 1] // WIDE, row_of, 0)
+    for copy in copies[:3]:
+        copy.wait()
+
+
+def backward_kernel(
+    pre_in, weight_in, edges, mask_rows, tiles, low_grad, pair, plain, bwd_one, pre_shift, semaphores
+):
+    two = 2 * WIDE
+    load_shifted(pre_in, weight_in, edges, 80, plain, bwd_one, pre_shift, semaphores)
+    order = iota((F, F), 0)
+    tile_order = one_hot(
+        iota((F, F), 1) == (((order >> 2) & 3) * WIDE + (order >> 4) * 4 + (order & 3))
+    )
+
+    def body(step, _):
+        at = pl.multiple_of(step * 512, 512)
+        grad_merged = conv(pre_shift, at, 512, bwd_one) * wide_mask(mask_rows, step)
+        rounded = grad_merged.astype(BF)
+        for tile_row in range(2):
+            tiles[pl.ds(at + tile_row * F, F), :] = dot(
+                tile_order, rounded[tile_row * F : (tile_row + 1) * F, :]
+            ).astype(BF)
+        for row in range(4):
+            both = grad_merged[row * two : row * two + WIDE, :] + grad_merged[row * two + WIDE : row * two + two, :]
+            for half in range(2):
+                pair[half, row * WIDE : (row + 1) * WIDE, :] = both[:, half * 128 : half * 128 + 128]
+        for half in range(2):
+            low_grad[pl.ds(pl.multiple_of(step * 128, 128), 128), half * 128 : half * 128 + 128] = (
+                pair[half, pl.ds(0, 128, stride=2), :] + pair[half, pl.ds(1, 128, stride=2), :]
+            ).astype(BF)
+        return 0
+
+    lax.fori_loop(0, 4, body, 0)
+
+
+def forward_kernel(
+    hidden_in, weight_in, edges, mask_rows, output, plain, fwd_two, hidden_shift, semaphores
+):
+    load_shifted(hidden_in, weight_in, edges, 0, plain, fwd_two, hidden_shift, semaphores)
+
+    def body(step, _):
+        at = pl.multiple_of(step * 512, 512)
+        output[pl.ds(at, 512), :] = (
+            conv(hidden_shift, at, 512, fwd_two) * wide_mask(mask_rows, step)
+        ).astype(BF)
+        return 0
+
+    lax.fori_loop(0, 4, body, 0)
+
+
+def pack_kernel(places, tiles, got, slot_rows, send):
+    def copy(group, _):
+        for sub in range(8):
+            tile = group * 8 + sub
+            place = places[0, tile]
+            send[place >> 1, pl.ds(pl.multiple_of((place & 1) * 16, 16), 16), :] = tiles[
+                pl.ds(pl.multiple_of(tile * 16, 16), 16), :
+            ]
+        return 0
+
+    lax.fori_loop(0, 16, copy, 0)
+    total = jnp.zeros((16, 128), F32)
     for part in range(128):
-        terms = got[part, 32:40, :].astype(F32)
-        total = total + terms
-        gathered[part : part + 1, :] = terms[1:2, 128:256]
-    rounded = jnp.concatenate([total[:, 0:128], total[:, 128:256]], axis=0).astype(BF)
+        total = total + got[part, :, :].astype(F32)
+    low = total[0:8, :].astype(BF)
+    high = jnp.where(iota((8, 128), 0) == 0, total[8:16, :], 0.0)
     for part in range(128):
-        message[part, :, :] = rounded
-    slots[...] = gathered[...].T[0:8, :].astype(jnp.int32)
-
-
-def place_kernel(slots, got, skip_grad):
-    def put(index, _):
-        for which in range(2):
-            slot = slots[which, index]
-
-            @pl.when(slot >= 0)
-            def _():
-                skip_grad[pl.ds(pl.multiple_of(slot * 16, 16), 16), :] = got[
-                    index, which * 16 : which * 16 + 16, :
-                ]
-
-        return 0
-
-    lax.fori_loop(0, 128, put, 0)
-
-
-def finish_kernel(scale, sums, one, two, folded):
+        send[part, 32:40, 0:128] = low
+        send[part, 32:40, 128:256] = jnp.where(
+            iota((8, 128), 0) == 1, slot_rows[part : part + 1, :], high
+        ).astype(BF)
+
+
+def place_kernel(scale, got, skip_grad, one, two, gathered, sources, folded, table, semaphore):
     for part in range(128):
+        terms = got[part, 32:40, :].astype(F32) * scale
         start, lanes = 9 * (part % 64), (part // 64) * 128
-        folded[start : start + 16, lanes : lanes + 128] = sums[part, :, :].astype(F32) * scale
+        folded[start : start + 8, lanes : lanes + 128] = terms[:, 0:128]
+        folded[start + 8 : start + 9, lanes : lanes + 128] = terms[0:1, 128:256]
+        gathered[part : part + 1, :] = terms[1:2, 128:256] / scale
     one[...] = folded[0:288, :]
     two[...] = folded[288:576, :]
+    slots = gathered[...].T
+    wanted = iota((128, 128), 0).astype(F32)
+    index = iota((128, 128), 1).astype(F32)
+    source = jnp.zeros((128, 128), F32)
+    for which in range(2):
+        source = source + jnp.where(slots[which : which + 1, :] == wanted, index * 2.0 + which, 0.0)
+    sources[...] = jnp.broadcast_to(jnp.sum(source, axis=1, keepdims=True), (128, 128)).T[0:8, :].astype(jnp.int32)
+    copy = pltpu.make_async_copy(sources, table, semaphore)
+    copy.start()
+    copy.wait()
+
+    def put(group, _):
+        for sub in range(8):
+            slot = group * 8 + sub
+            place = table[0, slot]
+            tile = got[place >> 1, pl.ds(pl.multiple_of((place & 1) * 16, 16), 16), :]
+            skip_grad[slot] = tile.reshape(4, 4, F)
+        return 0
+
+    lax.fori_loop(0, 16, put, 0)
 
 
 def shift(values, axis, step):
     size = lax.axis_size(axis)
-    if step > 0:
-        pairs = [(i, i + 1) for i in range(size - 1)]
-    else:
-        pairs = [(i + 1, i) for i in range(size - 1)]
+    pairs = [(i, (i + step) % size) for i in range(size)]
     return lax.ppermute(values, axis, pairs)
 
 
@@ -418,59 +518,82 @@
     everyone = ("rows", "cols")
     height, breadth, features = skip_feats.shape
     pixels = height * breadth
-    mask_rows = jnp.broadcast_to(tissue_mask.astype(F32).reshape(128, 1), (128, F))
-    merged, grad_two, up, down = call(
+    merged, grad_two, up, down, mask_rows = call(
         prep_kernel,
-        [shape((pixels, F)), shape((pixels, F)), shape((272, F)), shape((272, F))],
-        4, name="prep",
+        [shape((pixels, F)), shape((pixels, F)), shape((272, F)), shape((272, F)), shape((128, F), F32)],
+        4,
+        [
+            pltpu.VMEM((pixels // 4, F), BF), pltpu.VMEM((pixels, F), BF), pltpu.VMEM((pixels, F), BF),
+            pltpu.SemaphoreType.DMA((12,)),
+        ],
+        specs=[HBM, HBM, HBM, VMEM], name="prep",
     )(
-        low_feats.reshape(-1, F), skip_feats.reshape(pixels, F), out_grad.reshape(pixels, F), mask_rows
-    )
-    bottom = shift(up, "rows", -1)
-    top = shift(down, "rows", 1)
+        kept(low_feats.reshape(-1, F)), kept(skip_feats.reshape(pixels, F)),
+        kept(out_grad.reshape(pixels, F)), tissue_mask,
+    )
+    below = shift(up, "rows", -1)
+    above = shift(down, "rows", 1)
     bases = [f.transpose(1, 2, 0, 3).reshape(288, F) for f in (filter_one, filter_two)]
-    fwd_one, fwd_two, bwd_one, bwd_two = call(
-        expand_kernel, [shape((9 * F, F))] * 4, 2, name="expand"
-    )(*bases)
-    left, right = call(
+    weights = shape((9 * F, F))
+    fwd_one, bwd_two, fwd_two, bwd_one, places, slot_rows = call(
+        expand_kernel,
+        [weights] * 2 + [far((9 * F, F))] * 2 + [shape((8, 128), jnp.int32), shape((128, 128), F32)],
+        3,
+        [pltpu.VMEM((9 * F, F), BF), pltpu.VMEM((9 * F, F), BF), pltpu.SemaphoreType.DMA((2,))],
+        outs=[VMEM, VMEM, HBM, HBM, VMEM, VMEM], name="expand",
+    )(owner_slot, *bases)
+    left, right, top, bottom = call(
         edge_kernel,
-        [shape((5 * STRIP, F))] * 2,
+        [shape((5 * STRIP, F))] * 2 + [shape((272, F))] * 2,
         5, [pltpu.VMEM((2, 48 * 16, 128), F32), pltpu.VMEM((STRIP, F), F32)], name="edge",
-    )(merged, grad_two, top, bottom, mask_rows)
+    )(merged, grad_two, above, below, mask_rows)
     from_right = shift(left, "cols", -1)
     from_left = shift(right, "cols", 1)
-    output, low_grad, send = call(
-        main_kernel,
-        [shape((pixels, F)), shape((pixels // 4, F)), shape((128, 40, F))],
-        14,
+    hidden, grad_pre, edges, message = call(
+        first_kernel,
+        [far((34 * WIDE, F)), far((34 * WIDE, F)), shape((160, F), F32), shape((128, 16, 128))],
+        11,
         [
-            pltpu.VMEM((36 * WIDE, 3 * F), BF), pltpu.VMEM((34 * WIDE, 3 * F), BF),
-            pltpu.VMEM((36 * WIDE, 3 * F), BF), pltpu.VMEM((34 * WIDE, 3 * F), BF),
-            pltpu.VMEM((6 * STRIP, F), F32), pltpu.VMEM((160, F), F32), pltpu.VMEM((10 * WIDE, F), F32),
+            pltpu.VMEM((34 * WIDE, 3 * F), BF), pltpu.VMEM((34 * WIDE, 3 * F), BF),
+            pltpu.VMEM((10 * WIDE, F), F32),
+            pltpu.VMEM((36 * WIDE, 3 * F), BF), pltpu.VMEM((36 * WIDE, 3 * F), BF),
+            pltpu.VMEM((6 * STRIP, F), F32),
             pltpu.VMEM((34 * WIDE, F), F32), pltpu.VMEM((34 * WIDE, F), F32),
-            pltpu.VMEM((2, 4 * WIDE, 128), F32), pltpu.VMEM((pixels, F), BF),
-            pltpu.VMEM((128, 128), F32), pltpu.VMEM((592, F), F32), pltpu.SMEM((128,), jnp.int32),
+            pltpu.VMEM((592, F), F32), pltpu.SemaphoreType.DMA((2,)),
         ],
-        specs=[SMEM] + [VMEM] * 13, flops=16 << 30, name="convs",
-    )(
-        owner_slot, merged, grad_two, top, bottom, left, right, from_left, from_right, mask_rows,
-        fwd_one, fwd_two, bwd_one, bwd_two,
-    )
+        outs=[HBM, HBM, VMEM, VMEM], flops=10 << 30, limit=36 << 20, name="first",
+    )(merged, grad_two, top, bottom, left, right, from_left, from_right, mask_rows, fwd_one, bwd_two)
+    got_terms = lax.all_to_all(message, everyone, 0, 0, tiled=True)
+    loading = [
+        pltpu.VMEM((34 * WIDE, F), BF), pltpu.VMEM((9 * F, F), BF), pltpu.VMEM((34 * WIDE, 3 * F), BF),
+        pltpu.SemaphoreType.DMA((7,)),
+    ]
+    tiles, low_grad = call(
+        backward_kernel, [shape((pixels, F)), shape((pixels // 4, F))], 4,
+        [pltpu.VMEM((2, 4 * WIDE, 128), F32)] + loading, specs=[HBM, HBM, VMEM, VMEM],
+        flops=3 << 30, name="backward",
+    )(kept(grad_pre), kept(bwd_one), edges, mask_rows)
+    output = call(
+        forward_kernel, shape((pixels, F)), 4, loading, specs=[HBM, HBM, VMEM, VMEM],
+        flops=3 << 30, name="forward",
+    )(kept(hidden), kept(fwd_two), edges, mask_rows)
+    send = call(
+        pack_kernel, shape((128, 40, F)), 4, specs=[SMEM, VMEM, VMEM, VMEM], name="pack"
+    )(places, tiles, got_terms, slot_rows)
     got = lax.all_to_all(send, everyone, 0, 0, tiled=True)
-    sums, slots = call(
-        sum_kernel, [shape((128, 16, 128)), shape((8, 128), jnp.int32)], 1,
-        [pltpu.VMEM((128, 128), F32)], name="sums",
+    scale = 1.0 / math.sqrt(pixels * lax.axis_size("rows") * lax.axis_size("cols"))
+    skip_grad, one, two = call(
+        functools.partial(place_kernel, scale),
+        [shape((128, 4, 4, F)), shape((288, F), F32), shape((288, F), F32)], 1,
+        [
+            pltpu.VMEM((128, 128), F32), pltpu.VMEM((8, 128), jnp.int32), pltpu.VMEM((592, F), F32),
+            pltpu.SMEM((8, 128), jnp.int32), pltpu.SemaphoreType.DMA,
+        ],
+        name="place",
     )(got)
-    got_sums = lax.all_to_all(sums, everyone, 0, 0, tiled=True)
-    skip_grad = call(place_kernel, shape((2048, F)), 2, specs=[SMEM, VMEM], name="place")(slots, got)
-    scale = 1.0 / math.sqrt(pixels * lax.axis_size("rows") * lax.axis_size("cols"))
-    one, two = call(
-        functools.partial(finish_kernel, scale),
-        [shape((288, F), F32), shape((288, F), F32)], 1, [pltpu.VMEM((592, F), F32)], name="finish",
-    )(got_sums)
     return (
         output.reshape(height, breadth, F),
-        skip_grad.reshape(128, 4, 4, F),
+        skip_grad,
         low_grad.reshape(height // 2, breadth // 2, F),
         one.reshape(3, 3, 32, F).transpose(2, 0, 1, 3),
         two.reshape(3, 3, 32, F).transpose(2, 0, 1, 3),

time: 121 us -> 107 us (0.88)
  blocking collectives: 48 us -> 0 us
  waiting for transfers between devices: 11.8 us -> 44.5 us
  Pallas kernels: 34.7 us -> 43 us
  local copies, waits for them, and re-layouts: 7.48 us -> 0.69 us
    all_to_all x1 -> x0, blocking collectives: 48 us -> none  [on_device(): got = lax.all_to_all(send, everyone, 0, 0, tiled=True)]
    all_to_all x1 -> x2, waiting for transfers between devices: 7.39 us -> 35.6 us  [the longest x1 28.6 us: on_device(): got = lax.all_to_all(send, everyone, 0, 0, tiled=True)]
    pallas_call x6 -> x7, Pallas kernels: 34.2 us -> 40.9 us  [the longest x1 18.4 us: on_device(): call(first_kernel, [far((34 * WIDE, F)), far((34 * WIDE, F)), shape((160,...]
    unnamed x16 -> x8, local copies, waits for them, and re-layouts: 5.19 us -> 0.69 us
    ppermute x4, waiting for transfers between devices: 4.45 us -> 8.86 us  [shift(): return lax.ppermute(values, axis, pairs)]
    all_to_all x1 -> x2, starting transfers between devices: 5.33 us -> 8.82 us  [the longest x1 4.77 us: on_device(): got_terms = lax.all_to_all(message, everyone, 0, 0, tiled=True)]
    ppermute x4, starting transfers between devices: 11.7 us -> 8.89 us  [shift(): return lax.ppermute(values, axis, pairs)]
    reshape x1 -> x0, local copies, waits for them, and re-layouts: 2.13 us -> none  [on_device(): skip_grad.reshape(128, 4, 4, F)]
  transfers between devices with their start and end apart: 5 -> 6, of which waited for: 3 -> 5; matrix products, arithmetic and copies ran while one was open for 2% -> 0% of each run, Pallas kernels for 5% -> 16%
where the time goes in v3:
time: 107 us
  waiting for transfers between devices  44.5 us (42%)
  Pallas kernels  43 us (40%)
  starting transfers between devices  17.7 us (17%)
    all_to_all x1, waiting for transfers between devices, on_device(): got = lax.all_to_all(send, everyone, 0, 0, tiled=True)  28.6 us
    pallas_call x1, Pallas kernels, on_device(): call(first_kernel, [far((34 * WIDE, F)), far((34 * WIDE, F)), shape((160,...  18.4 us
    ppermute x4, starting transfers between devices, shift(): return lax.ppermute(values, axis, pairs)  8.89 us
    ppermute x4, waiting for transfers between devices, shift(): return lax.ppermute(values, axis, pairs)  8.86 us
    pallas_call x1, Pallas kernels, on_device(): call(backward_kernel, [shape((pixels, F)), shape((pixels // 4, F))], 4, [...  7.17 us
    all_to_all x1, waiting for transfers between devices, on_device(): got_terms = lax.all_to_all(message, everyone, 0, 0, tiled=True)  6.98 us
    pallas_call x1, Pallas kernels, on_device(): call(forward_kernel, shape((pixels, F)), 4, loading, specs=[HBM, HBM, VME...  6.13 us
    all_to_all x1, starting transfers between devices, on_device(): got_terms = lax.all_to_all(message, everyone, 0, 0, tiled=True)  4.77 us
  transfers between devices with their start and end apart: 6, of which 5 were waited for; matrix products, arithmetic and copies ran while one was open for 0% of the time, Pallas kernels for 16%

profile of v3, /device:TPU:1, one launch (start us, length us, event | category | flops | bytes accessed | tf_op | source)
XLA Modules:
  0.0 106.7 jit_solution(12354906742467831380)
XLA Ops:
  0.6 0.0 copy-start.2
  0.6 0.7 copy-done.2
  1.3 2.0 %prep.1 = (bf16[2048,256]{1,0:T(8,128)(2,1)S(1)}, bf16[2048,256]{1,0:T(8,128)(2,1)S(1)}, bf16[272,256]{1,0:T(8,128)(2,1)S(1)}, bf16[272,256]{1,0:T(8,128)(2,1)S(1)}, f32[128,256]{1,0:T(8,128)S(1)}) custom-call(bf16[512,256]{1,0:T(8,128)(2,1)} %bitcast.21, bf16[2048,256]{1,0:T(8,128)(2,1)} %bitcast.19, bf16[2048,256]{1,0:T(8,128)(2,1)} %bitcast.20, ...), custom_call_target="tpu_custom_call" | custom-call | flops 1073741824 | bytes 4194304 | tf_op jit(solution)/shard_map/prep/pallas_call | solution.py:521
  3.4 2.6 %collective-permute-start = (bf16[272,256]{1,0:T(8,128)(2,1)S(1)}, bf16[272,256]{1,0:T(8,128)(2,1)S(1)}, u32[]{:S(2)}, u32[]{:S(2)}) collective-permute-start(bf16[272,256]{1,0:T(8,128)(2,1)S(1)} %get-tuple-element.31), channel_id=1, source_target_pairs={{0,16},{16,32},{32,48},{48,64},{64,80},{80,96},{96,112},{112,0},{1... | collective-permute-start | bytes 417800 | tf_op jit(solution)/shard_map/ppermute | solution.py:514
  6.0 0.0 collective-permute-start.1
  6.0 2.0 %collective-permute-done.above_in = bf16[272,256]{1,0:T(8,128)(2,1)S(1)} collective-permute-done((bf16[272,256]{1,0:T(8,128)(2,1)S(1)}, bf16[272,256]{1,0:T(8,128)(2,1)S(1)}, u32[]{:S(2)}, u32[]{:S(2)}) %collective-permute-start) | collective-permute-done | bytes 139296 | tf_op jit(solution)/shard_map/ppermute | solution.py:514
  8.0 2.5 %collective-permute-done.1.below_in = bf16[272,256]{1,0:T(8,128)(2,1)S(1)} collective-permute-done((bf16[272,256]{1,0:T(8,128)(2,1)S(1)}, bf16[272,256]{1,0:T(8,128)(2,1)S(1)}, u32[]{:S(2)}, u32[]{:S(2)}) %collective-permute-start.1) | collective-permute-done | bytes 139296 | tf_op jit(solution)/shard_map/ppermute | solution.py:514
  10.5 0.0 copy-start
  10.5 0.0 copy-start.1
  10.5 0.0 copy-start.3
  10.5 0.3 edge.1
  10.8 6.3 %collective-permute-start.3 = (bf16[240,256]{1,0:T(8,128)(2,1)S(1)}, bf16[240,256]{1,0:T(8,128)(2,1)S(1)}, u32[]{:S(2)}, u32[]{:S(2)}) collective-permute-start(bf16[240,256]{1,0:T(8,128)(2,1)S(1)} %get-tuple-element.36.left), channel_id=1, source_target_pairs={{0,15},{1,0},{2,1},{3,2},{4,3},{5,4},{6,5},{7,6},{8,7},{9,8},{10,9... | collective-permute-start | bytes 368648 | tf_op jit(solution)/shard_map/ppermute | solution.py:514
  17.0 0.0 collective-permute-start.2
  17.1 0.0 copy-done
  17.1 0.0 copy-done.1
  17.1 0.0 copy-done.3
  17.1 3.4 %expand.1 = (bf16[2304,256]{1,0:T(8,128)(2,1)S(1)}, bf16[2304,256]{1,0:T(8,128)(2,1)S(1)}, bf16[2304,256]{1,0:T(8,128)(2,1)}, bf16[2304,256]{1,0:T(8,128)(2,1)},...) custom-call(s32[8,16]{1,0:T(8,128)S(1)} %copy-done.3, bf16[288,256]{1,0:T(8,128)(2,1)S(1)} %bitcast.17, ...), custom_call_target="tpu_custom_call" | custom-call | flops 1073741824 | bytes 4194304 | tf_op jit(solution)/shard_map/expand/pallas_call | solution.py:538
  20.4 0.0 collective-permute-done.3.from_right
  20.5 4.4 %collective-permute-done.2.from_left = bf16[240,256]{1,0:T(8,128)(2,1)S(1)} collective-permute-done((bf16[240,256]{1,0:T(8,128)(2,1)S(1)}, bf16[240,256]{1,0:T(8,128)(2,1)S(1)}, u32[]{:S(2)}, u32[]{:S(2)}) %collective-permute-start.2) | collective-permute-done | bytes 122912 | tf_op jit(solution)/shard_map/ppermute | solution.py:514
  24.8 18.4 %first.1 = (bf16[2176,256]{1,0:T(8,128)(2,1)}, bf16[2176,256]{1,0:T(8,128)(2,1)}, f32[160,256]{1,0:T(8,128)S(1)}, bf16[128,16,128]{2,1,0:T(8,128)(2,1)}) custom-call(bf16[2048,256]{1,0:T(8,128)(2,1)S(1)} %get-tuple-element.29.merged, bf16[2048,256]{1,0:T(8,128)(2,1)S(1)} %get-tuple-element.30.grad_two, bf16[272,256]{1,0:T(8,128)(2,1)S(1)} %get-tuple-element.34.top, ...), custom_call_target="tpu_custom_call" | custom-call | flops 10737418240 | bytes 4194304 | tf_op jit(solution)/shard_map/first/pallas_call | solution.py:552
  43.2 4.8 %all-to-all-start = ((bf16[128,16,128]{2,1,0:T(8,128)(2,1)}), bf16[128,16,128]{2,1,0:T(8,128)(2,1)S(1)}, u32[]{:S(2)}, u32[]{:S(2)}) async-start(bf16[128,16,128]{2,1,0:T(8,128)(2,1)} %get-tuple-element.47), calls=%async_computation | async-start | bytes 1048576 | tf_op jit(solution)/shard_map/all_to_all | solution.py:566
  48.0 7.2 %backward.1 = (bf16[2048,256]{1,0:T(8,128)(2,1)S(1)}, bf16[512,256]{1,0:T(8,128)(2,1)}) custom-call(bf16[2176,256]{1,0:T(8,128)(2,1)} %get-tuple-element.44.pre_in, bf16[2304,256]{1,0:T(8,128)(2,1)} %get-tuple-element.45.weight_in, f32[160,256]{1,0:T(8,128)S(1)} %get-tuple-element.42.edges, f32[128,256]{1,0:T(8,128)S(1)} %get-tuple-element.33.mask_rows), custom_call_target="tpu_custom_call" | custom-call | flops 3221225472 | bytes 4194304 | tf_op jit(solution)/shard_map/backward/pallas_call | solution.py:571
  55.2 7.0 %all-to-all-done.got = bf16[128,16,128]{2,1,0:T(8,128)(2,1)S(1)} async-done(((bf16[128,16,128]{2,1,0:T(8,128)(2,1)}), bf16[128,16,128]{2,1,0:T(8,128)(2,1)S(1)}, u32[]{:S(2)}, u32[]{:S(2)}) %all-to-all-start) | async-done | bytes 524320 | tf_op jit(solution)/shard_map/all_to_all | solution.py:566
  62.1 2.9 %pack.1 = bf16[128,40,256]{2,1,0:T(8,128)(2,1)} custom-call(s32[8,128]{1,0:T(8,128)S(1)} %get-tuple-element.43.places, bf16[2048,256]{1,0:T(8,128)(2,1)S(1)} %get-tuple-element.46.tiles, bf16[128,16,128]{2,1,0:T(8,128)(2,1)S(1)} %all-to-all-done.got, f32[128,128]{1,0:T(8,128)S(1)} %get-tuple-element.48.slot_rows), custom_call_target="tpu_custom_call" | custom-call | flops 1073741824 | bytes 4194304 | tf_op jit(solution)/shard_map/pack/pallas_call | solution.py:580
  65.1 4.0 %all-to-all-start.1 = ((bf16[128,40,256]{2,1,0:T(8,128)(2,1)}), bf16[128,40,256]{2,1,0:T(8,128)(2,1)S(1)}, u32[]{:S(2)}, u32[]{:S(2)}) async-start(bf16[128,40,256]{2,1,0:T(8,128)(2,1)} %pack.1), calls=%async_computation.1 | async-start | bytes 5242880 | tf_op jit(solution)/shard_map/all_to_all | solution.py:583
  69.1 6.1 %forward.1 = bf16[2048,256]{1,0:T(8,128)(2,1)} custom-call(bf16[2176,256]{1,0:T(8,128)(2,1)} %get-tuple-element.40.hidden_in, bf16[2304,256]{1,0:T(8,128)(2,1)} %get-tuple-element.41.weight_in, f32[160,256]{1,0:T(8,128)S(1)} %get-tuple-element.42.edges, f32[128,256]{1,0:T(8,128)S(1)} %get-tuple-element.33.mask_rows), custom_call_target="tpu_custom_call" | custom-call | flops 3221225472 | bytes 4194304 | tf_op jit(solution)/shard_map/forward/pallas_call | solution.py:576
  75.3 28.6 %all-to-all-done.1.got = bf16[128,40,256]{2,1,0:T(8,128)(2,1)S(1)} async-done(((bf16[128,40,256]{2,1,0:T(8,128)(2,1)}), bf16[128,40,256]{2,1,0:T(8,128)(2,1)S(1)}, u32[]{:S(2)}, u32[]{:S(2)}) %all-to-all-start.1) | async-done | bytes 2621472 | tf_op jit(solution)/shard_map/all_to_all | solution.py:583
  103.9 2.6 %place.1 = (bf16[128,4,4,256]{3,2,1,0:T(4,128)(2,1)}, f32[288,256]{1,0:T(8,128)}, f32[288,256]{1,0:T(8,128)}) custom-call(bf16[128,40,256]{2,1,0:T(8,128)(2,1)S(1)} %all-to-all-done.1.got), custom_call_target="tpu_custom_call" | custom-call | flops 1073741824 | bytes 4194304 | tf_op jit(solution)/shard_map/place/pallas_call | solution.py:585
Async XLA Ops:
  0.6 0.7 copy-start.2
  3.4 4.6 %collective-permute-start = (bf16[272,256]{1,0:T(8,128)(2,1)S(1)}, bf16[272,256]{1,0:T(8,128)(2,1)S(1)}, u32[]{:S(2)}, u32[]{:S(2)}) collective-permute-start(bf16[272,256]{1,0:T(8,128)(2,1)S(1)} %get-tuple-element.31), channel_id=1, source_target_pairs={{0,16},{16,32},{32,48},{48,64},{64,80},{80,96},{96,112},{112,0},{1... | collective-permute-start | bytes 417800 | tf_op jit(solution)/shard_map/ppermute | solution.py:514
  6.0 4.5 %collective-permute-start.1 = (bf16[272,256]{1,0:T(8,128)(2,1)S(1)}, bf16[272,256]{1,0:T(8,128)(2,1)S(1)}, u32[]{:S(2)}, u32[]{:S(2)}) collective-permute-start(bf16[272,256]{1,0:T(8,128)(2,1)S(1)} %get-tuple-element.32), channel_id=1, source_target_pairs={{0,112},{16,0},{32,16},{48,32},{64,48},{80,64},{96,80},{112,96},{1... | collective-permute-start | bytes 417800 | tf_op jit(solution)/shard_map/ppermute | solution.py:514
  10.5 6.6 %copy-start = (bf16[32,3,3,256]{3,0,2,1:T(8,128)(2,1)S(1)}, bf16[32,3,3,256]{3,0,2,1:T(8,128)(2,1)}, u32[]{:S(2)}) copy-start(bf16[32,3,3,256]{3,0,2,1:T(8,128)(2,1)} %param.11) | copy-start | bytes 442372
  10.5 6.6 %copy-start.1 = (bf16[32,3,3,256]{3,0,2,1:T(8,128)(2,1)S(1)}, bf16[32,3,3,256]{3,0,2,1:T(8,128)(2,1)}, u32[]{:S(2)}) copy-start(bf16[32,3,3,256]{3,0,2,1:T(8,128)(2,1)} %param.12) | copy-start | bytes 442372
  10.5 6.6 %copy-start.3 = (s32[8,16]{1,0:T(8,128)S(1)}, s32[8,16]{1,0:T(8,128)}, u32[]{:S(2)}) copy-start(s32[8,16]{1,0:T(8,128)} %slots.1) | copy-start | bytes 1540
  10.8 9.7 %collective-permute-start.3 = (bf16[240,256]{1,0:T(8,128)(2,1)S(1)}, bf16[240,256]{1,0:T(8,128)(2,1)S(1)}, u32[]{:S(2)}, u32[]{:S(2)}) collective-permute-start(bf16[240,256]{1,0:T(8,128)(2,1)S(1)} %get-tuple-element.36.left), channel_id=1, source_target_pairs={{0,15},{1,0},{2,1},{3,2},{4,3},{5,4},{6,5},{7,6},{8,7},{9,8},{10,9... | collective-permute-start | bytes 368648 | tf_op jit(solution)/shard_map/ppermute | solution.py:514
  17.0 7.8 %collective-permute-start.2 = (bf16[240,256]{1,0:T(8,128)(2,1)S(1)}, bf16[240,256]{1,0:T(8,128)(2,1)S(1)}, u32[]{:S(2)}, u32[]{:S(2)}) collective-permute-start(bf16[240,256]{1,0:T(8,128)(2,1)S(1)} %get-tuple-element.37.right), channel_id=1, source_target_pairs={{0,1},{1,2},{2,3},{3,4},{4,5},{5,6},{6,7},{7,8},{8,9},{9,10},{10,1... | collective-permute-start | bytes 368648 | tf_op jit(solution)/shard_map/ppermute | solution.py:514
  43.2 18.9 %all-to-all-start = ((bf16[128,16,128]{2,1,0:T(8,128)(2,1)}), bf16[128,16,128]{2,1,0:T(8,128)(2,1)S(1)}, u32[]{:S(2)}, u32[]{:S(2)}) async-start(bf16[128,16,128]{2,1,0:T(8,128)(2,1)} %get-tuple-element.47), calls=%async_computation | async-start | bytes 1048576 | tf_op jit(solution)/shard_map/all_to_all | solution.py:566
  65.1 38.8 %all-to-all-start.1 = ((bf16[128,40,256]{2,1,0:T(8,128)(2,1)}), bf16[128,40,256]{2,1,0:T(8,128)(2,1)S(1)}, u32[]{:S(2)}, u32[]{:S(2)}) async-start(bf16[128,40,256]{2,1,0:T(8,128)(2,1)} %pack.1), calls=%async_computation.1 | async-start | bytes 5242880 | tf_op jit(solution)/shard_map/all_to_all | solution.py:583

commit v4 on v3

--- a/solution.py
+++ b/solution.py
@@ -105,43 +105,73 @@
     return copies
 
 
+def fill_mask_rows(tissue, mask_rows, tile_rows):
+    same = iota((16, 16), 0) == iota((16, 16), 1)
+    for tile_row in tile_rows:
+        values = jnp.broadcast_to(tissue[tile_row : tile_row + 1, :].astype(F32), (16, 16))
+        column = jnp.sum(jnp.where(same, values, 0.0), axis=1, keepdims=True)
+        mask_rows[tile_row * 16 : tile_row * 16 + 16, :] = jnp.broadcast_to(column, (16, F))
+
+
+def masked_rows(tile_row, half, low, skip, grad, mask_rows, low_at, at, merged, grad_two, put):
+    spread = one_hot((iota((WIDE, 16), 0) >> 2) == iota((WIDE, 16), 1))
+    twice = one_hot((iota((WIDE, 32), 0) >> 1) == iota((WIDE, 32), 1))
+    mask = dot(spread, mask_rows[tile_row * 16 : tile_row * 16 + 16, :].astype(BF))
+    coarse = dot(twice, low[low_at : low_at + 32, :])
+    for sub in range(2):
+        here, there = pl.ds(at + sub * WIDE, WIDE), pl.ds(put + sub * WIDE, WIDE)
+        merged[there, :] = ((coarse + skip[here, :].astype(F32)) * mask).astype(BF)
+        grad_two[there, :] = (grad[here, :].astype(F32) * mask).astype(BF)
+
+
+def head_kernel(
+    low_in, skip_in, grad_in, tissue_in, near, far_side, low, skip, grad, tissue, mask_rows, merged, grad_two,
+    semaphores,
+):
+    two = 2 * WIDE
+    last = ROWS * WIDE - two
+    pairs = [(tissue_in, tissue)]
+    for part in range(2):
+        pairs.append((low_in.at[pl.ds(part * 480, 32)], low.at[pl.ds(part * 32, 32)]))
+        pairs.append((skip_in.at[pl.ds(part * last, two)], skip.at[pl.ds(part * two, two)]))
+        pairs.append((grad_in.at[pl.ds(part * last, two)], grad.at[pl.ds(part * two, two)]))
+    for copy in start_copies(pairs, semaphores):
+        copy.wait()
+    fill_mask_rows(tissue, mask_rows, (0, 7))
+    for part in range(2):
+        masked_rows(
+            part * 7, part, low, skip, grad, mask_rows, part * 32, part * two, merged, grad_two, part * two
+        )
+    odd = lax.axis_index("rows") % 2 == 1
+    for at, source in ((0, merged), (two, grad_two)):
+        head, tail = source[0:two, :], source[two : 2 * two, :]
+        near[at : at + two, :] = jnp.where(odd, head, tail)
+        far_side[at : at + two, :] = jnp.where(odd, tail, head)
+    head, tail = mask_rows[0:16, :].astype(BF), mask_rows[112:128, :].astype(BF)
+    near[2 * two : 2 * two + 16, :] = jnp.where(odd, head, tail)
+    far_side[2 * two : 2 * two + 16, :] = jnp.where(odd, tail, head)
+
+
 def prep_kernel(
-    low_in, skip_in, grad_in, tissue, merged, grad_two, up, down, mask_rows, low, skip, grad, semaphores
-):
-    pairs = []
+    low_in, skip_in, grad_in, tissue_in, merged, grad_two, mask_rows, low, skip, grad, tissue, semaphores
+):
+    pairs = [(tissue_in, tissue)]
     for part in range(4):
         fine, coarse = pl.ds(part * 512, 512), pl.ds(part * 128, 128)
         pairs.append((low_in.at[coarse], low.at[coarse]))
         pairs.append((skip_in.at[fine], skip.at[fine]))
         pairs.append((grad_in.at[fine], grad.at[fine]))
     copies = start_copies(pairs, semaphores)
-    spread = one_hot((iota((WIDE, 16), 0) >> 2) == iota((WIDE, 16), 1))
-    twice = one_hot((iota((WIDE, 32), 0) >> 1) == iota((WIDE, 32), 1))
-    same = iota((16, 16), 0) == iota((16, 16), 1)
-    for tile_row in range(8):
-        values = jnp.broadcast_to(tissue[tile_row : tile_row + 1, :].astype(F32), (16, 16))
-        column = jnp.sum(jnp.where(same, values, 0.0), axis=1, keepdims=True)
-        mask_rows[tile_row * 16 : tile_row * 16 + 16, :] = jnp.broadcast_to(column, (16, F))
+    copies[0].wait()
+    fill_mask_rows(tissue, mask_rows, range(8))
     for tile_row in range(8):
         if tile_row % 2 == 0:
-            for copy in copies[tile_row // 2 * 3 : tile_row // 2 * 3 + 3]:
+            for copy in copies[tile_row // 2 * 3 + 1 : tile_row // 2 * 3 + 4]:
                 copy.wait()
-        mask = dot(spread, mask_rows[tile_row * 16 : tile_row * 16 + 16, :].astype(BF))
         for half in range(2):
             low_row = tile_row * 2 + half
-            coarse = dot(twice, low[low_row * 32 : low_row * 32 + 32, :])
-            for sub in range(2):
-                here = pl.ds((low_row * 2 + sub) * WIDE, WIDE)
-                merged[here, :] = ((coarse + skip[here, :].astype(F32)) * mask).astype(BF)
-                grad_two[here, :] = (grad[here, :].astype(F32) * mask).astype(BF)
-    two = 2 * WIDE
-    up[0:two, :] = merged[0:two, :]
-    up[two : 2 * two, :] = grad_two[0:two, :]
-    up[2 * two : 2 * two + 16, :] = mask_rows[0:16, :].astype(BF)
-    last = ROWS * WIDE - two
-    down[0:two, :] = merged[last : last + two, :]
-    down[two : 2 * two, :] = grad_two[last : last + two, :]
-    down[2 * two : 2 * two + 16, :] = mask_rows[112:128, :].astype(BF)
+            at = low_row * 2 * WIDE
+            masked_rows(tile_row, half, low, skip, grad, mask_rows, low_row * 32, at, merged, grad_two, at)
 
 
 def expand_kernel(
@@ -179,12 +209,16 @@
         copy.wait()
 
 
-def edge_kernel(merged, grad_two, above_in, below_in, mask_rows, left, right, top, bottom, tall, masks):
+def edge_kernel(
+    merged, grad_two, near_in, far_in, mask_rows, left, right, top, bottom, near, far_side, tall, masks
+):
     two = 2 * WIDE
     at_top = lax.axis_index("rows") == 0
     at_bottom = lax.axis_index("rows") == lax.axis_size("rows") - 1
-    top[...] = jnp.where(at_top, jnp.zeros_like(above_in), above_in[...])
-    bottom[...] = jnp.where(at_bottom, jnp.zeros_like(below_in), below_in[...])
+    odd = lax.axis_index("rows") % 2 == 1
+    zero = jnp.zeros((272, F), BF)
+    top[...] = jnp.where(at_top, zero, jnp.where(odd, near_in[...], far_in[...]))
+    bottom[...] = jnp.where(at_bottom, zero, jnp.where(odd, far_in[...], near_in[...]))
     tall[:, 36 * 16 : 48 * 16, :] = jnp.zeros((2, 12 * 16, 128), F32)
 
     def keep(row, values):
@@ -217,6 +251,9 @@
             at = tile_row * 16 + tile_col
             masks[2 + 4 * tile_row : 6 + 4 * tile_row, :] = jnp.broadcast_to(mask_rows[at : at + 1, :], (4, F))
         target[4 * STRIP : 5 * STRIP, :] = masks[...].astype(BF)
+    odd = lax.axis_index("cols") % 2 == 1
+    near[...] = jnp.where(odd, left[...], right[...])
+    far_side[...] = jnp.where(odd, right[...], left[...])
 
 
 def shifted_store(target, at, value, plain, before, after):
@@ -233,20 +270,60 @@
     return dot(lhs, weight[...])
 
 
+def interior_kernel(
+    merged, grad_two, fwd_one, bwd_two, merged_shift, pre, grad_hidden, grad_ends, grad_shift
+):
+    nothing = jnp.zeros((1, F), F32)
+    for source, target in ((merged, merged_shift), (grad_two, grad_shift)):
+
+        def shift_row(row, _, source=source, target=target):
+            at = pl.multiple_of(row * WIDE, WIDE)
+            plain = source[pl.ds(at, WIDE), :]
+            shifted_store(target, at, plain.astype(F32), plain, nothing, nothing)
+            return 0
+
+        lax.fori_loop(0, ROWS, shift_row, 0)
+
+    def convs(step, _):
+        at = pl.multiple_of(step * 480, 16)
+        pre[pl.ds(at, 480), :] = conv(merged_shift, at, 480, fwd_one)
+        grad_hidden[pl.ds(at, 480), :] = conv(grad_shift, at, 480, bwd_two)
+        return 0
+
+    lax.fori_loop(0, 4, convs, 0)
+    grad_ends[0 : 2 * WIDE, :] = grad_shift[0 : 2 * WIDE, :]
+    grad_ends[2 * WIDE : 4 * WIDE, :] = grad_shift[30 * WIDE : 32 * WIDE, :]
+
+
+def patched_copy(source, source_at, target, target_at, before, after):
+    row = iota((16, F), 0)
+    target[pl.ds(target_at, WIDE), :] = source[pl.ds(source_at, WIDE), :]
+    first = source[pl.ds(source_at, 16), 0:F].astype(F32)
+    target[pl.ds(target_at, 16), 0:F] = jnp.where(row == 0, before, first).astype(BF)
+    last = source[pl.ds(source_at + 48, 16), 2 * F : 3 * F].astype(F32)
+    target[pl.ds(target_at + 48, 16), 2 * F : 3 * F] = jnp.where(row == 15, after, last).astype(BF)
+
+
 def first_kernel(
-    merged, grad_two, top, bottom, left, right, from_left, from_right, mask_rows, fwd_one, bwd_two,
+    merged, grad_two, top, bottom, left, right, near, far_side, mask_rows, fwd_one, bwd_two,
+    merged_inner, pre, grad_hidden, grad_ends,
     hidden_out, pre_out, edge, message,
-    hidden_shift, pre_shift, mask_wide, merged_shift, grad_shift, strips, pre, grad_hidden, folded, semaphores,
+    hidden_shift, pre_shift, mask_wide, merged_shift, grad_edges, strips, pre_edge, grad_edge, correction, folded, semaphores,
 ):
     at_left = lax.axis_index("cols") == 0
     at_right = lax.axis_index("cols") == lax.axis_size("cols") - 1
+    odd = lax.axis_index("cols") % 2 == 1
     zero = jnp.zeros((STRIP, F), F32)
 
     def left_strip(index):
-        return jnp.where(at_left, zero, from_left[index * STRIP : (index + 1) * STRIP, :].astype(F32))
+        here = slice(index * STRIP, (index + 1) * STRIP)
+        value = jnp.where(odd, near[here, :], far_side[here, :])
+        return jnp.where(at_left, zero, value.astype(F32))
 
     def right_strip(index):
-        return jnp.where(at_right, zero, from_right[index * STRIP : (index + 1) * STRIP, :].astype(F32))
+        here = slice(index * STRIP, (index + 1) * STRIP)
+        value = jnp.where(odd, far_side[here, :], near[here, :])
+        return jnp.where(at_right, zero, value.astype(F32))
 
     two = 2 * WIDE
     spread = one_hot((iota((WIDE, 16), 0) >> 2) == iota((WIDE, 16), 1))
@@ -257,9 +334,8 @@
             spread, mask_rows[tile_row * 16 : tile_row * 16 + 16, :].astype(BF)
         )
     strip_pre = []
-    for image, (source, target, weight) in enumerate(
-        ((merged, merged_shift, fwd_one), (grad_two, grad_shift, bwd_two))
-    ):
+    quad = 4 * WIDE
+    for image, (weight, result) in enumerate(((fwd_one, pre_edge), (bwd_two, grad_edge))):
         first = image * 2
         columns = (
             left_strip(first),
@@ -271,26 +347,52 @@
         )
         for index, column in enumerate(columns):
             strips[index * STRIP : (index + 1) * STRIP, :] = column
+
+        def before(row):
+            return strips[pl.ds(STRIP + row, 1), :]
+
+        def after(row):
+            return strips[pl.ds(4 * STRIP + row, 1), :]
+
         for row in range(2):
             at = image * two + row * WIDE
-            for halo, place in ((top, row), (bottom, 34 + row)):
+            for halo, place, edge_at in ((top, row, row), (bottom, 34 + row, 6 + row)):
                 plain = halo[at : at + WIDE, :]
+                target, where_to = (grad_edges, edge_at) if image else (merged_shift, place)
                 shifted_store(
-                    target, place * WIDE, plain.astype(F32), plain,
-                    strips[STRIP + place : STRIP + place + 1, :],
-                    strips[4 * STRIP + place : 4 * STRIP + place + 1, :],
+                    target, where_to * WIDE, plain.astype(F32), plain, before(place), after(place)
                 )
-
-        def shift_row(row, _, source=source, target=target):
-            plain = source[pl.ds(pl.multiple_of(row * WIDE, WIDE), WIDE), :]
-            shifted_store(
-                target, pl.multiple_of((row + 2) * WIDE, WIDE), plain.astype(F32), plain,
-                strips[pl.ds(STRIP + 2 + row, 1), :],
-                strips[pl.ds(4 * STRIP + 2 + row, 1), :],
+        if image:
+            for row in range(4):
+                place = (2, 3, 32, 33)[row]
+                patched_copy(grad_ends, row * WIDE, grad_edges, (2 + row) * WIDE, before(place), after(place))
+            ends = [grad_edges[ky * WIDE : ky * WIDE + two, :] for ky in range(3)]
+            tails = [grad_edges[quad + ky * WIDE : quad + ky * WIDE + two, :] for ky in range(3)]
+        else:
+
+            def patch(row, _):
+                patched_copy(
+                    merged_inner, pl.multiple_of(row * WIDE, WIDE), merged_shift,
+                    pl.multiple_of((row + 2) * WIDE, WIDE), before(row + 2), after(row + 2),
+                )
+                return 0
+
+            lax.fori_loop(0, ROWS, patch, 0)
+            ends = [merged_shift[ky * WIDE : ky * WIDE + two, :] for ky in range(3)]
+            tails = [merged_shift[(32 + ky) * WIDE : (32 + ky) * WIDE + two, :] for ky in range(3)]
+        lhs = jnp.concatenate([jnp.concatenate(ends, axis=1), jnp.concatenate(tails, axis=1)], axis=0)
+        result[...] = dot(lhs, weight[...])
+        row = iota((40, F), 0)
+        inner = (row >= 2) & (row < 32)
+        for side, (index, kx) in enumerate(((1, 0), (4, 2))):
+            column = jnp.concatenate(
+                [strips[index * STRIP + ky : index * STRIP + ky + 40, :] for ky in range(3)], axis=1
+            ).astype(BF)
+            taps = jnp.concatenate(
+                [weight[(ky * 3 + kx) * F : (ky * 3 + kx + 1) * F, :] for ky in range(3)], axis=0
             )
-            return 0
-
-        lax.fori_loop(0, ROWS, shift_row, 0)
+            at = (image * 2 + side) * 40
+            correction[at : at + 40, :] = jnp.where(inner, dot(column, taps), 0.0)
         parts = []
         for ky in range(3):
             for kx in range(3):
@@ -313,22 +415,22 @@
         (strip_pre[1] * (sigma * (1.0 + strip_pre[0] * (1.0 - sigma))) * strip_mask).astype(BF).astype(F32)
     )
 
-    def first_convs(step, _):
-        at = pl.multiple_of(step * 544, 16)
-        pre[pl.ds(at, 544), :] = conv(merged_shift, at, 544, fwd_one)
-        grad_hidden[pl.ds(at, 544), :] = conv(grad_shift, at, 544, bwd_two)
-        return 0
-
-    lax.fori_loop(0, 4, first_convs, 0)
-
-    def activate(row, _):
+    column = iota((WIDE, F), 0)
+
+    def activate(row, _, pre_from=None, grad_from=None, source_row=0):
         at = pl.multiple_of(row * WIDE, WIDE)
+        here = pl.ds(pl.multiple_of((row - source_row) * WIDE, WIDE), WIDE)
+
+        def corrected(value, base):
+            value = jnp.where(column == 0, value + correction[pl.ds(base + row, 1), :], value)
+            return jnp.where(column == WIDE - 1, value + correction[pl.ds(base + 40 + row, 1), :], value)
+
         mask = mask_wide[pl.ds(pl.multiple_of(((row + 3) >> 2) * WIDE, WIDE), WIDE), :]
-        value = pre[pl.ds(at, WIDE), :]
+        value = corrected(pre_from[here, :], 0)
         sigma = jax.nn.sigmoid(value)
         hidden = value * sigma * mask
         slope = sigma * (1.0 + value * (1.0 - sigma))
-        grad_value = grad_hidden[pl.ds(at, WIDE), :] * slope * mask
+        grad_value = corrected(grad_from[here, :], 80) * slope * mask
         shifted_store(
             hidden_shift, at, hidden, hidden.astype(BF), edge[pl.ds(row, 1), :], edge[pl.ds(40 + row, 1), :]
         )
@@ -338,7 +440,10 @@
         )
         return 0
 
-    lax.fori_loop(0, ROWS + 2, activate, 0)
+    ends = functools.partial(activate, pre_from=pre_edge, grad_from=grad_edge)
+    lax.fori_loop(0, 2, functools.partial(ends, source_row=0), 0)
+    lax.fori_loop(2, 32, functools.partial(activate, pre_from=pre, grad_from=grad_hidden, source_row=2), 0)
+    lax.fori_loop(32, 34, functools.partial(ends, source_row=30), 0)
     copies = start_copies(
         [(hidden_shift.at[:, F : 2 * F], hidden_out), (pre_shift.at[:, F : 2 * F], pre_out)], semaphores
     )
@@ -508,31 +613,43 @@
     lax.fori_loop(0, 16, put, 0)
 
 
-def shift(values, axis, step):
+def swap(values, axis, first):
     size = lax.axis_size(axis)
-    pairs = [(i, (i + step) % size) for i in range(size)]
-    return lax.ppermute(values, axis, pairs)
+    partner = list(range(size))
+    for index in range(first, size - 1, 2):
+        partner[index], partner[index + 1] = index + 1, index
+    return lax.ppermute(values, axis, list(enumerate(partner)))
 
 
 def on_device(low_feats, skip_feats, tissue_mask, owner_slot, filter_one, filter_two, out_grad):
     everyone = ("rows", "cols")
     height, breadth, features = skip_feats.shape
     pixels = height * breadth
-    merged, grad_two, up, down, mask_rows = call(
+    given = (
+        kept(low_feats.reshape(-1, F)), kept(skip_feats.reshape(pixels, F)),
+        kept(out_grad.reshape(pixels, F)), kept(tissue_mask),
+    )
+    near, far_side = call(
+        head_kernel, [shape((272, F))] * 2, 4,
+        [
+            pltpu.VMEM((64, F), BF), pltpu.VMEM((4 * WIDE, F), BF), pltpu.VMEM((4 * WIDE, F), BF),
+            pltpu.VMEM((8, 16), jnp.int32), pltpu.VMEM((128, F), F32), pltpu.VMEM((4 * WIDE, F), BF),
+            pltpu.VMEM((4 * WIDE, F), BF), pltpu.SemaphoreType.DMA((7,)),
+        ],
+        specs=[HBM] * 4, name="head",
+    )(*given)
+    merged, grad_two, mask_rows = call(
         prep_kernel,
-        [shape((pixels, F)), shape((pixels, F)), shape((272, F)), shape((272, F)), shape((128, F), F32)],
+        [shape((pixels, F)), shape((pixels, F)), shape((128, F), F32)],
         4,
         [
             pltpu.VMEM((pixels // 4, F), BF), pltpu.VMEM((pixels, F), BF), pltpu.VMEM((pixels, F), BF),
-            pltpu.SemaphoreType.DMA((12,)),
+            pltpu.VMEM((8, 16), jnp.int32), pltpu.SemaphoreType.DMA((13,)),
         ],
-        specs=[HBM, HBM, HBM, VMEM], name="prep",
-    )(
-        kept(low_feats.reshape(-1, F)), kept(skip_feats.reshape(pixels, F)),
-        kept(out_grad.reshape(pixels, F)), tissue_mask,
-    )
-    below = shift(up, "rows", -1)
-    above = shift(down, "rows", 1)
+        specs=[HBM] * 4, name="prep",
+    )(*given)
+    near_rows = swap(near, "rows", 0)
+    far_rows = swap(far_side, "rows", 1)
     bases = [f.transpose(1, 2, 0, 3).reshape(288, F) for f in (filter_one, filter_two)]
     weights = shape((9 * F, F))
     fwd_one, bwd_two, fwd_two, bwd_one, places, slot_rows = call(
@@ -542,27 +659,35 @@
         [pltpu.VMEM((9 * F, F), BF), pltpu.VMEM((9 * F, F), BF), pltpu.SemaphoreType.DMA((2,))],
         outs=[VMEM, VMEM, HBM, HBM, VMEM, VMEM], name="expand",
     )(owner_slot, *bases)
-    left, right, top, bottom = call(
+    left, right, top, bottom, near, far_side = call(
         edge_kernel,
-        [shape((5 * STRIP, F))] * 2 + [shape((272, F))] * 2,
+        [shape((5 * STRIP, F))] * 2 + [shape((272, F))] * 2 + [shape((5 * STRIP, F))] * 2,
         5, [pltpu.VMEM((2, 48 * 16, 128), F32), pltpu.VMEM((STRIP, F), F32)], name="edge",
-    )(merged, grad_two, above, below, mask_rows)
-    from_right = shift(left, "cols", -1)
-    from_left = shift(right, "cols", 1)
+    )(merged, grad_two, near_rows, far_rows, mask_rows)
+    near_cols = swap(near, "cols", 0)
+    far_cols = swap(far_side, "cols", 1)
+    inner = call(
+        interior_kernel,
+        [
+            shape((pixels, 3 * F)), shape((30 * WIDE, F), F32), shape((30 * WIDE, F), F32),
+            shape((4 * WIDE, 3 * F)),
+        ],
+        4, [pltpu.VMEM((pixels, 3 * F), BF)], flops=5 << 30, limit=16 << 20, name="interior",
+    )(merged, grad_two, fwd_one, bwd_two)
     hidden, grad_pre, edges, message = call(
         first_kernel,
         [far((34 * WIDE, F)), far((34 * WIDE, F)), shape((160, F), F32), shape((128, 16, 128))],
-        11,
+        15,
         [
             pltpu.VMEM((34 * WIDE, 3 * F), BF), pltpu.VMEM((34 * WIDE, 3 * F), BF),
             pltpu.VMEM((10 * WIDE, F), F32),
-            pltpu.VMEM((36 * WIDE, 3 * F), BF), pltpu.VMEM((36 * WIDE, 3 * F), BF),
+            pltpu.VMEM((36 * WIDE, 3 * F), BF), pltpu.VMEM((8 * WIDE, 3 * F), BF),
             pltpu.VMEM((6 * STRIP, F), F32),
-            pltpu.VMEM((34 * WIDE, F), F32), pltpu.VMEM((34 * WIDE, F), F32),
+            pltpu.VMEM((4 * WIDE, F), F32), pltpu.VMEM((4 * WIDE, F), F32), pltpu.VMEM((160, F), F32),
             pltpu.VMEM((592, F), F32), pltpu.SemaphoreType.DMA((2,)),
         ],
         outs=[HBM, HBM, VMEM, VMEM], flops=10 << 30, limit=36 << 20, name="first",
-    )(merged, grad_two, top, bottom, left, right, from_left, from_right, mask_rows, fwd_one, bwd_two)
+    )(merged, grad_two, top, bottom, left, right, near_cols, far_cols, mask_rows, fwd_one, bwd_two, *inner)
     got_terms = lax.all_to_all(message, everyone, 0, 0, tiled=True)
     loading = [
         pltpu.VMEM((34 * WIDE, F), BF), pltpu.VMEM((9 * F, F), BF), pltpu.VMEM((34 * WIDE, 3 * F), BF),

time: 107 us -> 105 us (0.981)
  waiting for transfers between devices: 44.5 us -> 35.5 us
  starting transfers between devices: 17.7 us -> 22.9 us
  Pallas kernels: 43 us -> 44.9 us
    ppermute x4, waiting for transfers between devices: 8.86 us -> 0.01 us  [swap(): return lax.ppermute(values, axis, list(enumerate(partner)))]
    pallas_call x2 -> x4, Pallas kernels: 2.34 us -> 10.1 us  [the longest x1 6.38 us: on_device(): call(interior_kernel, [shape((pixels, 3 * F)), shape((30 * WIDE, F), F32)...]
    all_to_all x1, starting transfers between devices: 4.77 us -> 12 us  [on_device(): got_terms = lax.all_to_all(message, everyone, 0, 0, tiled=True)]
    pallas_call x1, Pallas kernels: 18.4 us -> 12.5 us  [on_device(): call(first_kernel, [far((34 * WIDE, F)), far((34 * WIDE, F)), shape((160,...]
    ppermute x4, starting transfers between devices: 8.89 us -> 6.81 us  [swap(): return lax.ppermute(values, axis, list(enumerate(partner)))]
  transfers between devices with their start and end apart: 6 -> 6, of which waited for: 5 -> 2; matrix products, arithmetic and copies ran while one was open for 0% -> 0% of each run, Pallas kernels for 16% -> 24%
where the time goes in v4:
time: 105 us; the launch traced here: 104 us
  Pallas kernels  44.9 us (43%)
  waiting for transfers between devices  35.5 us (34%)
  starting transfers between devices  22.9 us (22%)
    all_to_all x1, waiting for transfers between devices, on_device(): got = lax.all_to_all(send, everyone, 0, 0, tiled=True)  28.6 us
    pallas_call x1, Pallas kernels, on_device(): call(first_kernel, [far((34 * WIDE, F)), far((34 * WIDE, F)), shape((160,...  12.5 us
    all_to_all x1, starting transfers between devices, on_device(): got_terms = lax.all_to_all(message, everyone, 0, 0, tiled=True)  12 us
    pallas_call x1, Pallas kernels, on_device(): call(backward_kernel, [shape((pixels, F)), shape((pixels // 4, F))], 4, [...  7.16 us
    all_to_all x1, waiting for transfers between devices, on_device(): got_terms = lax.all_to_all(message, everyone, 0, 0, tiled=True)  6.91 us
    ppermute x4, starting transfers between devices, swap(): return lax.ppermute(values, axis, list(enumerate(partner)))  6.81 us
    pallas_call x1, Pallas kernels, on_device(): call(interior_kernel, [shape((pixels, 3 * F)), shape((30 * WIDE, F), F32)...  6.38 us
    pallas_call x1, Pallas kernels, on_device(): call(forward_kernel, shape((pixels, F)), 4, loading, specs=[HBM, HBM, VME...  6.13 us
  transfers between devices with their start and end apart: 6, of which 2 were waited for; matrix products, arithmetic and copies ran while one was open for 0% of the time, Pallas kernels for 24%

profile of v4, /device:TPU:1, one launch (start us, length us, event | category | flops | bytes accessed | tf_op | source)
XLA Modules:
  0.0 104.2 jit_solution(5098052225068315848)
XLA Ops:
  0.6 1.3 %head.1 = (bf16[272,256]{1,0:T(8,128)(2,1)S(1)}, bf16[272,256]{1,0:T(8,128)(2,1)S(1)}) custom-call(bf16[512,256]{1,0:T(8,128)(2,1)} %bitcast.23, bf16[2048,256]{1,0:T(8,128)(2,1)} %bitcast.19, bf16[2048,256]{1,0:T(8,128)(2,1)} %bitcast.21, s32[8,16]{1,0:T(8,128)} %tissue_in.3), custom_call_target="tpu_custom_call" | custom-call | flops 1073741824 | bytes 4194304 | tf_op jit(solution)/shard_map/head/pallas_call | solution.py:632
  1.9 1.5 %collective-permute-start = (bf16[272,256]{1,0:T(8,128)(2,1)S(1)}, bf16[272,256]{1,0:T(8,128)(2,1)S(1)}, u32[]{:S(2)}, u32[]{:S(2)}) collective-permute-start(bf16[272,256]{1,0:T(8,128)(2,1)S(1)} %get-tuple-element.37), channel_id=1, source_target_pairs={{0,16},{16,0},{32,48},{48,32},{64,80},{80,64},{96,112},{112,96},{1... | collective-permute-start | bytes 417800 | tf_op jit(solution)/shard_map/ppermute | solution.py:621
  3.4 0.0 copy-start
  3.4 0.0 copy-start.1
  3.4 0.0 copy-start.2
  3.4 3.3 %collective-permute-start.1 = (bf16[272,256]{1,0:T(8,128)(2,1)S(1)}, bf16[272,256]{1,0:T(8,128)(2,1)S(1)}, u32[]{:S(2)}, u32[]{:S(2)}) collective-permute-start(bf16[272,256]{1,0:T(8,128)(2,1)S(1)} %get-tuple-element.38), channel_id=1, source_target_pairs={{0,0},{16,32},{32,16},{48,64},{64,48},{80,96},{96,80},{112,112},{1... | collective-permute-start | bytes 417800 | tf_op jit(solution)/shard_map/ppermute | solution.py:621
  6.7 2.1 %prep.1 = (bf16[2048,256]{1,0:T(8,128)(2,1)S(1)}, bf16[2048,256]{1,0:T(8,128)(2,1)S(1)}, f32[128,256]{1,0:T(8,128)S(1)}) custom-call(bf16[512,256]{1,0:T(8,128)(2,1)} %bitcast.24, bf16[2048,256]{1,0:T(8,128)(2,1)} %bitcast.20, bf16[2048,256]{1,0:T(8,128)(2,1)} %bitcast.22, s32[8,16]{1,0:T(8,128)} %tissue_in.3), custom_call_target="tpu_custom_call" | custom-call | flops 1073741824 | bytes 4194304 | tf_op jit(solution)/shard_map/prep/pallas_call | solution.py:641
  8.8 0.0 copy-done
  8.8 0.0 copy-done.1
  8.8 0.0 copy-done.2
  8.8 3.4 %expand.1 = (bf16[2304,256]{1,0:T(8,128)(2,1)S(1)}, bf16[2304,256]{1,0:T(8,128)(2,1)S(1)}, bf16[2304,256]{1,0:T(8,128)(2,1)}, bf16[2304,256]{1,0:T(8,128)(2,1)},...) custom-call(s32[8,16]{1,0:T(8,128)S(1)} %copy-done.2, bf16[288,256]{1,0:T(8,128)(2,1)S(1)} %bitcast.17, ...), custom_call_target="tpu_custom_call" | custom-call | flops 1073741824 | bytes 4194304 | tf_op jit(solution)/shard_map/expand/pallas_call | solution.py:655
  12.2 0.0 collective-permute-done.near_in
  12.2 0.0 collective-permute-done.1.far_in
  12.2 0.3 edge.1
  12.6 1.4 %collective-permute-start.2 = (bf16[240,256]{1,0:T(8,128)(2,1)S(1)}, bf16[240,256]{1,0:T(8,128)(2,1)S(1)}, u32[]{:S(2)}, u32[]{:S(2)}) collective-permute-start(bf16[240,256]{1,0:T(8,128)(2,1)S(1)} %get-tuple-element.44), channel_id=1, source_target_pairs={{0,1},{1,0},{2,3},{3,2},{4,5},{5,4},{6,7},{7,6},{8,9},{9,8},{10,11... | collective-permute-start | bytes 368648 | tf_op jit(solution)/shard_map/ppermute | solution.py:621
  13.9 0.7 collective-permute-start.3
  14.6 6.4 %interior.1 = (bf16[2048,768]{1,0:T(8,128)(2,1)S(1)}, f32[1920,256]{1,0:T(8,128)S(1)}, f32[1920,256]{1,0:T(8,128)S(1)}, bf16[256,768]{1,0:T(8,128)(2,1)S(1)}) custom-call(bf16[2048,256]{1,0:T(8,128)(2,1)S(1)} %get-tuple-element.35.merged, bf16[2048,256]{1,0:T(8,128)(2,1)S(1)} %get-tuple-element.36.grad_two, bf16[2304,256]{1,0:T(8,128)(2,1)S(1)} %get-tuple-element.46.fwd_one, ...), custom_call_target="tpu_custom_call" | custom-call | flops 5368709120 | bytes 4194304 | tf_op jit(solution)/shard_map/interior/pallas_call | solution.py:669
  21.0 0.0 collective-permute-done.2.near
  21.0 0.0 collective-permute-done.3.far_side
  21.0 12.5 %first.1 = (bf16[2176,256]{1,0:T(8,128)(2,1)}, bf16[2176,256]{1,0:T(8,128)(2,1)}, f32[160,256]{1,0:T(8,128)S(1)}, bf16[128,16,128]{2,1,0:T(8,128)(2,1)}) custom-call(bf16[2048,256]{1,0:T(8,128)(2,1)S(1)} %get-tuple-element.35.merged, bf16[2048,256]{1,0:T(8,128)(2,1)S(1)} %get-tuple-element.36.grad_two, bf16[272,256]{1,0:T(8,128)(2,1)S(1)} %get-tuple-element.40.top, ...), custom_call_target="tpu_custom_call" | custom-call | flops 10737418240 | bytes 4194304 | tf_op jit(solution)/shard_map/first/pallas_call | solution.py:677
  33.6 12.0 %all-to-all-start = ((bf16[128,16,128]{2,1,0:T(8,128)(2,1)}), bf16[128,16,128]{2,1,0:T(8,128)(2,1)S(1)}, u32[]{:S(2)}, u32[]{:S(2)}) async-start(bf16[128,16,128]{2,1,0:T(8,128)(2,1)} %get-tuple-element.59), calls=%async_computation | async-start | bytes 1048576 | tf_op jit(solution)/shard_map/all_to_all | solution.py:691
  45.6 7.2 %backward.1 = (bf16[2048,256]{1,0:T(8,128)(2,1)S(1)}, bf16[512,256]{1,0:T(8,128)(2,1)}) custom-call(bf16[2176,256]{1,0:T(8,128)(2,1)} %get-tuple-element.56.pre_in, bf16[2304,256]{1,0:T(8,128)(2,1)} %get-tuple-element.57.weight_in, f32[160,256]{1,0:T(8,128)S(1)} %get-tuple-element.54.edges, f32[128,256]{1,0:T(8,128)S(1)} %get-tuple-element.39.mask_rows), custom_call_target="tpu_custom_call" | custom-call | flops 3221225472 | bytes 4194304 | tf_op jit(solution)/shard_map/backward/pallas_call | solution.py:696
  52.7 6.9 %all-to-all-done.got = bf16[128,16,128]{2,1,0:T(8,128)(2,1)S(1)} async-done(((bf16[128,16,128]{2,1,0:T(8,128)(2,1)}), bf16[128,16,128]{2,1,0:T(8,128)(2,1)S(1)}, u32[]{:S(2)}, u32[]{:S(2)}) %all-to-all-start) | async-done | bytes 524320 | tf_op jit(solution)/shard_map/all_to_all | solution.py:691
  59.7 2.9 %pack.1 = bf16[128,40,256]{2,1,0:T(8,128)(2,1)} custom-call(s32[8,128]{1,0:T(8,128)S(1)} %get-tuple-element.55.places, bf16[2048,256]{1,0:T(8,128)(2,1)S(1)} %get-tuple-element.58.tiles, bf16[128,16,128]{2,1,0:T(8,128)(2,1)S(1)} %all-to-all-done.got, f32[128,128]{1,0:T(8,128)S(1)} %get-tuple-element.60.slot_rows), custom_call_target="tpu_custom_call" | custom-call | flops 1073741824 | bytes 4194304 | tf_op jit(solution)/shard_map/pack/pallas_call | solution.py:705
  62.6 4.0 %all-to-all-start.1 = ((bf16[128,40,256]{2,1,0:T(8,128)(2,1)}), bf16[128,40,256]{2,1,0:T(8,128)(2,1)S(1)}, u32[]{:S(2)}, u32[]{:S(2)}) async-start(bf16[128,40,256]{2,1,0:T(8,128)(2,1)} %pack.1), calls=%async_computation.1 | async-start | bytes 5242880 | tf_op jit(solution)/shard_map/all_to_all | solution.py:708
  66.7 6.1 %forward.1 = bf16[2048,256]{1,0:T(8,128)(2,1)} custom-call(bf16[2176,256]{1,0:T(8,128)(2,1)} %get-tuple-element.52.hidden_in, bf16[2304,256]{1,0:T(8,128)(2,1)} %get-tuple-element.53.weight_in, f32[160,256]{1,0:T(8,128)S(1)} %get-tuple-element.54.edges, f32[128,256]{1,0:T(8,128)S(1)} %get-tuple-element.39.mask_rows), custom_call_target="tpu_custom_call" | custom-call | flops 3221225472 | bytes 4194304 | tf_op jit(solution)/shard_map/forward/pallas_call | solution.py:701
  72.8 28.6 %all-to-all-done.1.got = bf16[128,40,256]{2,1,0:T(8,128)(2,1)S(1)} async-done(((bf16[128,40,256]{2,1,0:T(8,128)(2,1)}), bf16[128,40,256]{2,1,0:T(8,128)(2,1)S(1)}, u32[]{:S(2)}, u32[]{:S(2)}) %all-to-all-start.1) | async-done | bytes 2621472 | tf_op jit(solution)/shard_map/all_to_all | solution.py:708
  101.4 2.6 %place.1 = (bf16[128,4,4,256]{3,2,1,0:T(4,128)(2,1)}, f32[288,256]{1,0:T(8,128)}, f32[288,256]{1,0:T(8,128)}) custom-call(bf16[128,40,256]{2,1,0:T(8,128)(2,1)S(1)} %all-to-all-done.1.got), custom_call_target="tpu_custom_call" | custom-call | flops 1073741824 | bytes 4194304 | tf_op jit(solution)/shard_map/place/pallas_call | solution.py:710
Async XLA Ops:
  1.9 10.3 %collective-permute-start = (bf16[272,256]{1,0:T(8,128)(2,1)S(1)}, bf16[272,256]{1,0:T(8,128)(2,1)S(1)}, u32[]{:S(2)}, u32[]{:S(2)}) collective-permute-start(bf16[272,256]{1,0:T(8,128)(2,1)S(1)} %get-tuple-element.37), channel_id=1, source_target_pairs={{0,16},{16,0},{32,48},{48,32},{64,80},{80,64},{96,112},{112,96},{1... | collective-permute-start | bytes 417800 | tf_op jit(solution)/shard_map/ppermute | solution.py:621
  3.4 5.3 %copy-start = (bf16[32,3,3,256]{3,0,2,1:T(8,128)(2,1)S(1)}, bf16[32,3,3,256]{3,0,2,1:T(8,128)(2,1)}, u32[]{:S(2)}) copy-start(bf16[32,3,3,256]{3,0,2,1:T(8,128)(2,1)} %param.11) | copy-start | bytes 442372
  3.4 5.4 %copy-start.1 = (bf16[32,3,3,256]{3,0,2,1:T(8,128)(2,1)S(1)}, bf16[32,3,3,256]{3,0,2,1:T(8,128)(2,1)}, u32[]{:S(2)}) copy-start(bf16[32,3,3,256]{3,0,2,1:T(8,128)(2,1)} %param.12) | copy-start | bytes 442372
  3.4 5.4 %copy-start.2 = (s32[8,16]{1,0:T(8,128)S(1)}, s32[8,16]{1,0:T(8,128)}, u32[]{:S(2)}) copy-start(s32[8,16]{1,0:T(8,128)} %slots.1) | copy-start | bytes 1540
  3.4 8.8 %collective-permute-start.1 = (bf16[272,256]{1,0:T(8,128)(2,1)S(1)}, bf16[272,256]{1,0:T(8,128)(2,1)S(1)}, u32[]{:S(2)}, u32[]{:S(2)}) collective-permute-start(bf16[272,256]{1,0:T(8,128)(2,1)S(1)} %get-tuple-element.38), channel_id=1, source_target_pairs={{0,0},{16,32},{32,16},{48,64},{64,48},{80,96},{96,80},{112,112},{1... | collective-permute-start | bytes 417800 | tf_op jit(solution)/shard_map/ppermute | solution.py:621
  12.6 8.4 %collective-permute-start.2 = (bf16[240,256]{1,0:T(8,128)(2,1)S(1)}, bf16[240,256]{1,0:T(8,128)(2,1)S(1)}, u32[]{:S(2)}, u32[]{:S(2)}) collective-permute-start(bf16[240,256]{1,0:T(8,128)(2,1)S(1)} %get-tuple-element.44), channel_id=1, source_target_pairs={{0,1},{1,0},{2,3},{3,2},{4,5},{5,4},{6,7},{7,6},{8,9},{9,8},{10,11... | collective-permute-start | bytes 368648 | tf_op jit(solution)/shard_map/ppermute | solution.py:621
  13.9 7.1 %collective-permute-start.3 = (bf16[240,256]{1,0:T(8,128)(2,1)S(1)}, bf16[240,256]{1,0:T(8,128)(2,1)S(1)}, u32[]{:S(2)}, u32[]{:S(2)}) collective-permute-start(bf16[240,256]{1,0:T(8,128)(2,1)S(1)} %get-tuple-element.45), channel_id=1, source_target_pairs={{0,0},{1,2},{2,1},{3,4},{4,3},{5,6},{6,5},{7,8},{8,7},{9,10},{10,9... | collective-permute-start | bytes 368648 | tf_op jit(solution)/shard_map/ppermute | solution.py:621
  33.6 26.1 %all-to-all-start = ((bf16[128,16,128]{2,1,0:T(8,128)(2,1)}), bf16[128,16,128]{2,1,0:T(8,128)(2,1)S(1)}, u32[]{:S(2)}, u32[]{:S(2)}) async-start(bf16[128,16,128]{2,1,0:T(8,128)(2,1)} %get-tuple-element.59), calls=%async_computation | async-start | bytes 1048576 | tf_op jit(solution)/shard_map/all_to_all | solution.py:691
  62.6 38.8 %all-to-all-start.1 = ((bf16[128,40,256]{2,1,0:T(8,128)(2,1)}), bf16[128,40,256]{2,1,0:T(8,128)(2,1)S(1)}, u32[]{:S(2)}, u32[]{:S(2)}) async-start(bf16[128,40,256]{2,1,0:T(8,128)(2,1)} %pack.1), calls=%async_computation.1 | async-start | bytes 5242880 | tf_op jit(solution)/shard_map/all_to_all | solution.py:708

commit v5 on v4

--- a/solution.py
+++ b/solution.py
@@ -152,8 +152,27 @@
     far_side[2 * two : 2 * two + 16, :] = jnp.where(odd, tail, head)
 
 
-def prep_kernel(
-    low_in, skip_in, grad_in, tissue_in, merged, grad_two, mask_rows, low, skip, grad, tissue, semaphores
+def build_weight(base, weight, forward):
+    across = iota((F, F), 0)
+    along = iota((F, F), 1)
+    weave = one_hot(((across & 7) * 32 + (across >> 3)) == along)
+    turned = [dot(base[...], one_hot(across == permuted_index(along, elem))).astype(BF) for elem in range(G)]
+    for pos in range(9):
+        rows = []
+        for elem in range(G):
+            cell = source_cell(elem, pos)
+            rows.append(turned[elem][cell * 32 : cell * 32 + 32, :])
+        woven = dot(weave, jnp.concatenate(rows, axis=0))
+        if forward:
+            weight[pos * F : (pos + 1) * F, :] = woven.T.astype(BF)
+        else:
+            weight[(8 - pos) * F : (9 - pos) * F, :] = woven.astype(BF)
+
+
+def prepare_kernel(
+    low_in, skip_in, grad_in, tissue_in, slots, filter_one, filter_two,
+    merged, grad_two, mask_rows, fwd_one, bwd_two, places, slot_rows,
+    low, skip, grad, tissue, semaphores,
 ):
     pairs = [(tissue_in, tissue)]
     for part in range(4):
@@ -162,22 +181,6 @@
         pairs.append((skip_in.at[fine], skip.at[fine]))
         pairs.append((grad_in.at[fine], grad.at[fine]))
     copies = start_copies(pairs, semaphores)
-    copies[0].wait()
-    fill_mask_rows(tissue, mask_rows, range(8))
-    for tile_row in range(8):
-        if tile_row % 2 == 0:
-            for copy in copies[tile_row // 2 * 3 + 1 : tile_row // 2 * 3 + 4]:
-                copy.wait()
-        for half in range(2):
-            low_row = tile_row * 2 + half
-            at = low_row * 2 * WIDE
-            masked_rows(tile_row, half, low, skip, grad, mask_rows, low_row * 32, at, merged, grad_two, at)
-
-
-def expand_kernel(
-    slots, filter_one, filter_two, fwd_one, bwd_two, fwd_two_out, bwd_one_out, places, slot_rows,
-    fwd_two, bwd_one, semaphores,
-):
     flat = jnp.concatenate([slots[row : row + 1, :] for row in range(8)], axis=1)
     owner, local = flat >> 7, (flat & 127).astype(F32)
     tile = iota((128, 128), 1)
@@ -190,23 +193,17 @@
     slot_one = jnp.sum(jnp.where(match & (index == first), local + 1.0, 0.0), axis=1, keepdims=True)
     slot_two = jnp.sum(jnp.where(second, local + 1.0, 0.0), axis=1, keepdims=True)
     slot_rows[...] = jnp.where(tile == 0, slot_one, jnp.where(tile == 1, slot_two, 0.0)) - 1.0
-    across = iota((F, F), 0)
-    along = iota((F, F), 1)
-    weave = one_hot(((across & 7) * 32 + (across >> 3)) == along)
-    perms = [one_hot(across == permuted_index(along, elem)) for elem in range(G)]
-    for base, fwd, bwd in ((filter_one, fwd_one, bwd_one), (filter_two, fwd_two, bwd_two)):
-        turned = [dot(base[...], perms[elem]).astype(BF) for elem in range(G)]
-        for pos in range(9):
-            rows = []
-            for elem in range(G):
-                cell = source_cell(elem, pos)
-                rows.append(turned[elem][cell * 32 : cell * 32 + 32, :])
-            gathered = jnp.concatenate(rows, axis=0)
-            woven = dot(weave, gathered)
-            bwd[(8 - pos) * F : (9 - pos) * F, :] = woven.astype(BF)
-            fwd[pos * F : (pos + 1) * F, :] = woven.T.astype(BF)
-    for copy in start_copies([(fwd_two, fwd_two_out), (bwd_one, bwd_one_out)], semaphores):
+    build_weight(filter_one, fwd_one, True)
+    build_weight(filter_two, bwd_two, False)
+    copies[0].wait()
+    fill_mask_rows(tissue, mask_rows, range(8))
+    for copy in copies[1:]:
         copy.wait()
+    for low_row in range(16):
+        at = low_row * 2 * WIDE
+        masked_rows(
+            low_row // 2, low_row % 2, low, skip, grad, mask_rows, low_row * 32, at, merged, grad_two, at
+        )
 
 
 def edge_kernel(
@@ -284,13 +281,8 @@
 
         lax.fori_loop(0, ROWS, shift_row, 0)
 
-    def convs(step, _):
-        at = pl.multiple_of(step * 480, 16)
-        pre[pl.ds(at, 480), :] = conv(merged_shift, at, 480, fwd_one)
-        grad_hidden[pl.ds(at, 480), :] = conv(grad_shift, at, 480, bwd_two)
-        return 0
-
-    lax.fori_loop(0, 4, convs, 0)
+    pre[...] = conv(merged_shift, 0, 30 * WIDE, fwd_one)
+    grad_hidden[...] = conv(grad_shift, 0, 30 * WIDE, bwd_two)
     grad_ends[0 : 2 * WIDE, :] = grad_shift[0 : 2 * WIDE, :]
     grad_ends[2 * WIDE : 4 * WIDE, :] = grad_shift[30 * WIDE : 32 * WIDE, :]
 
@@ -484,15 +476,15 @@
 def wide_mask(mask_rows, step):
     spread = one_hot((iota((WIDE, 16), 0) >> 2) == iota((WIDE, 16), 1))
     parts = []
-    for tile_row in range(2):
-        at = pl.multiple_of((step * 2 + tile_row) * 16, 16)
+    for tile_row in range(4):
+        at = pl.multiple_of((step * 4 + tile_row) * 16, 16)
         parts.extend([dot(spread, mask_rows[pl.ds(at, 16), :].astype(BF))] * 4)
     return jnp.concatenate(parts, axis=0)
 
 
-def load_shifted(values, weight, edges, base, plain, held, shifted, semaphores):
+def load_shifted(values, filter_in, edges, base, plain, filter_held, weight, forward, shifted, semaphores):
     cuts = (0, 640, 1152, 1664, 2176)
-    pairs = [(weight.at[pl.ds(part * 768, 768)], held.at[pl.ds(part * 768, 768)]) for part in range(3)]
+    pairs = [(filter_in, filter_held)]
     for first, last in zip(cuts[:-1], cuts[1:]):
         pairs.append((values.at[pl.ds(first, last - first)], plain.at[pl.ds(first, last - first)]))
     copies = start_copies(pairs, semaphores)
@@ -506,60 +498,61 @@
         )
         return 0
 
-    for part in range(4):
-        copies[3 + part].wait()
-        lax.fori_loop(cuts[part] // WIDE, cuts[part + 1] // WIDE, row_of, 0)
-    for copy in copies[:3]:
+    copies[0].wait()
+    build_weight(filter_held, weight, forward)
+    for copy in copies[1:]:
         copy.wait()
+    lax.fori_loop(0, ROWS + 2, row_of, 0)
 
 
 def backward_kernel(
-    pre_in, weight_in, edges, mask_rows, tiles, low_grad, pair, plain, bwd_one, pre_shift, semaphores
+    pre_in, filter_in, edges, mask_rows, tiles, low_grad,
+    pair, plain, filter_held, bwd_one, pre_shift, semaphores,
 ):
     two = 2 * WIDE
-    load_shifted(pre_in, weight_in, edges, 80, plain, bwd_one, pre_shift, semaphores)
+    load_shifted(pre_in, filter_in, edges, 80, plain, filter_held, bwd_one, False, pre_shift, semaphores)
     order = iota((F, F), 0)
     tile_order = one_hot(
         iota((F, F), 1) == (((order >> 2) & 3) * WIDE + (order >> 4) * 4 + (order & 3))
     )
 
     def body(step, _):
-        at = pl.multiple_of(step * 512, 512)
-        grad_merged = conv(pre_shift, at, 512, bwd_one) * wide_mask(mask_rows, step)
+        at = pl.multiple_of(step * 1024, 1024)
+        grad_merged = conv(pre_shift, at, 1024, bwd_one) * wide_mask(mask_rows, step)
         rounded = grad_merged.astype(BF)
-        for tile_row in range(2):
+        for tile_row in range(4):
             tiles[pl.ds(at + tile_row * F, F), :] = dot(
                 tile_order, rounded[tile_row * F : (tile_row + 1) * F, :]
             ).astype(BF)
-        for row in range(4):
+        for row in range(8):
             both = grad_merged[row * two : row * two + WIDE, :] + grad_merged[row * two + WIDE : row * two + two, :]
             for half in range(2):
                 pair[half, row * WIDE : (row + 1) * WIDE, :] = both[:, half * 128 : half * 128 + 128]
         for half in range(2):
-            low_grad[pl.ds(pl.multiple_of(step * 128, 128), 128), half * 128 : half * 128 + 128] = (
-                pair[half, pl.ds(0, 128, stride=2), :] + pair[half, pl.ds(1, 128, stride=2), :]
+            low_grad[pl.ds(pl.multiple_of(step * 256, 256), 256), half * 128 : half * 128 + 128] = (
+                pair[half, pl.ds(0, 256, stride=2), :] + pair[half, pl.ds(1, 256, stride=2), :]
             ).astype(BF)
         return 0
 
-    lax.fori_loop(0, 4, body, 0)
+    lax.fori_loop(0, 2, body, 0)
 
 
 def forward_kernel(
-    hidden_in, weight_in, edges, mask_rows, output, plain, fwd_two, hidden_shift, semaphores
+    hidden_in, filter_in, edges, mask_rows, output, plain, filter_held, fwd_two, hidden_shift, semaphores
 ):
-    load_shifted(hidden_in, weight_in, edges, 0, plain, fwd_two, hidden_shift, semaphores)
+    load_shifted(hidden_in, filter_in, edges, 0, plain, filter_held, fwd_two, True, hidden_shift, semaphores)
 
     def body(step, _):
-        at = pl.multiple_of(step * 512, 512)
-        output[pl.ds(at, 512), :] = (
-            conv(hidden_shift, at, 512, fwd_two) * wide_mask(mask_rows, step)
+        at = pl.multiple_of(step * 1024, 1024)
+        output[pl.ds(at, 1024), :] = (
+            conv(hidden_shift, at, 1024, fwd_two) * wide_mask(mask_rows, step)
         ).astype(BF)
         return 0
 
-    lax.fori_loop(0, 4, body, 0)
-
-
-def pack_kernel(places, tiles, got, slot_rows, send):
+    lax.fori_loop(0, 2, body, 0)
+
+
+def pack_kernel(places, tiles, send):
     def copy(group, _):
         for sub in range(8):
             tile = group * 8 + sub
@@ -570,16 +563,21 @@
         return 0
 
     lax.fori_loop(0, 16, copy, 0)
+
+
+def terms_kernel(send_in, got, slot_rows, send, rows, semaphore):
     total = jnp.zeros((16, 128), F32)
     for part in range(128):
         total = total + got[part, :, :].astype(F32)
     low = total[0:8, :].astype(BF)
-    high = jnp.where(iota((8, 128), 0) == 0, total[8:16, :], 0.0)
+    row = iota((8, 128), 0)
+    high = jnp.where(row == 0, total[8:16, :], 0.0)
     for part in range(128):
-        send[part, 32:40, 0:128] = low
-        send[part, 32:40, 128:256] = jnp.where(
-            iota((8, 128), 0) == 1, slot_rows[part : part + 1, :], high
-        ).astype(BF)
+        rows[part, :, 0:128] = low
+        rows[part, :, 128:256] = jnp.where(row == 1, slot_rows[part : part + 1, :], high).astype(BF)
+    copy = pltpu.make_async_copy(rows, send.at[:, pl.ds(32, 8)], semaphore)
+    copy.start()
+    copy.wait()
 
 
 def place_kernel(scale, got, skip_grad, one, two, gathered, sources, folded, table, semaphore):
@@ -638,27 +636,22 @@
         ],
         specs=[HBM] * 4, name="head",
     )(*given)
-    merged, grad_two, mask_rows = call(
-        prep_kernel,
-        [shape((pixels, F)), shape((pixels, F)), shape((128, F), F32)],
-        4,
+    near_rows = swap(near, "rows", 0)
+    far_rows = swap(far_side, "rows", 1)
+    bases = [f.transpose(1, 2, 0, 3).reshape(288, F) for f in (filter_one, filter_two)]
+    merged, grad_two, mask_rows, fwd_one, bwd_two, places, slot_rows = call(
+        prepare_kernel,
+        [
+            shape((pixels, F)), shape((pixels, F)), shape((128, F), F32), shape((9 * F, F)),
+            shape((9 * F, F)), shape((8, 128), jnp.int32), shape((128, 128), F32),
+        ],
+        7,
         [
             pltpu.VMEM((pixels // 4, F), BF), pltpu.VMEM((pixels, F), BF), pltpu.VMEM((pixels, F), BF),
             pltpu.VMEM((8, 16), jnp.int32), pltpu.SemaphoreType.DMA((13,)),
         ],
-        specs=[HBM] * 4, name="prep",
-    )(*given)
-    near_rows = swap(near, "rows", 0)
-    far_rows = swap(far_side, "rows", 1)
-    bases = [f.transpose(1, 2, 0, 3).reshape(288, F) for f in (filter_one, filter_two)]
-    weights = shape((9 * F, F))
-    fwd_one, bwd_two, fwd_two, bwd_one, places, slot_rows = call(
-        expand_kernel,
-        [weights] * 2 + [far((9 * F, F))] * 2 + [shape((8, 128), jnp.int32), shape((128, 128), F32)],
-        3,
-        [pltpu.VMEM((9 * F, F), BF), pltpu.VMEM((9 * F, F), BF), pltpu.SemaphoreType.DMA((2,))],
-        outs=[VMEM, VMEM, HBM, HBM, VMEM, VMEM], name="expand",
-    )(owner_slot, *bases)
+        specs=[HBM] * 4 + [VMEM] * 3, flops=3 << 30, name="prepare",
+    )(*given, owner_slot, *bases)
     left, right, top, bottom, near, far_side = call(
         edge_kernel,
         [shape((5 * STRIP, F))] * 2 + [shape((272, F))] * 2 + [shape((5 * STRIP, F))] * 2,
@@ -690,21 +683,30 @@
     )(merged, grad_two, top, bottom, left, right, near_cols, far_cols, mask_rows, fwd_one, bwd_two, *inner)
     got_terms = lax.all_to_all(message, everyone, 0, 0, tiled=True)
     loading = [
-        pltpu.VMEM((34 * WIDE, F), BF), pltpu.VMEM((9 * F, F), BF), pltpu.VMEM((34 * WIDE, 3 * F), BF),
-        pltpu.SemaphoreType.DMA((7,)),
+        pltpu.VMEM((34 * WIDE, F), BF), pltpu.VMEM((288, F), BF), pltpu.VMEM((9 * F, F), BF),
+        pltpu.VMEM((34 * WIDE, 3 * F), BF), pltpu.SemaphoreType.DMA((5,)),
     ]
     tiles, low_grad = call(
         backward_kernel, [shape((pixels, F)), shape((pixels // 4, F))], 4,
-        [pltpu.VMEM((2, 4 * WIDE, 128), F32)] + loading, specs=[HBM, HBM, VMEM, VMEM],
+        [pltpu.VMEM((2, 8 * WIDE, 128), F32)] + loading, specs=[HBM, HBM, VMEM, VMEM],
         flops=3 << 30, name="backward",
-    )(kept(grad_pre), kept(bwd_one), edges, mask_rows)
+    )(kept(grad_pre), kept(bases[0]), edges, mask_rows)
     output = call(
         forward_kernel, shape((pixels, F)), 4, loading, specs=[HBM, HBM, VMEM, VMEM],
         flops=3 << 30, name="forward",
-    )(kept(hidden), kept(fwd_two), edges, mask_rows)
-    send = call(
-        pack_kernel, shape((128, 40, F)), 4, specs=[SMEM, VMEM, VMEM, VMEM], name="pack"
-    )(places, tiles, got_terms, slot_rows)
+    )(kept(hidden), kept(bases[1]), edges, mask_rows)
+    send = call(pack_kernel, far((128, 40, F)), 2, specs=[SMEM, VMEM], name="pack")(places, tiles)
+    send = pl.pallas_call(
+        terms_kernel,
+        out_shape=far((128, 40, F)),
+        in_specs=[HBM, VMEM, VMEM],
+        out_specs=HBM,
+        scratch_shapes=[pltpu.VMEM((128, 8, F), BF), pltpu.SemaphoreType.DMA],
+        input_output_aliases={0: 0},
+        compiler_params=pltpu.CompilerParams(vmem_limit_bytes=24 << 20),
+        cost_estimate=pl.CostEstimate(flops=1 << 30, bytes_accessed=4 << 20, transcendentals=0),
+        name="terms",
+    )(kept(send), got_terms, slot_rows)
     got = lax.all_to_all(send, everyone, 0, 0, tiled=True)
     scale = 1.0 / math.sqrt(pixels * lax.axis_size("rows") * lax.axis_size("cols"))
     skip_grad, one, two = call(

time: 105 us -> 102 us (0.971)
  waiting for transfers between devices: 35.5 us -> 32.7 us
  Pallas kernels: 44.9 us -> 43.3 us
  starting transfers between devices: 22.9 us -> 24.2 us
    all_to_all x1, waiting for transfers between devices: 6.91 us -> 4.54 us  [on_device(): got_terms = lax.all_to_all(message, everyone, 0, 0, tiled=True)]
    all_to_all x1, starting transfers between devices: 4.05 us -> 5.22 us  [on_device(): got = lax.all_to_all(send, everyone, 0, 0, tiled=True)]
  transfers between devices with their start and end apart: 6 -> 6, of which waited for: 2 -> 2; matrix products, arithmetic and copies ran while one was open for 0% -> 0% of each run, Pallas kernels for 24% -> 25%
where the time goes in v5:
time: 102 us; the launch traced here: 101 us
  Pallas kernels  43.3 us (42%)
  waiting for transfers between devices  32.7 us (32%)
  starting transfers between devices  24.2 us (24%)
    all_to_all x1, waiting for transfers between devices, on_device(): got = lax.all_to_all(send, everyone, 0, 0, tiled=True)  28.2 us
    pallas_call x1, Pallas kernels, on_device(): call(first_kernel, [far((34 * WIDE, F)), far((34 * WIDE, F)), shape((160,...  12.4 us
    all_to_all x1, starting transfers between devices, on_device(): got_terms = lax.all_to_all(message, everyone, 0, 0, tiled=True)  12.2 us
    ppermute x4, starting transfers between devices, swap(): return lax.ppermute(values, axis, list(enumerate(partner)))  6.82 us
    pallas_call x1, Pallas kernels, on_device(): call(backward_kernel, [shape((pixels, F)), shape((pixels // 4, F))], 4, [...  6.77 us
    pallas_call x1, Pallas kernels, on_device(): call(forward_kernel, shape((pixels, F)), 4, loading, specs=[HBM, HBM, VME...  6.43 us
    pallas_call x1, Pallas kernels, on_device(): call(interior_kernel, [shape((pixels, 3 * F)), shape((30 * WIDE, F), F32)...  5.85 us
    all_to_all x1, starting transfers between devices, on_device(): got = lax.all_to_all(send, everyone, 0, 0, tiled=True)  5.22 us
  transfers between devices with their start and end apart: 6, of which 2 were waited for; matrix products, arithmetic and copies ran while one was open for 0% of the time, Pallas kernels for 25%

profile of v5, /device:TPU:1, one launch (start us, length us, event | category | flops | bytes accessed | tf_op | source)
XLA Modules:
  0.0 101.2 jit_solution(12536072094389565854)
XLA Ops:
  0.6 0.0 copy-start
  0.6 0.0 copy-start.1
  0.7 0.0 copy-start.2
  0.7 1.3 %head.1 = (bf16[272,256]{1,0:T(8,128)(2,1)S(1)}, bf16[272,256]{1,0:T(8,128)(2,1)S(1)}) custom-call(bf16[512,256]{1,0:T(8,128)(2,1)} %bitcast.25, bf16[2048,256]{1,0:T(8,128)(2,1)} %bitcast.21, bf16[2048,256]{1,0:T(8,128)(2,1)} %bitcast.23, s32[8,16]{1,0:T(8,128)} %tissue_in.3), custom_call_target="tpu_custom_call" | custom-call | flops 1073741824 | bytes 4194304 | tf_op jit(solution)/shard_map/head/pallas_call | solution.py:630
  2.0 1.5 %collective-permute-start = (bf16[272,256]{1,0:T(8,128)(2,1)S(1)}, bf16[272,256]{1,0:T(8,128)(2,1)S(1)}, u32[]{:S(2)}, u32[]{:S(2)}) collective-permute-start(bf16[272,256]{1,0:T(8,128)(2,1)S(1)} %get-tuple-element.35), channel_id=1, source_target_pairs={{0,16},{16,0},{32,48},{48,32},{64,80},{80,64},{96,112},{112,96},{1... | collective-permute-start | bytes 417800 | tf_op jit(solution)/shard_map/ppermute | solution.py:619
  3.5 3.1 %collective-permute-start.1 = (bf16[272,256]{1,0:T(8,128)(2,1)S(1)}, bf16[272,256]{1,0:T(8,128)(2,1)S(1)}, u32[]{:S(2)}, u32[]{:S(2)}) collective-permute-start(bf16[272,256]{1,0:T(8,128)(2,1)S(1)} %get-tuple-element.36), channel_id=1, source_target_pairs={{0,0},{16,32},{32,16},{48,64},{64,48},{80,96},{96,80},{112,112},{1... | collective-permute-start | bytes 417800 | tf_op jit(solution)/shard_map/ppermute | solution.py:619
  6.6 0.0 copy-done
  6.6 0.0 copy-done.1
  6.6 0.0 copy-done.2
  6.7 3.6 %prepare.1 = (bf16[2048,256]{1,0:T(8,128)(2,1)S(1)}, bf16[2048,256]{1,0:T(8,128)(2,1)S(1)}, f32[128,256]{1,0:T(8,128)S(1)}, bf16[2304,256]{1,0:T(8,128)(2,1)S(1)...) custom-call(bf16[512,256]{1,0:T(8,128)(2,1)} %bitcast.26, ...), custom_call_target="tpu_custom_call" | custom-call | flops 3221225472 | bytes 4194304 | tf_op jit(solution)/shard_map/prepare/pallas_call | solution.py:642
  10.3 0.0 collective-permute-done.near_in
  10.3 0.0 collective-permute-done.1.far_in
  10.3 0.3 edge.1
  10.6 1.4 %collective-permute-start.2 = (bf16[240,256]{1,0:T(8,128)(2,1)S(1)}, bf16[240,256]{1,0:T(8,128)(2,1)S(1)}, u32[]{:S(2)}, u32[]{:S(2)}) collective-permute-start(bf16[240,256]{1,0:T(8,128)(2,1)S(1)} %get-tuple-element.42), channel_id=1, source_target_pairs={{0,1},{1,0},{2,3},{3,2},{4,5},{5,4},{6,7},{7,6},{8,9},{9,8},{10,11... | collective-permute-start | bytes 368648 | tf_op jit(solution)/shard_map/ppermute | solution.py:619
  12.0 0.8 collective-permute-start.3
  12.8 5.9 %interior.1 = (bf16[2048,768]{1,0:T(8,128)(2,1)S(1)}, f32[1920,256]{1,0:T(8,128)S(1)}, f32[1920,256]{1,0:T(8,128)S(1)}, bf16[256,768]{1,0:T(8,128)(2,1)S(1)}) custom-call(bf16[2048,256]{1,0:T(8,128)(2,1)S(1)} %get-tuple-element.33.merged, bf16[2048,256]{1,0:T(8,128)(2,1)S(1)} %get-tuple-element.34.grad_two, bf16[2304,256]{1,0:T(8,128)(2,1)S(1)} %get-tuple-element.44.fwd_one, ...), custom_call_target="tpu_custom_call" | custom-call | flops 5368709120 | bytes 4194304 | tf_op jit(solution)/shard_map/interior/pallas_call | solution.py:662
  18.7 0.0 collective-permute-done.2.near
  18.7 0.0 collective-permute-done.3.far_side
  18.7 12.4 %first.1 = (bf16[2176,256]{1,0:T(8,128)(2,1)}, bf16[2176,256]{1,0:T(8,128)(2,1)}, f32[160,256]{1,0:T(8,128)S(1)}, bf16[128,16,128]{2,1,0:T(8,128)(2,1)}) custom-call(bf16[2048,256]{1,0:T(8,128)(2,1)S(1)} %get-tuple-element.33.merged, bf16[2048,256]{1,0:T(8,128)(2,1)S(1)} %get-tuple-element.34.grad_two, bf16[272,256]{1,0:T(8,128)(2,1)S(1)} %get-tuple-element.38.top, ...), custom_call_target="tpu_custom_call" | custom-call | flops 10737418240 | bytes 4194304 | tf_op jit(solution)/shard_map/first/pallas_call | solution.py:670
  31.2 12.2 %all-to-all-start = ((bf16[128,16,128]{2,1,0:T(8,128)(2,1)}), bf16[128,16,128]{2,1,0:T(8,128)(2,1)S(1)}, u32[]{:S(2)}, u32[]{:S(2)}) async-start(bf16[128,16,128]{2,1,0:T(8,128)(2,1)} %get-tuple-element.55), calls=%async_computation | async-start | bytes 1048576 | tf_op jit(solution)/shard_map/all_to_all | solution.py:684
  43.4 6.8 %backward.1 = (bf16[2048,256]{1,0:T(8,128)(2,1)S(1)}, bf16[512,256]{1,0:T(8,128)(2,1)}) custom-call(bf16[2176,256]{1,0:T(8,128)(2,1)} %get-tuple-element.53.pre_in, bf16[288,256]{1,0:T(8,128)(2,1)} %bitcast.17, f32[160,256]{1,0:T(8,128)S(1)} %get-tuple-element.51.edges, f32[128,256]{1,0:T(8,128)S(1)} %get-tuple-element.37.mask_rows), custom_call_target="tpu_custom_call" | custom-call | flops 3221225472 | bytes 4194304 | tf_op jit(solution)/shard_map/backward/pallas_call | solution.py:689
  50.1 2.7 %pack.1.send_in = bf16[128,40,256]{2,1,0:T(8,128)(2,1)} custom-call(s32[8,128]{1,0:T(8,128)S(1)} %get-tuple-element.52.places, bf16[2048,256]{1,0:T(8,128)(2,1)S(1)} %get-tuple-element.54.tiles), custom_call_target="tpu_custom_call" | custom-call | flops 1073741824 | bytes 4194304 | tf_op jit(solution)/shard_map/pack/pallas_call | solution.py:698
  52.9 4.5 %all-to-all-done.got = bf16[128,16,128]{2,1,0:T(8,128)(2,1)S(1)} async-done(((bf16[128,16,128]{2,1,0:T(8,128)(2,1)}), bf16[128,16,128]{2,1,0:T(8,128)(2,1)S(1)}, u32[]{:S(2)}, u32[]{:S(2)}) %all-to-all-start) | async-done | bytes 524320 | tf_op jit(solution)/shard_map/all_to_all | solution.py:684
  57.4 1.1 %terms.1 = bf16[128,40,256]{2,1,0:T(8,128)(2,1)} custom-call(bf16[128,40,256]{2,1,0:T(8,128)(2,1)} %pack.1.send_in, bf16[128,16,128]{2,1,0:T(8,128)(2,1)S(1)} %all-to-all-done.got, f32[128,128]{1,0:T(8,128)S(1)} %get-tuple-element.56.slot_rows), custom_call_target="tpu_custom_call", output_to_operand_aliasing={{}: (0, {})} | custom-call | flops 1073741824 | bytes 4194304 | tf_op jit(solution)/shard_map/terms/pallas_call | solution.py:699
  58.5 5.2 %all-to-all-start.1 = ((bf16[128,40,256]{2,1,0:T(8,128)(2,1)}), bf16[128,40,256]{2,1,0:T(8,128)(2,1)S(1)}, u32[]{:S(2)}, u32[]{:S(2)}) async-start(bf16[128,40,256]{2,1,0:T(8,128)(2,1)} %terms.1), calls=%async_computation.1 | async-start | bytes 5242880 | tf_op jit(solution)/shard_map/all_to_all | solution.py:710
  63.8 6.4 %forward.1 = bf16[2048,256]{1,0:T(8,128)(2,1)} custom-call(bf16[2176,256]{1,0:T(8,128)(2,1)} %get-tuple-element.50.hidden_in, bf16[288,256]{1,0:T(8,128)(2,1)} %bitcast.19, f32[160,256]{1,0:T(8,128)S(1)} %get-tuple-element.51.edges, f32[128,256]{1,0:T(8,128)S(1)} %get-tuple-element.37.mask_rows), custom_call_target="tpu_custom_call" | custom-call | flops 3221225472 | bytes 4194304 | tf_op jit(solution)/shard_map/forward/pallas_call | solution.py:694
  70.2 28.2 %all-to-all-done.1.got = bf16[128,40,256]{2,1,0:T(8,128)(2,1)S(1)} async-done(((bf16[128,40,256]{2,1,0:T(8,128)(2,1)}), bf16[128,40,256]{2,1,0:T(8,128)(2,1)S(1)}, u32[]{:S(2)}, u32[]{:S(2)}) %all-to-all-start.1) | async-done | bytes 2621472 | tf_op jit(solution)/shard_map/all_to_all | solution.py:710
  98.4 2.6 %place.1 = (bf16[128,4,4,256]{3,2,1,0:T(4,128)(2,1)}, f32[288,256]{1,0:T(8,128)}, f32[288,256]{1,0:T(8,128)}) custom-call(bf16[128,40,256]{2,1,0:T(8,128)(2,1)S(1)} %all-to-all-done.1.got), custom_call_target="tpu_custom_call" | custom-call | flops 1073741824 | bytes 4194304 | tf_op jit(solution)/shard_map/place/pallas_call | solution.py:712
Async XLA Ops:
  0.6 6.0 %copy-start = (bf16[32,3,3,256]{3,0,2,1:T(8,128)(2,1)S(1)}, bf16[32,3,3,256]{3,0,2,1:T(8,128)(2,1)}, u32[]{:S(2)}) copy-start(bf16[32,3,3,256]{3,0,2,1:T(8,128)(2,1)} %param.11) | copy-start | bytes 442372
  0.6 6.0 %copy-start.1 = (bf16[32,3,3,256]{3,0,2,1:T(8,128)(2,1)S(1)}, bf16[32,3,3,256]{3,0,2,1:T(8,128)(2,1)}, u32[]{:S(2)}) copy-start(bf16[32,3,3,256]{3,0,2,1:T(8,128)(2,1)} %param.12) | copy-start | bytes 442372
  0.7 6.0 %copy-start.2 = (s32[8,16]{1,0:T(8,128)S(1)}, s32[8,16]{1,0:T(8,128)}, u32[]{:S(2)}) copy-start(s32[8,16]{1,0:T(8,128)} %slots.1) | copy-start | bytes 1540
  2.0 8.3 %collective-permute-start = (bf16[272,256]{1,0:T(8,128)(2,1)S(1)}, bf16[272,256]{1,0:T(8,128)(2,1)S(1)}, u32[]{:S(2)}, u32[]{:S(2)}) collective-permute-start(bf16[272,256]{1,0:T(8,128)(2,1)S(1)} %get-tuple-element.35), channel_id=1, source_target_pairs={{0,16},{16,0},{32,48},{48,32},{64,80},{80,64},{96,112},{112,96},{1... | collective-permute-start | bytes 417800 | tf_op jit(solution)/shard_map/ppermute | solution.py:619
  3.5 6.8 %collective-permute-start.1 = (bf16[272,256]{1,0:T(8,128)(2,1)S(1)}, bf16[272,256]{1,0:T(8,128)(2,1)S(1)}, u32[]{:S(2)}, u32[]{:S(2)}) collective-permute-start(bf16[272,256]{1,0:T(8,128)(2,1)S(1)} %get-tuple-element.36), channel_id=1, source_target_pairs={{0,0},{16,32},{32,16},{48,64},{64,48},{80,96},{96,80},{112,112},{1... | collective-permute-start | bytes 417800 | tf_op jit(solution)/shard_map/ppermute | solution.py:619
  10.6 8.1 %collective-permute-start.2 = (bf16[240,256]{1,0:T(8,128)(2,1)S(1)}, bf16[240,256]{1,0:T(8,128)(2,1)S(1)}, u32[]{:S(2)}, u32[]{:S(2)}) collective-permute-start(bf16[240,256]{1,0:T(8,128)(2,1)S(1)} %get-tuple-element.42), channel_id=1, source_target_pairs={{0,1},{1,0},{2,3},{3,2},{4,5},{5,4},{6,7},{7,6},{8,9},{9,8},{10,11... | collective-permute-start | bytes 368648 | tf_op jit(solution)/shard_map/ppermute | solution.py:619
  12.0 6.7 %collective-permute-start.3 = (bf16[240,256]{1,0:T(8,128)(2,1)S(1)}, bf16[240,256]{1,0:T(8,128)(2,1)S(1)}, u32[]{:S(2)}, u32[]{:S(2)}) collective-permute-start(bf16[240,256]{1,0:T(8,128)(2,1)S(1)} %get-tuple-element.43), channel_id=1, source_target_pairs={{0,0},{1,2},{2,1},{3,4},{4,3},{5,6},{6,5},{7,8},{8,7},{9,10},{10,9... | collective-permute-start | bytes 368648 | tf_op jit(solution)/shard_map/ppermute | solution.py:619
  31.2 26.3 %all-to-all-start = ((bf16[128,16,128]{2,1,0:T(8,128)(2,1)}), bf16[128,16,128]{2,1,0:T(8,128)(2,1)S(1)}, u32[]{:S(2)}, u32[]{:S(2)}) async-start(bf16[128,16,128]{2,1,0:T(8,128)(2,1)} %get-tuple-element.55), calls=%async_computation | async-start | bytes 1048576 | tf_op jit(solution)/shard_map/all_to_all | solution.py:684
  58.5 39.9 %all-to-all-start.1 = ((bf16[128,40,256]{2,1,0:T(8,128)(2,1)}), bf16[128,40,256]{2,1,0:T(8,128)(2,1)S(1)}, u32[]{:S(2)}, u32[]{:S(2)}) async-start(bf16[128,40,256]{2,1,0:T(8,128)(2,1)} %terms.1), calls=%async_computation.1 | async-start | bytes 5242880 | tf_op jit(solution)/shard_map/all_to_all | solution.py:710

commit v6 on v5

--- a/solution.py
+++ b/solution.py
@@ -468,7 +468,8 @@
     folded[576:592, :] = jnp.zeros((16, F), F32)
     for part in range(128):
         start, lanes = 9 * (part % 64), (part // 64) * 128
-        message[part, :, :] = folded[start : start + 16, lanes : lanes + 128].astype(BF)
+        data = folded[start : start + 16, lanes : lanes + 128].reshape(4, 4, 128)
+        message[part] = data[0:3].astype(BF)
     for copy in copies:
         copy.wait()
 
@@ -557,36 +558,36 @@
         for sub in range(8):
             tile = group * 8 + sub
             place = places[0, tile]
-            send[place >> 1, pl.ds(pl.multiple_of((place & 1) * 16, 16), 16), :] = tiles[
-                pl.ds(pl.multiple_of(tile * 16, 16), 16), :
-            ]
+            for half in range(2):
+                value = tiles[pl.ds(pl.multiple_of(tile * 16, 16), 16), half * 128 : half * 128 + 128]
+                send[place >> 1, pl.ds((place & 1) * 8 + half * 4, 4)] = value.reshape(4, 4, 128)
         return 0
 
     lax.fori_loop(0, 16, copy, 0)
 
 
 def terms_kernel(send_in, got, slot_rows, send, rows, semaphore):
-    total = jnp.zeros((16, 128), F32)
+    total = jnp.zeros((3, 4, 128), F32)
     for part in range(128):
-        total = total + got[part, :, :].astype(F32)
-    low = total[0:8, :].astype(BF)
-    row = iota((8, 128), 0)
-    high = jnp.where(row == 0, total[8:16, :], 0.0)
+        total = total + got[part].astype(F32)
+    front = total[0:2].astype(BF)
+    row = iota((4, 128), 0)
     for part in range(128):
-        rows[part, :, 0:128] = low
-        rows[part, :, 128:256] = jnp.where(row == 1, slot_rows[part : part + 1, :], high).astype(BF)
-    copy = pltpu.make_async_copy(rows, send.at[:, pl.ds(32, 8)], semaphore)
+        rows[part, 0:2] = front
+        rows[part, 2] = jnp.where(row == 1, slot_rows[part : part + 1, :], total[2]).astype(BF)
+    copy = pltpu.make_async_copy(rows, send.at[:, pl.ds(16, 3)], semaphore)
     copy.start()
     copy.wait()
 
 
 def place_kernel(scale, got, skip_grad, one, two, gathered, sources, folded, table, semaphore):
     for part in range(128):
-        terms = got[part, 32:40, :].astype(F32) * scale
         start, lanes = 9 * (part % 64), (part // 64) * 128
-        folded[start : start + 8, lanes : lanes + 128] = terms[:, 0:128]
-        folded[start + 8 : start + 9, lanes : lanes + 128] = terms[0:1, 128:256]
-        gathered[part : part + 1, :] = terms[1:2, 128:256] / scale
+        terms = got[part, 16:19].astype(F32)
+        folded[start : start + 4, lanes : lanes + 128] = terms[0] * scale
+        folded[start + 4 : start + 8, lanes : lanes + 128] = terms[1] * scale
+        folded[start + 8 : start + 9, lanes : lanes + 128] = terms[2, 0:1] * scale
+        gathered[part : part + 1, :] = terms[2, 1:2]
     one[...] = folded[0:288, :]
     two[...] = folded[288:576, :]
     slots = gathered[...].T
@@ -604,8 +605,10 @@
         for sub in range(8):
             slot = group * 8 + sub
             place = table[0, slot]
-            tile = got[place >> 1, pl.ds(pl.multiple_of((place & 1) * 16, 16), 16), :]
-            skip_grad[slot] = tile.reshape(4, 4, F)
+            for half in range(2):
+                skip_grad[slot, :, :, half * 128 : half * 128 + 128] = got[
+                    place >> 1, pl.ds((place & 1) * 8 + half * 4, 4)
+                ]
         return 0
 
     lax.fori_loop(0, 16, put, 0)
@@ -669,7 +672,7 @@
     )(merged, grad_two, fwd_one, bwd_two)
     hidden, grad_pre, edges, message = call(
         first_kernel,
-        [far((34 * WIDE, F)), far((34 * WIDE, F)), shape((160, F), F32), shape((128, 16, 128))],
+        [far((34 * WIDE, F)), far((34 * WIDE, F)), shape((160, F), F32), shape((128, 3, 4, 128))],
         15,
         [
             pltpu.VMEM((34 * WIDE, 3 * F), BF), pltpu.VMEM((34 * WIDE, 3 * F), BF),
@@ -695,13 +698,13 @@
         forward_kernel, shape((pixels, F)), 4, loading, specs=[HBM, HBM, VMEM, VMEM],
         flops=3 << 30, name="forward",
     )(kept(hidden), kept(bases[1]), edges, mask_rows)
-    send = call(pack_kernel, far((128, 40, F)), 2, specs=[SMEM, VMEM], name="pack")(places, tiles)
+    send = call(pack_kernel, far((128, 19, 4, 128)), 2, specs=[SMEM, VMEM], name="pack")(places, tiles)
     send = pl.pallas_call(
         terms_kernel,
-        out_shape=far((128, 40, F)),
+        out_shape=far((128, 19, 4, 128)),
         in_specs=[HBM, VMEM, VMEM],
         out_specs=HBM,
-        scratch_shapes=[pltpu.VMEM((128, 8, F), BF), pltpu.SemaphoreType.DMA],
+        scratch_shapes=[pltpu.VMEM((128, 3, 4, 128), BF), pltpu.SemaphoreType.DMA],
         input_output_aliases={0: 0},
         compiler_params=pltpu.CompilerParams(vmem_limit_bytes=24 << 20),
         cost_estimate=pl.CostEstimate(flops=1 << 30, bytes_accessed=4 << 20, transcendentals=0),

time: 102 us -> 100 us (0.980)
  waiting for transfers between devices: 32.7 us -> 30.1 us
  starting transfers between devices: 24.2 us -> 25.5 us
    all_to_all x1, waiting for transfers between devices: 28.2 us -> 26.8 us  [on_device(): got = lax.all_to_all(send, everyone, 0, 0, tiled=True)]
    all_to_all x1, starting transfers between devices: 5.22 us -> 6.52 us  [on_device(): got = lax.all_to_all(send, everyone, 0, 0, tiled=True)]
    all_to_all x1, waiting for transfers between devices: 4.54 us -> 3.25 us  [on_device(): got_terms = lax.all_to_all(message, everyone, 0, 0, tiled=True)]
where the time goes in v6:
time: 100 us; the launch traced here: 99.9 us
  Pallas kernels  43.3 us (43%)
  waiting for transfers between devices  30.1 us (30%)
  starting transfers between devices  25.5 us (26%)
    all_to_all x1, waiting for transfers between devices, on_device(): got = lax.all_to_all(send, everyone, 0, 0, tiled=True)  26.8 us
    pallas_call x1, Pallas kernels, on_device(): call(first_kernel, [far((34 * WIDE, F)), far((34 * WIDE, F)), shape((160,...  12.4 us
    all_to_all x1, starting transfers between devices, on_device(): got_terms = lax.all_to_all(message, everyone, 0, 0, tiled=True)  12.2 us
    ppermute x4, starting transfers between devices, swap(): return lax.ppermute(values, axis, list(enumerate(partner)))  6.82 us
    pallas_call x1, Pallas kernels, on_device(): call(backward_kernel, [shape((pixels, F)), shape((pixels // 4, F))], 4, [...  6.77 us
    all_to_all x1, starting transfers between devices, on_device(): got = lax.all_to_all(send, everyone, 0, 0, tiled=True)  6.52 us
    pallas_call x1, Pallas kernels, on_device(): call(forward_kernel, shape((pixels, F)), 4, loading, specs=[HBM, HBM, VME...  6.44 us
    pallas_call x1, Pallas kernels, on_device(): call(interior_kernel, [shape((pixels, 3 * F)), shape((30 * WIDE, F), F32)...  5.85 us
  transfers between devices with their start and end apart: 6, of which 2 were waited for; matrix products, arithmetic and copies ran while one was open for 0% of the time, Pallas kernels for 25%

profile of v6, /device:TPU:1, one launch (start us, length us, event | category | flops | bytes accessed | tf_op | source)
XLA Modules:
  0.0 99.9 jit_solution(14004798702086730656)
XLA Ops:
  0.6 0.0 copy-start
  0.6 0.0 copy-start.1
  0.7 0.0 copy-start.2
  0.7 1.3 %head.1 = (bf16[272,256]{1,0:T(8,128)(2,1)S(1)}, bf16[272,256]{1,0:T(8,128)(2,1)S(1)}) custom-call(bf16[512,256]{1,0:T(8,128)(2,1)} %bitcast.25, bf16[2048,256]{1,0:T(8,128)(2,1)} %bitcast.21, bf16[2048,256]{1,0:T(8,128)(2,1)} %bitcast.23, s32[8,16]{1,0:T(8,128)} %tissue_in.3), custom_call_target="tpu_custom_call" | custom-call | flops 1073741824 | bytes 4194304 | tf_op jit(solution)/shard_map/head/pallas_call | solution.py:633
  2.0 1.5 %collective-permute-start = (bf16[272,256]{1,0:T(8,128)(2,1)S(1)}, bf16[272,256]{1,0:T(8,128)(2,1)S(1)}, u32[]{:S(2)}, u32[]{:S(2)}) collective-permute-start(bf16[272,256]{1,0:T(8,128)(2,1)S(1)} %get-tuple-element.35), channel_id=1, source_target_pairs={{0,16},{16,0},{32,48},{48,32},{64,80},{80,64},{96,112},{112,96},{1... | collective-permute-start | bytes 417800 | tf_op jit(solution)/shard_map/ppermute | solution.py:622
  3.5 3.1 %collective-permute-start.1 = (bf16[272,256]{1,0:T(8,128)(2,1)S(1)}, bf16[272,256]{1,0:T(8,128)(2,1)S(1)}, u32[]{:S(2)}, u32[]{:S(2)}) collective-permute-start(bf16[272,256]{1,0:T(8,128)(2,1)S(1)} %get-tuple-element.36), channel_id=1, source_target_pairs={{0,0},{16,32},{32,16},{48,64},{64,48},{80,96},{96,80},{112,112},{1... | collective-permute-start | bytes 417800 | tf_op jit(solution)/shard_map/ppermute | solution.py:622
  6.6 0.0 copy-done
  6.6 0.0 copy-done.1
  6.6 0.0 copy-done.2
  6.7 3.6 %prepare.1 = (bf16[2048,256]{1,0:T(8,128)(2,1)S(1)}, bf16[2048,256]{1,0:T(8,128)(2,1)S(1)}, f32[128,256]{1,0:T(8,128)S(1)}, bf16[2304,256]{1,0:T(8,128)(2,1)S(1)...) custom-call(bf16[512,256]{1,0:T(8,128)(2,1)} %bitcast.26, ...), custom_call_target="tpu_custom_call" | custom-call | flops 3221225472 | bytes 4194304 | tf_op jit(solution)/shard_map/prepare/pallas_call | solution.py:645
  10.3 0.0 collective-permute-done.near_in
  10.3 0.0 collective-permute-done.1.far_in
  10.3 0.3 edge.1
  10.6 1.4 %collective-permute-start.2 = (bf16[240,256]{1,0:T(8,128)(2,1)S(1)}, bf16[240,256]{1,0:T(8,128)(2,1)S(1)}, u32[]{:S(2)}, u32[]{:S(2)}) collective-permute-start(bf16[240,256]{1,0:T(8,128)(2,1)S(1)} %get-tuple-element.42), channel_id=1, source_target_pairs={{0,1},{1,0},{2,3},{3,2},{4,5},{5,4},{6,7},{7,6},{8,9},{9,8},{10,11... | collective-permute-start | bytes 368648 | tf_op jit(solution)/shard_map/ppermute | solution.py:622
  12.0 0.8 collective-permute-start.3
  12.8 5.9 %interior.1 = (bf16[2048,768]{1,0:T(8,128)(2,1)S(1)}, f32[1920,256]{1,0:T(8,128)S(1)}, f32[1920,256]{1,0:T(8,128)S(1)}, bf16[256,768]{1,0:T(8,128)(2,1)S(1)}) custom-call(bf16[2048,256]{1,0:T(8,128)(2,1)S(1)} %get-tuple-element.33.merged, bf16[2048,256]{1,0:T(8,128)(2,1)S(1)} %get-tuple-element.34.grad_two, bf16[2304,256]{1,0:T(8,128)(2,1)S(1)} %get-tuple-element.44.fwd_one, ...), custom_call_target="tpu_custom_call" | custom-call | flops 5368709120 | bytes 4194304 | tf_op jit(solution)/shard_map/interior/pallas_call | solution.py:665
  18.7 0.0 collective-permute-done.2.near
  18.7 0.0 collective-permute-done.3.far_side
  18.7 12.4 %first.1 = (bf16[2176,256]{1,0:T(8,128)(2,1)}, bf16[2176,256]{1,0:T(8,128)(2,1)}, f32[160,256]{1,0:T(8,128)S(1)}, bf16[128,3,4,128]{3,2,1,0:T(4,128)(2,1)}) custom-call(bf16[2048,256]{1,0:T(8,128)(2,1)S(1)} %get-tuple-element.33.merged, bf16[2048,256]{1,0:T(8,128)(2,1)S(1)} %get-tuple-element.34.grad_two, bf16[272,256]{1,0:T(8,128)(2,1)S(1)} %get-tuple-element.38.top, ...), custom_call_target="tpu_custom_call" | custom-call | flops 10737418240 | bytes 4194304 | tf_op jit(solution)/shard_map/first/pallas_call | solution.py:673
  31.1 12.2 %all-to-all-start = ((bf16[128,3,4,128]{3,2,1,0:T(4,128)(2,1)}), bf16[128,3,4,128]{3,2,1,0:T(4,128)(2,1)S(1)}, u32[]{:S(2)}, u32[]{:S(2)}) async-start(bf16[128,3,4,128]{3,2,1,0:T(4,128)(2,1)} %get-tuple-element.55), calls=%async_computation | async-start | bytes 786432 | tf_op jit(solution)/shard_map/all_to_all | solution.py:687
  43.3 6.8 %backward.1 = (bf16[2048,256]{1,0:T(8,128)(2,1)S(1)}, bf16[512,256]{1,0:T(8,128)(2,1)}) custom-call(bf16[2176,256]{1,0:T(8,128)(2,1)} %get-tuple-element.53.pre_in, bf16[288,256]{1,0:T(8,128)(2,1)} %bitcast.17, f32[160,256]{1,0:T(8,128)S(1)} %get-tuple-element.51.edges, f32[128,256]{1,0:T(8,128)S(1)} %get-tuple-element.37.mask_rows), custom_call_target="tpu_custom_call" | custom-call | flops 3221225472 | bytes 4194304 | tf_op jit(solution)/shard_map/backward/pallas_call | solution.py:692
  50.1 2.7 %pack.1.send_in = bf16[128,19,4,128]{3,2,1,0:T(4,128)(2,1)} custom-call(s32[8,128]{1,0:T(8,128)S(1)} %get-tuple-element.52.places, bf16[2048,256]{1,0:T(8,128)(2,1)S(1)} %get-tuple-element.54.tiles), custom_call_target="tpu_custom_call" | custom-call | flops 1073741824 | bytes 4194304 | tf_op jit(solution)/shard_map/pack/pallas_call | solution.py:701
  52.8 3.3 %all-to-all-done.got = bf16[128,3,4,128]{3,2,1,0:T(4,128)(2,1)S(1)} async-done(((bf16[128,3,4,128]{3,2,1,0:T(4,128)(2,1)}), bf16[128,3,4,128]{3,2,1,0:T(4,128)(2,1)S(1)}, u32[]{:S(2)}, u32[]{:S(2)}) %all-to-all-start) | async-done | bytes 393248 | tf_op jit(solution)/shard_map/all_to_all | solution.py:687
  56.1 1.1 %terms.1 = bf16[128,19,4,128]{3,2,1,0:T(4,128)(2,1)} custom-call(bf16[128,19,4,128]{3,2,1,0:T(4,128)(2,1)} %pack.1.send_in, bf16[128,3,4,128]{3,2,1,0:T(4,128)(2,1)S(1)} %all-to-all-done.got, f32[128,128]{1,0:T(8,128)S(1)} %get-tuple-element.56.slot_rows), custom_call_target="tpu_custom_call", output_to_operand_aliasing={{}: (0, {})} | custom-call | flops 1073741824 | bytes 4194304 | tf_op jit(solution)/shard_map/terms/pallas_call | solution.py:702
  57.1 6.5 %all-to-all-start.1 = ((bf16[128,19,4,128]{3,2,1,0:T(4,128)(2,1)}), bf16[128,19,4,128]{3,2,1,0:T(4,128)(2,1)S(1)}, u32[]{:S(2)}, u32[]{:S(2)}) async-start(bf16[128,19,4,128]{3,2,1,0:T(4,128)(2,1)} %terms.1), calls=%async_computation.1 | async-start | bytes 4980736 | tf_op jit(solution)/shard_map/all_to_all | solution.py:713
  63.7 6.4 %forward.1 = bf16[2048,256]{1,0:T(8,128)(2,1)} custom-call(bf16[2176,256]{1,0:T(8,128)(2,1)} %get-tuple-element.50.hidden_in, bf16[288,256]{1,0:T(8,128)(2,1)} %bitcast.19, f32[160,256]{1,0:T(8,128)S(1)} %get-tuple-element.51.edges, f32[128,256]{1,0:T(8,128)S(1)} %get-tuple-element.37.mask_rows), custom_call_target="tpu_custom_call" | custom-call | flops 3221225472 | bytes 4194304 | tf_op jit(solution)/shard_map/forward/pallas_call | solution.py:697
  70.1 26.8 %all-to-all-done.1.got = bf16[128,19,4,128]{3,2,1,0:T(4,128)(2,1)S(1)} async-done(((bf16[128,19,4,128]{3,2,1,0:T(4,128)(2,1)}), bf16[128,19,4,128]{3,2,1,0:T(4,128)(2,1)S(1)}, u32[]{:S(2)}, u32[]{:S(2)}) %all-to-all-start.1) | async-done | bytes 2490400 | tf_op jit(solution)/shard_map/all_to_all | solution.py:713
  96.9 2.8 %place.1 = (bf16[128,4,4,256]{3,2,1,0:T(4,128)(2,1)}, f32[288,256]{1,0:T(8,128)}, f32[288,256]{1,0:T(8,128)}) custom-call(bf16[128,19,4,128]{3,2,1,0:T(4,128)(2,1)S(1)} %all-to-all-done.1.got), custom_call_target="tpu_custom_call" | custom-call | flops 1073741824 | bytes 4194304 | tf_op jit(solution)/shard_map/place/pallas_call | solution.py:715
Async XLA Ops:
  0.6 6.0 %copy-start = (bf16[32,3,3,256]{3,0,2,1:T(8,128)(2,1)S(1)}, bf16[32,3,3,256]{3,0,2,1:T(8,128)(2,1)}, u32[]{:S(2)}) copy-start(bf16[32,3,3,256]{3,0,2,1:T(8,128)(2,1)} %param.11) | copy-start | bytes 442372
  0.6 6.0 %copy-start.1 = (bf16[32,3,3,256]{3,0,2,1:T(8,128)(2,1)S(1)}, bf16[32,3,3,256]{3,0,2,1:T(8,128)(2,1)}, u32[]{:S(2)}) copy-start(bf16[32,3,3,256]{3,0,2,1:T(8,128)(2,1)} %param.12) | copy-start | bytes 442372
  0.7 6.0 %copy-start.2 = (s32[8,16]{1,0:T(8,128)S(1)}, s32[8,16]{1,0:T(8,128)}, u32[]{:S(2)}) copy-start(s32[8,16]{1,0:T(8,128)} %slots.1) | copy-start | bytes 1540
  2.0 8.3 %collective-permute-start = (bf16[272,256]{1,0:T(8,128)(2,1)S(1)}, bf16[272,256]{1,0:T(8,128)(2,1)S(1)}, u32[]{:S(2)}, u32[]{:S(2)}) collective-permute-start(bf16[272,256]{1,0:T(8,128)(2,1)S(1)} %get-tuple-element.35), channel_id=1, source_target_pairs={{0,16},{16,0},{32,48},{48,32},{64,80},{80,64},{96,112},{112,96},{1... | collective-permute-start | bytes 417800 | tf_op jit(solution)/shard_map/ppermute | solution.py:622
  3.5 6.8 %collective-permute-start.1 = (bf16[272,256]{1,0:T(8,128)(2,1)S(1)}, bf16[272,256]{1,0:T(8,128)(2,1)S(1)}, u32[]{:S(2)}, u32[]{:S(2)}) collective-permute-start(bf16[272,256]{1,0:T(8,128)(2,1)S(1)} %get-tuple-element.36), channel_id=1, source_target_pairs={{0,0},{16,32},{32,16},{48,64},{64,48},{80,96},{96,80},{112,112},{1... | collective-permute-start | bytes 417800 | tf_op jit(solution)/shard_map/ppermute | solution.py:622
  10.6 8.1 %collective-permute-start.2 = (bf16[240,256]{1,0:T(8,128)(2,1)S(1)}, bf16[240,256]{1,0:T(8,128)(2,1)S(1)}, u32[]{:S(2)}, u32[]{:S(2)}) collective-permute-start(bf16[240,256]{1,0:T(8,128)(2,1)S(1)} %get-tuple-element.42), channel_id=1, source_target_pairs={{0,1},{1,0},{2,3},{3,2},{4,5},{5,4},{6,7},{7,6},{8,9},{9,8},{10,11... | collective-permute-start | bytes 368648 | tf_op jit(solution)/shard_map/ppermute | solution.py:622
  12.0 6.7 %collective-permute-start.3 = (bf16[240,256]{1,0:T(8,128)(2,1)S(1)}, bf16[240,256]{1,0:T(8,128)(2,1)S(1)}, u32[]{:S(2)}, u32[]{:S(2)}) collective-permute-start(bf16[240,256]{1,0:T(8,128)(2,1)S(1)} %get-tuple-element.43), channel_id=1, source_target_pairs={{0,0},{1,2},{2,1},{3,4},{4,3},{5,6},{6,5},{7,8},{8,7},{9,10},{10,9... | collective-permute-start | bytes 368648 | tf_op jit(solution)/shard_map/ppermute | solution.py:622
  31.1 24.9 %all-to-all-start = ((bf16[128,3,4,128]{3,2,1,0:T(4,128)(2,1)}), bf16[128,3,4,128]{3,2,1,0:T(4,128)(2,1)S(1)}, u32[]{:S(2)}, u32[]{:S(2)}) async-start(bf16[128,3,4,128]{3,2,1,0:T(4,128)(2,1)} %get-tuple-element.55), calls=%async_computation | async-start | bytes 786432 | tf_op jit(solution)/shard_map/all_to_all | solution.py:687
  57.1 39.8 %all-to-all-start.1 = ((bf16[128,19,4,128]{3,2,1,0:T(4,128)(2,1)}), bf16[128,19,4,128]{3,2,1,0:T(4,128)(2,1)S(1)}, u32[]{:S(2)}, u32[]{:S(2)}) async-start(bf16[128,19,4,128]{3,2,1,0:T(4,128)(2,1)} %terms.1), calls=%async_computation.1 | async-start | bytes 4980736 | tf_op jit(solution)/shard_map/all_to_all | solution.py:713

commit v7 on v6

--- a/solution.py
+++ b/solution.py
@@ -279,7 +279,7 @@
             shifted_store(target, at, plain.astype(F32), plain, nothing, nothing)
             return 0
 
-        lax.fori_loop(0, ROWS, shift_row, 0)
+        lax.fori_loop(0, ROWS, shift_row, 0, unroll=4)
 
     pre[...] = conv(merged_shift, 0, 30 * WIDE, fwd_one)
     grad_hidden[...] = conv(grad_shift, 0, 30 * WIDE, bwd_two)
@@ -369,11 +369,9 @@
                 )
                 return 0
 
-            lax.fori_loop(0, ROWS, patch, 0)
+            lax.fori_loop(0, ROWS, patch, 0, unroll=4)
             ends = [merged_shift[ky * WIDE : ky * WIDE + two, :] for ky in range(3)]
             tails = [merged_shift[(32 + ky) * WIDE : (32 + ky) * WIDE + two, :] for ky in range(3)]
-        lhs = jnp.concatenate([jnp.concatenate(ends, axis=1), jnp.concatenate(tails, axis=1)], axis=0)
-        result[...] = dot(lhs, weight[...])
         row = iota((40, F), 0)
         inner = (row >= 2) & (row < 32)
         for side, (index, kx) in enumerate(((1, 0), (4, 2))):
@@ -397,7 +395,10 @@
                         axis=0,
                     ).astype(BF)
                 )
-        strip_pre.append(dot(jnp.concatenate(parts, axis=1), weight[...]))
+        lhs = jnp.concatenate([jnp.concatenate(group, axis=1) for group in (ends, tails, parts)], axis=0)
+        values = dot(lhs, weight[...])
+        result[...] = values[0:quad, :]
+        strip_pre.append(values[quad:, :])
     strips[0:STRIP, :] = left_strip(4)
     strips[STRIP : 2 * STRIP, :] = right_strip(4)
     strip_mask = jnp.concatenate([strips[1:41, :], strips[STRIP + 1 : STRIP + 41, :]], axis=0)
@@ -434,7 +435,9 @@
 
     ends = functools.partial(activate, pre_from=pre_edge, grad_from=grad_edge)
     lax.fori_loop(0, 2, functools.partial(ends, source_row=0), 0)
-    lax.fori_loop(2, 32, functools.partial(activate, pre_from=pre, grad_from=grad_hidden, source_row=2), 0)
+    lax.fori_loop(
+        2, 32, functools.partial(activate, pre_from=pre, grad_from=grad_hidden, source_row=2), 0, unroll=2
+    )
     lax.fori_loop(32, 34, functools.partial(ends, source_row=30), 0)
     copies = start_copies(
         [(hidden_shift.at[:, F : 2 * F], hidden_out), (pre_shift.at[:, F : 2 * F], pre_out)], semaphores
@@ -503,7 +506,7 @@
     build_weight(filter_held, weight, forward)
     for copy in copies[1:]:
         copy.wait()
-    lax.fori_loop(0, ROWS + 2, row_of, 0)
+    lax.fori_loop(0, ROWS + 2, row_of, 0, unroll=2)
 
 
 def backward_kernel(

time: 100 us -> 100 us (level)
  no operation moved by 1% of the time
where the time goes in v7:
time: 100 us; the launch traced here: 99.7 us
  Pallas kernels  43.1 us (43%)
  waiting for transfers between devices  30.1 us (30%)
  starting transfers between devices  25.5 us (26%)
    all_to_all x1, waiting for transfers between devices, on_device(): got = lax.all_to_all(send, everyone, 0, 0, tiled=True)  26.8 us
    all_to_all x1, starting transfers between devices, on_device(): got_terms = lax.all_to_all(message, everyone, 0, 0, tiled=True)  12.2 us
    pallas_call x1, Pallas kernels, on_device(): call(first_kernel, [far((34 * WIDE, F)), far((34 * WIDE, F)), shape((160,...  12.2 us
    ppermute x4, starting transfers between devices, swap(): return lax.ppermute(values, axis, list(enumerate(partner)))  6.82 us
    pallas_call x1, Pallas kernels, on_device(): call(backward_kernel, [shape((pixels, F)), shape((pixels // 4, F))], 4, [...  6.76 us
    all_to_all x1, starting transfers between devices, on_device(): got = lax.all_to_all(send, everyone, 0, 0, tiled=True)  6.51 us
    pallas_call x1, Pallas kernels, on_device(): call(forward_kernel, shape((pixels, F)), 4, loading, specs=[HBM, HBM, VME...  6.41 us
    pallas_call x1, Pallas kernels, on_device(): call(interior_kernel, [shape((pixels, 3 * F)), shape((30 * WIDE, F), F32)...  5.89 us
  transfers between devices with their start and end apart: 6, of which 2 were waited for; matrix products, arithmetic and copies ran while one was open for 0% of the time, Pallas kernels for 25%

profile of v7, /device:TPU:1, one launch (start us, length us, event | category | flops | bytes accessed | tf_op | source)
XLA Modules:
  0.0 99.7 jit_solution(4285485648265935765)
XLA Ops:
  0.6 0.0 copy-start
  0.6 0.0 copy-start.1
  0.7 0.0 copy-start.2
  0.7 1.3 %head.1 = (bf16[272,256]{1,0:T(8,128)(2,1)S(1)}, bf16[272,256]{1,0:T(8,128)(2,1)S(1)}) custom-call(bf16[512,256]{1,0:T(8,128)(2,1)} %bitcast.25, bf16[2048,256]{1,0:T(8,128)(2,1)} %bitcast.21, bf16[2048,256]{1,0:T(8,128)(2,1)} %bitcast.23, s32[8,16]{1,0:T(8,128)} %tissue_in.3), custom_call_target="tpu_custom_call" | custom-call | flops 1073741824 | bytes 4194304 | tf_op jit(solution)/shard_map/head/pallas_call | solution.py:636
  2.0 1.5 %collective-permute-start = (bf16[272,256]{1,0:T(8,128)(2,1)S(1)}, bf16[272,256]{1,0:T(8,128)(2,1)S(1)}, u32[]{:S(2)}, u32[]{:S(2)}) collective-permute-start(bf16[272,256]{1,0:T(8,128)(2,1)S(1)} %get-tuple-element.35), channel_id=1, source_target_pairs={{0,16},{16,0},{32,48},{48,32},{64,80},{80,64},{96,112},{112,96},{1... | collective-permute-start | bytes 417800 | tf_op jit(solution)/shard_map/ppermute | solution.py:625
  3.5 3.1 %collective-permute-start.1 = (bf16[272,256]{1,0:T(8,128)(2,1)S(1)}, bf16[272,256]{1,0:T(8,128)(2,1)S(1)}, u32[]{:S(2)}, u32[]{:S(2)}) collective-permute-start(bf16[272,256]{1,0:T(8,128)(2,1)S(1)} %get-tuple-element.36), channel_id=1, source_target_pairs={{0,0},{16,32},{32,16},{48,64},{64,48},{80,96},{96,80},{112,112},{1... | collective-permute-start | bytes 417800 | tf_op jit(solution)/shard_map/ppermute | solution.py:625
  6.6 0.0 copy-done
  6.6 0.0 copy-done.1
  6.6 0.0 copy-done.2
  6.7 3.6 %prepare.1 = (bf16[2048,256]{1,0:T(8,128)(2,1)S(1)}, bf16[2048,256]{1,0:T(8,128)(2,1)S(1)}, f32[128,256]{1,0:T(8,128)S(1)}, bf16[2304,256]{1,0:T(8,128)(2,1)S(1)...) custom-call(bf16[512,256]{1,0:T(8,128)(2,1)} %bitcast.26, ...), custom_call_target="tpu_custom_call" | custom-call | flops 3221225472 | bytes 4194304 | tf_op jit(solution)/shard_map/prepare/pallas_call | solution.py:648
  10.3 0.0 collective-permute-done.near_in
  10.3 0.0 collective-permute-done.1.far_in
  10.3 0.3 edge.1
  10.6 1.4 %collective-permute-start.2 = (bf16[240,256]{1,0:T(8,128)(2,1)S(1)}, bf16[240,256]{1,0:T(8,128)(2,1)S(1)}, u32[]{:S(2)}, u32[]{:S(2)}) collective-permute-start(bf16[240,256]{1,0:T(8,128)(2,1)S(1)} %get-tuple-element.42), channel_id=1, source_target_pairs={{0,1},{1,0},{2,3},{3,2},{4,5},{5,4},{6,7},{7,6},{8,9},{9,8},{10,11... | collective-permute-start | bytes 368648 | tf_op jit(solution)/shard_map/ppermute | solution.py:625
  12.0 0.8 collective-permute-start.3
  12.8 5.9 %interior.1 = (bf16[2048,768]{1,0:T(8,128)(2,1)S(1)}, f32[1920,256]{1,0:T(8,128)S(1)}, f32[1920,256]{1,0:T(8,128)S(1)}, bf16[256,768]{1,0:T(8,128)(2,1)S(1)}) custom-call(bf16[2048,256]{1,0:T(8,128)(2,1)S(1)} %get-tuple-element.33.merged, bf16[2048,256]{1,0:T(8,128)(2,1)S(1)} %get-tuple-element.34.grad_two, bf16[2304,256]{1,0:T(8,128)(2,1)S(1)} %get-tuple-element.44.fwd_one, ...), custom_call_target="tpu_custom_call" | custom-call | flops 5368709120 | bytes 4194304 | tf_op jit(solution)/shard_map/interior/pallas_call | solution.py:668
  18.7 0.0 collective-permute-done.2.near
  18.7 0.0 collective-permute-done.3.far_side
  18.8 12.2 %first.1 = (bf16[2176,256]{1,0:T(8,128)(2,1)}, bf16[2176,256]{1,0:T(8,128)(2,1)}, f32[160,256]{1,0:T(8,128)S(1)}, bf16[128,3,4,128]{3,2,1,0:T(4,128)(2,1)}) custom-call(bf16[2048,256]{1,0:T(8,128)(2,1)S(1)} %get-tuple-element.33.merged, bf16[2048,256]{1,0:T(8,128)(2,1)S(1)} %get-tuple-element.34.grad_two, bf16[272,256]{1,0:T(8,128)(2,1)S(1)} %get-tuple-element.38.top, ...), custom_call_target="tpu_custom_call" | custom-call | flops 10737418240 | bytes 4194304 | tf_op jit(solution)/shard_map/first/pallas_call | solution.py:676
  30.9 12.2 %all-to-all-start = ((bf16[128,3,4,128]{3,2,1,0:T(4,128)(2,1)}), bf16[128,3,4,128]{3,2,1,0:T(4,128)(2,1)S(1)}, u32[]{:S(2)}, u32[]{:S(2)}) async-start(bf16[128,3,4,128]{3,2,1,0:T(4,128)(2,1)} %get-tuple-element.55), calls=%async_computation | async-start | bytes 786432 | tf_op jit(solution)/shard_map/all_to_all | solution.py:690
  43.1 6.8 %backward.1 = (bf16[2048,256]{1,0:T(8,128)(2,1)S(1)}, bf16[512,256]{1,0:T(8,128)(2,1)}) custom-call(bf16[2176,256]{1,0:T(8,128)(2,1)} %get-tuple-element.53.pre_in, bf16[288,256]{1,0:T(8,128)(2,1)} %bitcast.17, f32[160,256]{1,0:T(8,128)S(1)} %get-tuple-element.51.edges, f32[128,256]{1,0:T(8,128)S(1)} %get-tuple-element.37.mask_rows), custom_call_target="tpu_custom_call" | custom-call | flops 3221225472 | bytes 4194304 | tf_op jit(solution)/shard_map/backward/pallas_call | solution.py:695
  49.9 2.7 %pack.1.send_in = bf16[128,19,4,128]{3,2,1,0:T(4,128)(2,1)} custom-call(s32[8,128]{1,0:T(8,128)S(1)} %get-tuple-element.52.places, bf16[2048,256]{1,0:T(8,128)(2,1)S(1)} %get-tuple-element.54.tiles), custom_call_target="tpu_custom_call" | custom-call | flops 1073741824 | bytes 4194304 | tf_op jit(solution)/shard_map/pack/pallas_call | solution.py:704
  52.6 3.3 %all-to-all-done.got = bf16[128,3,4,128]{3,2,1,0:T(4,128)(2,1)S(1)} async-done(((bf16[128,3,4,128]{3,2,1,0:T(4,128)(2,1)}), bf16[128,3,4,128]{3,2,1,0:T(4,128)(2,1)S(1)}, u32[]{:S(2)}, u32[]{:S(2)}) %all-to-all-start) | async-done | bytes 393248 | tf_op jit(solution)/shard_map/all_to_all | solution.py:690
  55.9 1.1 %terms.1 = bf16[128,19,4,128]{3,2,1,0:T(4,128)(2,1)} custom-call(bf16[128,19,4,128]{3,2,1,0:T(4,128)(2,1)} %pack.1.send_in, bf16[128,3,4,128]{3,2,1,0:T(4,128)(2,1)S(1)} %all-to-all-done.got, f32[128,128]{1,0:T(8,128)S(1)} %get-tuple-element.56.slot_rows), custom_call_target="tpu_custom_call", output_to_operand_aliasing={{}: (0, {})} | custom-call | flops 1073741824 | bytes 4194304 | tf_op jit(solution)/shard_map/terms/pallas_call | solution.py:705
  56.9 6.5 %all-to-all-start.1 = ((bf16[128,19,4,128]{3,2,1,0:T(4,128)(2,1)}), bf16[128,19,4,128]{3,2,1,0:T(4,128)(2,1)S(1)}, u32[]{:S(2)}, u32[]{:S(2)}) async-start(bf16[128,19,4,128]{3,2,1,0:T(4,128)(2,1)} %terms.1), calls=%async_computation.1 | async-start | bytes 4980736 | tf_op jit(solution)/shard_map/all_to_all | solution.py:716
  63.4 6.4 %forward.1 = bf16[2048,256]{1,0:T(8,128)(2,1)} custom-call(bf16[2176,256]{1,0:T(8,128)(2,1)} %get-tuple-element.50.hidden_in, bf16[288,256]{1,0:T(8,128)(2,1)} %bitcast.19, f32[160,256]{1,0:T(8,128)S(1)} %get-tuple-element.51.edges, f32[128,256]{1,0:T(8,128)S(1)} %get-tuple-element.37.mask_rows), custom_call_target="tpu_custom_call" | custom-call | flops 3221225472 | bytes 4194304 | tf_op jit(solution)/shard_map/forward/pallas_call | solution.py:700
  69.9 26.8 %all-to-all-done.1.got = bf16[128,19,4,128]{3,2,1,0:T(4,128)(2,1)S(1)} async-done(((bf16[128,19,4,128]{3,2,1,0:T(4,128)(2,1)}), bf16[128,19,4,128]{3,2,1,0:T(4,128)(2,1)S(1)}, u32[]{:S(2)}, u32[]{:S(2)}) %all-to-all-start.1) | async-done | bytes 2490400 | tf_op jit(solution)/shard_map/all_to_all | solution.py:716
  96.7 2.8 %place.1 = (bf16[128,4,4,256]{3,2,1,0:T(4,128)(2,1)}, f32[288,256]{1,0:T(8,128)}, f32[288,256]{1,0:T(8,128)}) custom-call(bf16[128,19,4,128]{3,2,1,0:T(4,128)(2,1)S(1)} %all-to-all-done.1.got), custom_call_target="tpu_custom_call" | custom-call | flops 1073741824 | bytes 4194304 | tf_op jit(solution)/shard_map/place/pallas_call | solution.py:718
Async XLA Ops:
  0.6 6.0 %copy-start = (bf16[32,3,3,256]{3,0,2,1:T(8,128)(2,1)S(1)}, bf16[32,3,3,256]{3,0,2,1:T(8,128)(2,1)}, u32[]{:S(2)}) copy-start(bf16[32,3,3,256]{3,0,2,1:T(8,128)(2,1)} %param.11) | copy-start | bytes 442372
  0.6 6.0 %copy-start.1 = (bf16[32,3,3,256]{3,0,2,1:T(8,128)(2,1)S(1)}, bf16[32,3,3,256]{3,0,2,1:T(8,128)(2,1)}, u32[]{:S(2)}) copy-start(bf16[32,3,3,256]{3,0,2,1:T(8,128)(2,1)} %param.12) | copy-start | bytes 442372
  0.7 6.0 %copy-start.2 = (s32[8,16]{1,0:T(8,128)S(1)}, s32[8,16]{1,0:T(8,128)}, u32[]{:S(2)}) copy-start(s32[8,16]{1,0:T(8,128)} %slots.1) | copy-start | bytes 1540
  2.0 8.3 %collective-permute-start = (bf16[272,256]{1,0:T(8,128)(2,1)S(1)}, bf16[272,256]{1,0:T(8,128)(2,1)S(1)}, u32[]{:S(2)}, u32[]{:S(2)}) collective-permute-start(bf16[272,256]{1,0:T(8,128)(2,1)S(1)} %get-tuple-element.35), channel_id=1, source_target_pairs={{0,16},{16,0},{32,48},{48,32},{64,80},{80,64},{96,112},{112,96},{1... | collective-permute-start | bytes 417800 | tf_op jit(solution)/shard_map/ppermute | solution.py:625
  3.5 6.8 %collective-permute-start.1 = (bf16[272,256]{1,0:T(8,128)(2,1)S(1)}, bf16[272,256]{1,0:T(8,128)(2,1)S(1)}, u32[]{:S(2)}, u32[]{:S(2)}) collective-permute-start(bf16[272,256]{1,0:T(8,128)(2,1)S(1)} %get-tuple-element.36), channel_id=1, source_target_pairs={{0,0},{16,32},{32,16},{48,64},{64,48},{80,96},{96,80},{112,112},{1... | collective-permute-start | bytes 417800 | tf_op jit(solution)/shard_map/ppermute | solution.py:625
  10.6 8.1 %collective-permute-start.2 = (bf16[240,256]{1,0:T(8,128)(2,1)S(1)}, bf16[240,256]{1,0:T(8,128)(2,1)S(1)}, u32[]{:S(2)}, u32[]{:S(2)}) collective-permute-start(bf16[240,256]{1,0:T(8,128)(2,1)S(1)} %get-tuple-element.42), channel_id=1, source_target_pairs={{0,1},{1,0},{2,3},{3,2},{4,5},{5,4},{6,7},{7,6},{8,9},{9,8},{10,11... | collective-permute-start | bytes 368648 | tf_op jit(solution)/shard_map/ppermute | solution.py:625
  12.0 6.8 %collective-permute-start.3 = (bf16[240,256]{1,0:T(8,128)(2,1)S(1)}, bf16[240,256]{1,0:T(8,128)(2,1)S(1)}, u32[]{:S(2)}, u32[]{:S(2)}) collective-permute-start(bf16[240,256]{1,0:T(8,128)(2,1)S(1)} %get-tuple-element.43), channel_id=1, source_target_pairs={{0,0},{1,2},{2,1},{3,4},{4,3},{5,6},{6,5},{7,8},{8,7},{9,10},{10,9... | collective-permute-start | bytes 368648 | tf_op jit(solution)/shard_map/ppermute | solution.py:625
  30.9 24.9 %all-to-all-start = ((bf16[128,3,4,128]{3,2,1,0:T(4,128)(2,1)}), bf16[128,3,4,128]{3,2,1,0:T(4,128)(2,1)S(1)}, u32[]{:S(2)}, u32[]{:S(2)}) async-start(bf16[128,3,4,128]{3,2,1,0:T(4,128)(2,1)} %get-tuple-element.55), calls=%async_computation | async-start | bytes 786432 | tf_op jit(solution)/shard_map/all_to_all | solution.py:690
  56.9 39.8 %all-to-all-start.1 = ((bf16[128,19,4,128]{3,2,1,0:T(4,128)(2,1)}), bf16[128,19,4,128]{3,2,1,0:T(4,128)(2,1)S(1)}, u32[]{:S(2)}, u32[]{:S(2)}) async-start(bf16[128,19,4,128]{3,2,1,0:T(4,128)(2,1)} %terms.1), calls=%async_computation.1 | async-start | bytes 4980736 | tf_op jit(solution)/shard_map/all_to_all | solution.py:716

commit v8 on v7

--- a/solution.py
+++ b/solution.py
@@ -436,7 +436,7 @@
     ends = functools.partial(activate, pre_from=pre_edge, grad_from=grad_edge)
     lax.fori_loop(0, 2, functools.partial(ends, source_row=0), 0)
     lax.fori_loop(
-        2, 32, functools.partial(activate, pre_from=pre, grad_from=grad_hidden, source_row=2), 0, unroll=2
+        2, 32, functools.partial(activate, pre_from=pre, grad_from=grad_hidden, source_row=2), 0, unroll=3
     )
     lax.fori_loop(32, 34, functools.partial(ends, source_row=30), 0)
     copies = start_copies(
@@ -605,8 +605,8 @@
     copy.wait()
 
     def put(group, _):
-        for sub in range(8):
-            slot = group * 8 + sub
+        for sub in range(32):
+            slot = group * 32 + sub
             place = table[0, slot]
             for half in range(2):
                 skip_grad[slot, :, :, half * 128 : half * 128 + 128] = got[
@@ -614,7 +614,7 @@
                 ]
         return 0
 
-    lax.fori_loop(0, 16, put, 0)
+    lax.fori_loop(0, 4, put, 0)
 
 
 def swap(values, axis, first):

time: 100 us -> 100 us (level)
  no operation moved by 1% of the time
where the time goes in v8:
time: 100 us; the launch traced here: 99.7 us
  Pallas kernels  43.1 us (43%)
  waiting for transfers between devices  30.1 us (30%)
  starting transfers between devices  25.5 us (26%)
    all_to_all x1, waiting for transfers between devices, on_device(): got = lax.all_to_all(send, everyone, 0, 0, tiled=True)  26.8 us
    pallas_call x1, Pallas kernels, on_device(): call(first_kernel, [far((34 * WIDE, F)), far((34 * WIDE, F)), shape((160,...  12.2 us
    all_to_all x1, starting transfers between devices, on_device(): got_terms = lax.all_to_all(message, everyone, 0, 0, tiled=True)  12.2 us
    ppermute x4, starting transfers between devices, swap(): return lax.ppermute(values, axis, list(enumerate(partner)))  6.82 us
    pallas_call x1, Pallas kernels, on_device(): call(backward_kernel, [shape((pixels, F)), shape((pixels // 4, F))], 4, [...  6.76 us
    all_to_all x1, starting transfers between devices, on_device(): got = lax.all_to_all(send, everyone, 0, 0, tiled=True)  6.5 us
    pallas_call x1, Pallas kernels, on_device(): call(forward_kernel, shape((pixels, F)), 4, loading, specs=[HBM, HBM, VME...  6.41 us
    pallas_call x1, Pallas kernels, on_device(): call(interior_kernel, [shape((pixels, 3 * F)), shape((30 * WIDE, F), F32)...  5.89 us
  transfers between devices with their start and end apart: 6, of which 2 were waited for; matrix products, arithmetic and copies ran while one was open for 0% of the time, Pallas kernels for 25%

profile of v8, /device:TPU:1, one launch (start us, length us, event | category | flops | bytes accessed | tf_op | source)
XLA Modules:
  0.0 99.7 jit_solution(10792981521487998025)
XLA Ops:
  0.6 0.0 copy-start
  0.6 0.0 copy-start.1
  0.7 0.0 copy-start.2
  0.7 1.3 %head.1 = (bf16[272,256]{1,0:T(8,128)(2,1)S(1)}, bf16[272,256]{1,0:T(8,128)(2,1)S(1)}) custom-call(bf16[512,256]{1,0:T(8,128)(2,1)} %bitcast.25, bf16[2048,256]{1,0:T(8,128)(2,1)} %bitcast.21, bf16[2048,256]{1,0:T(8,128)(2,1)} %bitcast.23, s32[8,16]{1,0:T(8,128)} %tissue_in.3), custom_call_target="tpu_custom_call" | custom-call | flops 1073741824 | bytes 4194304 | tf_op jit(solution)/shard_map/head/pallas_call | solution.py:636
  2.0 1.5 %collective-permute-start = (bf16[272,256]{1,0:T(8,128)(2,1)S(1)}, bf16[272,256]{1,0:T(8,128)(2,1)S(1)}, u32[]{:S(2)}, u32[]{:S(2)}) collective-permute-start(bf16[272,256]{1,0:T(8,128)(2,1)S(1)} %get-tuple-element.35), channel_id=1, source_target_pairs={{0,16},{16,0},{32,48},{48,32},{64,80},{80,64},{96,112},{112,96},{1... | collective-permute-start | bytes 417800 | tf_op jit(solution)/shard_map/ppermute | solution.py:625
  3.5 3.1 %collective-permute-start.1 = (bf16[272,256]{1,0:T(8,128)(2,1)S(1)}, bf16[272,256]{1,0:T(8,128)(2,1)S(1)}, u32[]{:S(2)}, u32[]{:S(2)}) collective-permute-start(bf16[272,256]{1,0:T(8,128)(2,1)S(1)} %get-tuple-element.36), channel_id=1, source_target_pairs={{0,0},{16,32},{32,16},{48,64},{64,48},{80,96},{96,80},{112,112},{1... | collective-permute-start | bytes 417800 | tf_op jit(solution)/shard_map/ppermute | solution.py:625
  6.6 0.0 copy-done
  6.6 0.0 copy-done.1
  6.6 0.0 copy-done.2
  6.7 3.6 %prepare.1 = (bf16[2048,256]{1,0:T(8,128)(2,1)S(1)}, bf16[2048,256]{1,0:T(8,128)(2,1)S(1)}, f32[128,256]{1,0:T(8,128)S(1)}, bf16[2304,256]{1,0:T(8,128)(2,1)S(1)...) custom-call(bf16[512,256]{1,0:T(8,128)(2,1)} %bitcast.26, ...), custom_call_target="tpu_custom_call" | custom-call | flops 3221225472 | bytes 4194304 | tf_op jit(solution)/shard_map/prepare/pallas_call | solution.py:648
  10.3 0.0 collective-permute-done.near_in
  10.3 0.0 collective-permute-done.1.far_in
  10.3 0.3 edge.1
  10.6 1.4 %collective-permute-start.2 = (bf16[240,256]{1,0:T(8,128)(2,1)S(1)}, bf16[240,256]{1,0:T(8,128)(2,1)S(1)}, u32[]{:S(2)}, u32[]{:S(2)}) collective-permute-start(bf16[240,256]{1,0:T(8,128)(2,1)S(1)} %get-tuple-element.42), channel_id=1, source_target_pairs={{0,1},{1,0},{2,3},{3,2},{4,5},{5,4},{6,7},{7,6},{8,9},{9,8},{10,11... | collective-permute-start | bytes 368648 | tf_op jit(solution)/shard_map/ppermute | solution.py:625
  12.0 0.8 collective-permute-start.3
  12.8 5.9 %interior.1 = (bf16[2048,768]{1,0:T(8,128)(2,1)S(1)}, f32[1920,256]{1,0:T(8,128)S(1)}, f32[1920,256]{1,0:T(8,128)S(1)}, bf16[256,768]{1,0:T(8,128)(2,1)S(1)}) custom-call(bf16[2048,256]{1,0:T(8,128)(2,1)S(1)} %get-tuple-element.33.merged, bf16[2048,256]{1,0:T(8,128)(2,1)S(1)} %get-tuple-element.34.grad_two, bf16[2304,256]{1,0:T(8,128)(2,1)S(1)} %get-tuple-element.44.fwd_one, ...), custom_call_target="tpu_custom_call" | custom-call | flops 5368709120 | bytes 4194304 | tf_op jit(solution)/shard_map/interior/pallas_call | solution.py:668
  18.7 0.0 collective-permute-done.2.near
  18.7 0.0 collective-permute-done.3.far_side
  18.8 12.2 %first.1 = (bf16[2176,256]{1,0:T(8,128)(2,1)}, bf16[2176,256]{1,0:T(8,128)(2,1)}, f32[160,256]{1,0:T(8,128)S(1)}, bf16[128,3,4,128]{3,2,1,0:T(4,128)(2,1)}) custom-call(bf16[2048,256]{1,0:T(8,128)(2,1)S(1)} %get-tuple-element.33.merged, bf16[2048,256]{1,0:T(8,128)(2,1)S(1)} %get-tuple-element.34.grad_two, bf16[272,256]{1,0:T(8,128)(2,1)S(1)} %get-tuple-element.38.top, ...), custom_call_target="tpu_custom_call" | custom-call | flops 10737418240 | bytes 4194304 | tf_op jit(solution)/shard_map/first/pallas_call | solution.py:676
  31.0 12.2 %all-to-all-start = ((bf16[128,3,4,128]{3,2,1,0:T(4,128)(2,1)}), bf16[128,3,4,128]{3,2,1,0:T(4,128)(2,1)S(1)}, u32[]{:S(2)}, u32[]{:S(2)}) async-start(bf16[128,3,4,128]{3,2,1,0:T(4,128)(2,1)} %get-tuple-element.55), calls=%async_computation | async-start | bytes 786432 | tf_op jit(solution)/shard_map/all_to_all | solution.py:690
  43.1 6.8 %backward.1 = (bf16[2048,256]{1,0:T(8,128)(2,1)S(1)}, bf16[512,256]{1,0:T(8,128)(2,1)}) custom-call(bf16[2176,256]{1,0:T(8,128)(2,1)} %get-tuple-element.53.pre_in, bf16[288,256]{1,0:T(8,128)(2,1)} %bitcast.17, f32[160,256]{1,0:T(8,128)S(1)} %get-tuple-element.51.edges, f32[128,256]{1,0:T(8,128)S(1)} %get-tuple-element.37.mask_rows), custom_call_target="tpu_custom_call" | custom-call | flops 3221225472 | bytes 4194304 | tf_op jit(solution)/shard_map/backward/pallas_call | solution.py:695
  49.9 2.7 %pack.1.send_in = bf16[128,19,4,128]{3,2,1,0:T(4,128)(2,1)} custom-call(s32[8,128]{1,0:T(8,128)S(1)} %get-tuple-element.52.places, bf16[2048,256]{1,0:T(8,128)(2,1)S(1)} %get-tuple-element.54.tiles), custom_call_target="tpu_custom_call" | custom-call | flops 1073741824 | bytes 4194304 | tf_op jit(solution)/shard_map/pack/pallas_call | solution.py:704
  52.6 3.3 %all-to-all-done.got = bf16[128,3,4,128]{3,2,1,0:T(4,128)(2,1)S(1)} async-done(((bf16[128,3,4,128]{3,2,1,0:T(4,128)(2,1)}), bf16[128,3,4,128]{3,2,1,0:T(4,128)(2,1)S(1)}, u32[]{:S(2)}, u32[]{:S(2)}) %all-to-all-start) | async-done | bytes 393248 | tf_op jit(solution)/shard_map/all_to_all | solution.py:690
  55.9 1.1 %terms.1 = bf16[128,19,4,128]{3,2,1,0:T(4,128)(2,1)} custom-call(bf16[128,19,4,128]{3,2,1,0:T(4,128)(2,1)} %pack.1.send_in, bf16[128,3,4,128]{3,2,1,0:T(4,128)(2,1)S(1)} %all-to-all-done.got, f32[128,128]{1,0:T(8,128)S(1)} %get-tuple-element.56.slot_rows), custom_call_target="tpu_custom_call", output_to_operand_aliasing={{}: (0, {})} | custom-call | flops 1073741824 | bytes 4194304 | tf_op jit(solution)/shard_map/terms/pallas_call | solution.py:705
  57.0 6.5 %all-to-all-start.1 = ((bf16[128,19,4,128]{3,2,1,0:T(4,128)(2,1)}), bf16[128,19,4,128]{3,2,1,0:T(4,128)(2,1)S(1)}, u32[]{:S(2)}, u32[]{:S(2)}) async-start(bf16[128,19,4,128]{3,2,1,0:T(4,128)(2,1)} %terms.1), calls=%async_computation.1 | async-start | bytes 4980736 | tf_op jit(solution)/shard_map/all_to_all | solution.py:716
  63.5 6.4 %forward.1 = bf16[2048,256]{1,0:T(8,128)(2,1)} custom-call(bf16[2176,256]{1,0:T(8,128)(2,1)} %get-tuple-element.50.hidden_in, bf16[288,256]{1,0:T(8,128)(2,1)} %bitcast.19, f32[160,256]{1,0:T(8,128)S(1)} %get-tuple-element.51.edges, f32[128,256]{1,0:T(8,128)S(1)} %get-tuple-element.37.mask_rows), custom_call_target="tpu_custom_call" | custom-call | flops 3221225472 | bytes 4194304 | tf_op jit(solution)/shard_map/forward/pallas_call | solution.py:700
  69.9 26.8 %all-to-all-done.1.got = bf16[128,19,4,128]{3,2,1,0:T(4,128)(2,1)S(1)} async-done(((bf16[128,19,4,128]{3,2,1,0:T(4,128)(2,1)}), bf16[128,19,4,128]{3,2,1,0:T(4,128)(2,1)S(1)}, u32[]{:S(2)}, u32[]{:S(2)}) %all-to-all-start.1) | async-done | bytes 2490400 | tf_op jit(solution)/shard_map/all_to_all | solution.py:716
  96.7 2.8 %place.1 = (bf16[128,4,4,256]{3,2,1,0:T(4,128)(2,1)}, f32[288,256]{1,0:T(8,128)}, f32[288,256]{1,0:T(8,128)}) custom-call(bf16[128,19,4,128]{3,2,1,0:T(4,128)(2,1)S(1)} %all-to-all-done.1.got), custom_call_target="tpu_custom_call" | custom-call | flops 1073741824 | bytes 4194304 | tf_op jit(solution)/shard_map/place/pallas_call | solution.py:718
Async XLA Ops:
  0.6 6.0 %copy-start = (bf16[32,3,3,256]{3,0,2,1:T(8,128)(2,1)S(1)}, bf16[32,3,3,256]{3,0,2,1:T(8,128)(2,1)}, u32[]{:S(2)}) copy-start(bf16[32,3,3,256]{3,0,2,1:T(8,128)(2,1)} %param.11) | copy-start | bytes 442372
  0.6 6.0 %copy-start.1 = (bf16[32,3,3,256]{3,0,2,1:T(8,128)(2,1)S(1)}, bf16[32,3,3,256]{3,0,2,1:T(8,128)(2,1)}, u32[]{:S(2)}) copy-start(bf16[32,3,3,256]{3,0,2,1:T(8,128)(2,1)} %param.12) | copy-start | bytes 442372
  0.7 6.0 %copy-start.2 = (s32[8,16]{1,0:T(8,128)S(1)}, s32[8,16]{1,0:T(8,128)}, u32[]{:S(2)}) copy-start(s32[8,16]{1,0:T(8,128)} %slots.1) | copy-start | bytes 1540
  2.0 8.3 %collective-permute-start = (bf16[272,256]{1,0:T(8,128)(2,1)S(1)}, bf16[272,256]{1,0:T(8,128)(2,1)S(1)}, u32[]{:S(2)}, u32[]{:S(2)}) collective-permute-start(bf16[272,256]{1,0:T(8,128)(2,1)S(1)} %get-tuple-element.35), channel_id=1, source_target_pairs={{0,16},{16,0},{32,48},{48,32},{64,80},{80,64},{96,112},{112,96},{1... | collective-permute-start | bytes 417800 | tf_op jit(solution)/shard_map/ppermute | solution.py:625
  3.5 6.8 %collective-permute-start.1 = (bf16[272,256]{1,0:T(8,128)(2,1)S(1)}, bf16[272,256]{1,0:T(8,128)(2,1)S(1)}, u32[]{:S(2)}, u32[]{:S(2)}) collective-permute-start(bf16[272,256]{1,0:T(8,128)(2,1)S(1)} %get-tuple-element.36), channel_id=1, source_target_pairs={{0,0},{16,32},{32,16},{48,64},{64,48},{80,96},{96,80},{112,112},{1... | collective-permute-start | bytes 417800 | tf_op jit(solution)/shard_map/ppermute | solution.py:625
  10.6 8.1 %collective-permute-start.2 = (bf16[240,256]{1,0:T(8,128)(2,1)S(1)}, bf16[240,256]{1,0:T(8,128)(2,1)S(1)}, u32[]{:S(2)}, u32[]{:S(2)}) collective-permute-start(bf16[240,256]{1,0:T(8,128)(2,1)S(1)} %get-tuple-element.42), channel_id=1, source_target_pairs={{0,1},{1,0},{2,3},{3,2},{4,5},{5,4},{6,7},{7,6},{8,9},{9,8},{10,11... | collective-permute-start | bytes 368648 | tf_op jit(solution)/shard_map/ppermute | solution.py:625
  12.0 6.8 %collective-permute-start.3 = (bf16[240,256]{1,0:T(8,128)(2,1)S(1)}, bf16[240,256]{1,0:T(8,128)(2,1)S(1)}, u32[]{:S(2)}, u32[]{:S(2)}) collective-permute-start(bf16[240,256]{1,0:T(8,128)(2,1)S(1)} %get-tuple-element.43), channel_id=1, source_target_pairs={{0,0},{1,2},{2,1},{3,4},{4,3},{5,6},{6,5},{7,8},{8,7},{9,10},{10,9... | collective-permute-start | bytes 368648 | tf_op jit(solution)/shard_map/ppermute | solution.py:625
  31.0 24.9 %all-to-all-start = ((bf16[128,3,4,128]{3,2,1,0:T(4,128)(2,1)}), bf16[128,3,4,128]{3,2,1,0:T(4,128)(2,1)S(1)}, u32[]{:S(2)}, u32[]{:S(2)}) async-start(bf16[128,3,4,128]{3,2,1,0:T(4,128)(2,1)} %get-tuple-element.55), calls=%async_computation | async-start | bytes 786432 | tf_op jit(solution)/shard_map/all_to_all | solution.py:690
  57.0 39.8 %all-to-all-start.1 = ((bf16[128,19,4,128]{3,2,1,0:T(4,128)(2,1)}), bf16[128,19,4,128]{3,2,1,0:T(4,128)(2,1)S(1)}, u32[]{:S(2)}, u32[]{:S(2)}) async-start(bf16[128,19,4,128]{3,2,1,0:T(4,128)(2,1)} %terms.1), calls=%async_computation.1 | async-start | bytes 4980736 | tf_op jit(solution)/shard_map/all_to_all | solution.py:716
